TPU v7x, 256 devices: a whole 4x4x8 slice. The times are simulated.
256 devices in a mesh: row: 32 (over y, z_lo, core), col: 8 (over x, z_hi).
Axes of the slice: x: 4, y: 4, z: 8 (z_hi: 2, z_lo: 4; z = z_hi * 4 + z_lo), core: 2. Of those that a mesh axis runs over, the one named last changes fastest.
Arguments:
- object_field: bfloat16 [2, 8192, 8192], P(None, 'row', 'col'), may hold values from -6 to 6
- probe: float32 [2, 2, 256, 256], replicated, may hold values from -5 to 5
- measured: bfloat16 [32, 8, 12, 256, 256], P('row', 'col'), may hold values from 0.3984375 to 4
- positions: int32 [32, 8, 12, 2], P('row', 'col'), may hold values from 0 to 1023, as said below
- counts: int32 [32, 8], P('row', 'col'), may hold values from 1 to 12, as said below
Outputs:
- object_grad: float32 [2, 8192, 8192], P(None, 'row', 'col')
- probe_grad: float32 [2, 2, 256, 256], replicated
Inputs may be any that keep to these rules, and one draw needn't show every extreme that they name: positions[i, j, s, 0] lies in 0 to 255 and positions[i, j, s, 1] in 0 to 1023 for every slot, live or not. `counts`: some tile has all 12 slots live.
All inputs are finite; a program needn't handle non-finite values.
Results may differ from a plain program's by a relative error of at most 0.0048.
The roundings to bfloat16 on the way count: a program that leaves them out, or rounds other values in their place, can miss the bound.
Values may be sent and summed in bfloat16 or wider, within the bound.
No kernel may reach another device: no remote copies, remote signals or barrier semaphores. Data moves between devices by JAX's collectives and lax.ppermute only.
A program may use at most 128 MiB of HBM per device.

v0:
```python
import math

import jax
import jax.numpy as jnp
import numpy as np
from jax import lax
from jax.experimental import pallas as pl
from jax.experimental.pallas import tpu as pltpu
from jax.sharding import PartitionSpec as P


f32 = jnp.float32
bf16 = jnp.bfloat16


def shifted(x, axis, by):
    peers = lax.axis_size(axis)
    pairs = [(i, i + by) for i in range(peers) if 0 <= i + by < peers]
    return lax.ppermute(x, axis, pairs)


FIELDS = {
    "core": ("row", 0, 1),
    "zlo": ("row", 1, 2),
    "y": ("row", 3, 2),
    "row_hi": ("row", 1, 4),
    "zhi": ("col", 0, 1),
    "x": ("col", 1, 2),
    "col": ("col", 0, 3),
}


def partner(v, field, d):
    axis, low, _ = FIELDS[field]
    return lax.ppermute(v, axis, [(i, i ^ (d << low)) for i in range(lax.axis_size(axis))])


def place(field):
    axis, low, bits = FIELDS[field]
    return (lax.axis_index(axis) >> low) & ((1 << bits) - 1)


def scatter_sum(v, field, dtype):
    n = 1 << FIELDS[field][2]
    g = place(field)
    k = v.shape[0] // n
    total = lax.dynamic_slice_in_dim(v, g * k, k, 0)
    got = [
        partner(lax.dynamic_slice_in_dim(v, (g ^ d) * k, k, 0).astype(dtype), field, d)
        for d in range(1, n)
    ]
    for part in got:
        total = total + part.astype(f32)
    return total


def full_sum(v, field, dtype):
    n = 1 << FIELDS[field][2]
    sent = v.astype(dtype)
    parts = [sent.astype(f32)] + [partner(sent, field, d).astype(f32) for d in range(1, n)]
    while len(parts) > 1:
        parts = [parts[i] + parts[i + 1] for i in range(0, len(parts), 2)]
    return parts[0]


def gather(v, field, dtype):
    n = 1 << FIELDS[field][2]
    g = place(field)
    k = v.shape[0]
    sent = v.astype(dtype)
    got = [partner(sent, field, d) for d in range(1, n)]
    out = jnp.zeros((n * k,) + v.shape[1:], dtype)
    out = lax.dynamic_update_slice_in_dim(out, sent, g * k, 0)
    for d in range(1, n):
        out = lax.dynamic_update_slice_in_dim(out, got[d - 1], (g ^ d) * k, 0)
    return out


PLAN = (
    (scatter_sum, "core", bf16),
    (scatter_sum, "y", bf16),
    (full_sum, "x", bf16),
    (full_sum, "zlo", bf16),
    (full_sum, "zhi", bf16),
    (gather, "y", bf16),
    (gather, "core", bf16),
)


def reduce_all(v):
    for step, field, dtype in PLAN:
        v = step(v, field, dtype)
    return v.astype(f32)


def dft_parts(size):
    index = np.arange(size)
    phase = (index[:, None] * index[None, :]) % size
    angle = 2.0 * np.pi / size * phase
    cosine = (np.cos(angle) / np.sqrt(size)).astype(jnp.bfloat16).astype(np.float32)
    sine = (np.sin(angle) / np.sqrt(size)).astype(jnp.bfloat16).astype(np.float32)
    return cosine, sine


def tables(size):
    half = size // 2
    c, s = dft_parts(size)
    order = np.concatenate([np.arange(0, size, 2), np.arange(1, size, 2)])
    fc, fs = c[order], s[order]
    left = np.block([[fc, fs], [-fs, fc]])
    cols = []
    for q in range(2):
        pick = order[q * half : (q + 1) * half]
        cols.append(np.block([[c[:, pick], -s[:, pick]], [s[:, pick], c[:, pick]]]))
    right = np.concatenate(cols, 1)
    gl, gr = [], []
    for q in range(2):
        ce, se = c[:half, q::2], s[:half, q::2]
        gl.append(np.block([[ce, -se], [se, ce]]))
        cr, sr = c[q::2, :half], s[q::2, :half]
        gr.append(np.block([[cr, sr], [-sr, cr]]))
    perm = np.zeros((size, size), np.float32)
    perm[np.arange(size), order] = 1.0
    to = lambda a: jnp.asarray(np.asarray(a, np.float32).astype(jnp.bfloat16))
    return to(left), to(right), to(np.stack(gl)), to(np.stack(gr)), to(perm), to(perm.T)


def prep_kernel(frames, rows, cols, out):
    def one(s, _):
        a = jnp.dot(rows[...], frames[s], preferred_element_type=f32).astype(bf16)
        out[s] = jnp.dot(a, cols[...], preferred_element_type=f32).astype(bf16)
        return 0

    lax.fori_loop(0, frames.shape[0], one, 0)


def positions_pass(
    pos, cnt, wanted, base, blocks, clear, probe, frames, tables, p_out,
    ext, gext, xs, hs, sp, ws, ib, hb, eb, todo,
):
    left, right, gl, gr = tables
    n = probe.shape[-1]
    h = n // 2
    ch = 16
    todo[0] = 0

    def pick(s, k):
        take = wanted(pos[s, 1])

        @pl.when(take)
        def _():
            todo[k] = s

        return k + take.astype(jnp.int32)

    count = lax.fori_loop(0, cnt[0], pick, 0)
    last = jnp.maximum(count - 1, 0)

    def window(t):
        s = todo[jnp.clip(t, 0, last)]
        c = pos[s, 1]
        sh = lax.rem(c, 128)
        cb = jnp.clip(c // 128 - base, 0, blocks - 3)
        return s, pos[s, 0], cb, sh, lax.rem(384 - sh, 384)

    def patch_rows(win, i, ch=16):
        _, r, cb, _, unshift = win
        out = []
        for p in range(2):
            w = jnp.concatenate([ext[p, cb + b, pl.ds(r + i, ch), :] for b in range(3)], 1)
            out.append(pltpu.roll(w, unshift, 1)[:, :n])
        return out

    def wave_rows(win, i):
        o = patch_rows(win, i)
        for m in range(2):
            pr = probe[m, 0, i : i + ch, :]
            pi = probe[m, 1, i : i + ch, :]
            xs[m, i : i + ch, :] = (pr * o[0] - pi * o[1]).astype(bf16)
            xs[m, n + i : n + i + ch, :] = (pr * o[1] + pi * o[0]).astype(bf16)

    def forward_left(m, part):
        half = jnp.dot(left[part * n : (part + 1) * n, :], xs[m], preferred_element_type=f32)
        hs[m, :, part * n : (part + 1) * n] = half.astype(bf16)

    def forward_right(m, q):
        sp[m, q] = jnp.dot(hs[m], right[:, q * n : (q + 1) * n], preferred_element_type=f32)

    def weigh_rows(win, i):
        s = win[0]
        rows = i % h
        par = i // h
        for q in range(2):
            v = [sp[m, q, i : i + ch, :] for m in range(2)]
            e = v[0] * v[0] + v[1] * v[1]
            inten = e[:, :h] + e[:, h:] + 1.0
            f = 1.0 - frames[s, i : i + ch, q * h : (q + 1) * h].astype(f32) * lax.rsqrt(inten)
            for m in range(2):
                for part in range(2):
                    ws[m, par, part * h + rows : part * h + rows + ch, q * h : (q + 1) * h] = (
                        v[m][:, part * h : (part + 1) * h] * f
                    ).astype(bf16)

    def inverse_left(m, par):
        ib[m, par] = jnp.dot(gl[par], ws[m, par], preferred_element_type=f32)

    def join_rows(m, part, i):
        a = ib[m, 0, part * h + i : part * h + i + ch, :]
        b = ib[m, 1, part * h + i : part * h + i + ch, :]
        up = (a + b).astype(bf16)
        dn = (a - b).astype(bf16)
        for q in range(2):
            hb[m, q, i : i + ch, part * h : (part + 1) * h] = up[:, q * h : (q + 1) * h]
            hb[m, q, h + i : h + i + ch, part * h : (part + 1) * h] = dn[:, q * h : (q + 1) * h]

    def inverse_right(m, q):
        eb[m, q] = jnp.dot(hb[m, q], gr[q], preferred_element_type=f32)

    def add_rows(win, i0):
      for i in range(i0, i0 + ch, 8):
        add_some(win, i)

    def add_some(win, i):
        _, r, cb, sh, _ = win
        ore, oim = patch_rows(win, i, 8)
        acc = None
        for m in range(2):
            e = eb[m, 0, i : i + 8, :]
            d = eb[m, 1, i : i + 8, :]
            up = e + d
            dn = e - d
            bre = jnp.concatenate([up[:, :h], dn[:, :h]], 1)
            bim = jnp.concatenate([up[:, h:], dn[:, h:]], 1)
            pr = probe[m, 0, i : i + 8, :]
            pi = probe[m, 1, i : i + 8, :]
            g = (pr * bre + pi * bim, pr * bim - pi * bre)
            acc = g if m == 0 else (acc[0] + g[0], acc[1] + g[1])
            p_out[m, 0, i : i + 8, :] += ore * bre + oim * bim
            p_out[m, 1, i : i + 8, :] += ore * bim - oim * bre
        zero = jnp.zeros((8, 128), f32)
        v = [pltpu.roll(jnp.concatenate([x, zero], 1), sh, 1) for x in acc]
        new = [
            gext[p, cb + b, pl.ds(r + i, 8), :] + v[p][:, b * 128 : (b + 1) * 128]
            for p in range(2)
            for b in range(3)
        ]
        for p in range(2):
            for b in range(3):
                gext[p, cb + b, pl.ds(r + i, 8), :] = new[p * 3 + b]

    chunks = list(range(0, n, ch))
    pairs = [(m, k) for m in range(2) for k in range(2)]

    def step(t, _):
        now = window(t)
        old = window(t - 1)
        for k, (m, par) in enumerate(pairs):
            inverse_left(m, par)
            for i in chunks[2 * k : 2 * k + 2]:
                wave_rows(now, i)
        for m in range(2):
            for part in range(2):
                for i in range(0, h, ch):
                    join_rows(m, part, i)
        for k, (m, q) in enumerate(pairs):
            inverse_right(m, q)
            for i in chunks[8 + 2 * k : 8 + 2 * k + 2]:
                wave_rows(now, i)
        for k, (m, part) in enumerate(pairs):
            forward_left(m, part)
            for i in chunks[2 * k : 2 * k + 2]:
                add_rows(old, i)
        for k, (m, q) in enumerate(pairs):
            forward_right(m, q)
            for i in chunks[8 + 2 * k : 8 + 2 * k + 2]:
                add_rows(old, i)
        for i in chunks:
            weigh_rows(now, i)

        @pl.when(t == 0)
        def _():
            clear()

        return 0

    lax.fori_loop(0, count + 1, step, 0)


def fill(ext, sources):
    for p in range(2):
        for src, c_from, c_to, r0, c0 in sources:
            for b in range((c_to - c_from) // 128):
                lo = c_from + b * 128
                ext[p, c0 // 128 + b, r0 : r0 + src.shape[1], :] = src[p, :, lo : lo + 128].astype(f32)


def drain(gext, targets):
    for p in range(2):
        for dst, d0, width, r0, c0 in targets:
            for b in range(width // 128):
                dst[p, :, d0 + b * 128 : d0 + (b + 1) * 128] = gext[
                    p, c0 // 128 + b, r0 : r0 + dst.shape[1], :
                ].astype(dst.dtype)


def inner_kernel(
    pos, cnt, own, below, probe, frames, left, right, gl, gr,
    g_own, g_below, carry, p_out,
    ext, gext, *scratch,
):
    n = probe.shape[-1]
    tr, tc = own.shape[1:]
    inner = tc - n
    fill(ext, ((own, 0, tc, 0, 0), (below, 0, tc, tr, 0)))

    def clear():
        gext[...] = jnp.zeros_like(gext)
        p_out[...] = jnp.zeros_like(p_out)

    positions_pass(
        pos, cnt, lambda c: c < inner, 0, tc // 128, clear, probe, frames, (left, right, gl, gr), p_out,
        ext, gext, *scratch,
    )
    drain(gext, ((g_own, 0, inner, 0, 0), (g_below, 0, inner, tr, 0)))
    for p in range(2):
        for b in range(n // 128):
            carry[p, b] = gext[p, inner // 128 + b]


def edge_kernel(
    scale, pos, cnt, own, below, strip, corner, carry, p_in, probe, frames, left, right, gl, gr,
    g_own, g_rows, g_strip, p_out,
    ext, gext, *scratch,
):
    n = probe.shape[-1]
    tr, tc = own.shape[1:]
    inner = tc - n
    fill(
        ext,
        ((own, inner, tc, 0, 0), (below, inner, tc, tr, 0), (strip, 0, n, 0, n), (corner, 0, n, tr, n)),
    )

    def clear():
        p_out[...] = p_in[...]
        for p in range(2):
            for b in range(n // 128):
                gext[p, b] = carry[p, b]
                gext[p, n // 128 + b] = jnp.zeros_like(gext[p, b])

    positions_pass(
        pos, cnt, lambda c: c >= inner, inner // 128, 2 * n // 128, clear, probe, frames,
        (left, right, gl, gr), p_out, ext, gext, *scratch,
    )
    p_out[...] = p_out[...] * scale
    drain(gext, ((g_own, 0, n, 0, 0), (g_rows, 0, 2 * n, tr, 0), (g_strip, 0, n, 0, n)))


def body(object_field, probe, measured, positions, counts):
    size = probe.shape[-1]
    tile_rows, tile_cols = object_field.shape[1:]
    slots = measured.shape[2]
    left, right, gl, gr, perm, perm_t = tables(size)
    vmem = pl.BlockSpec(memory_space=pltpu.VMEM)
    smem = pl.BlockSpec(memory_space=pltpu.SMEM)
    pos, cnt = positions[0, 0], counts[0]
    inner = tile_cols - size
    rows = tile_rows + size

    below = shifted(object_field, "row", -1)
    strip = shifted(object_field[:, :, :size], "col", -1)
    corner = shifted(strip, "row", -1)
    frames = pl.pallas_call(
        prep_kernel,
        out_shape=jax.ShapeDtypeStruct(measured.shape[2:], bf16),
        in_specs=[vmem] * 3,
        out_specs=vmem,
        compiler_params=pltpu.CompilerParams(vmem_limit_bytes=8 * 2**20),
        cost_estimate=pl.CostEstimate(
            flops=slots * 4 * size**3, bytes_accessed=4 * slots * size * size, transcendentals=0
        ),
    )(measured[0, 0], perm, perm_t)

    def scratch(blocks):
        return [
            pltpu.VMEM((2, blocks, rows, 128), f32),
            pltpu.VMEM((2, blocks, rows, 128), f32),
            pltpu.VMEM((2, 2 * size, size), bf16),
            pltpu.VMEM((2, size, 2 * size), bf16),
            pltpu.VMEM((2, 2, size, size), f32),
            pltpu.VMEM((2, 2, size, size), bf16),
            pltpu.VMEM((2, 2, size, size), f32),
            pltpu.VMEM((2, 2, size, size), bf16),
            pltpu.VMEM((2, 2, size, size), f32),
            pltpu.SMEM((slots,), jnp.int32),
        ]

    params = pltpu.CompilerParams(vmem_limit_bytes=32 * 2**20)
    g_main, g_band, carry, p_part = pl.pallas_call(
        inner_kernel,
        out_shape=(
            jax.ShapeDtypeStruct((2, tile_rows, inner), f32),
            jax.ShapeDtypeStruct((2, size, inner), bf16),
            jax.ShapeDtypeStruct((2, size // 128, rows, 128), f32),
            jax.ShapeDtypeStruct(probe.shape, f32),
        ),
        in_specs=[smem, smem] + [vmem] * 8,
        out_specs=[vmem] * 4,
        scratch_shapes=scratch(tile_cols // 128),
        compiler_params=params,
        cost_estimate=pl.CostEstimate(flops=9 * 2**30, bytes_accessed=12 * 2**20, transcendentals=0),
    )(pos, cnt, object_field, below, probe, frames, left, right, gl, gr)
    total = slots * lax.axis_size("row") * lax.axis_size("col")
    scale = 1.0 / math.sqrt(total)
    g_right, g_rows, g_strip, p_sum = pl.pallas_call(
        lambda *refs: edge_kernel(scale, *refs),
        out_shape=(
            jax.ShapeDtypeStruct((2, tile_rows, size), f32),
            jax.ShapeDtypeStruct((2, size, 2 * size), bf16),
            jax.ShapeDtypeStruct((2, tile_rows, size), bf16),
            jax.ShapeDtypeStruct(probe.shape, f32),
        ),
        in_specs=[smem, smem] + [vmem] * 12,
        out_specs=[vmem] * 4,
        scratch_shapes=scratch(2 * size // 128),
        compiler_params=params,
        cost_estimate=pl.CostEstimate(flops=3 * 2**30, bytes_accessed=12 * 2**20, transcendentals=0),
    )(pos, cnt, object_field, below, strip, corner, carry, p_part, probe, frames, left, right, gl, gr)

    band = shifted(g_band, "row", 1)
    tail = shifted(g_rows, "row", 1)
    to_right = (g_strip.astype(f32) + tail[:, :, size:].astype(f32)).astype(bf16)
    side = shifted(to_right, "col", 1)
    probe_grad = reduce_all(p_sum.reshape(-1, size)).reshape(probe.shape)
    object_grad = jnp.concatenate(
        [g_main + band.astype(f32), g_right + tail[:, :, :size].astype(f32)], 2
    )
    object_grad = object_grad.at[:, :, :size].add(side.astype(f32))
    return (object_grad, probe_grad)


def solution(mesh):
    placed = (
        P(None, "row", "col"),
        P(),
        P("row", "col", None, None, None),
        P("row", "col", None, None),
        P("row", "col"),
    )
    return jax.shard_map(
        body, mesh=mesh, in_specs=placed, out_specs=(P(None, "row", "col"), P()), check_vma=False
    )
```

profile of v0, /device:TPU:35, one launch (start us, length us, event | category | flops | bytes accessed | tf_op | source)
XLA Modules:
  0.0 130.3 jit_solution(11343690592445862652)
XLA Ops:
  0.6 2.6 %collective-permute-start = (bf16[2,256,1024]{2,1,0:T(8,128)(2,1)}, bf16[2,256,1024]{2,1,0:T(8,128)(2,1)S(1)}, u32[]{:S(2)}, u32[]{:S(2)}) collective-permute-start(bf16[2,256,1024]{2,1,0:T(8,128)(2,1)} %refs_2_.1), channel_id=1, source_target_pairs={{8,0},{16,8},{24,16},{32,24},{40,32},{48,40},{56,48},{64,56},{72,6... | collective-permute-start | bytes 3145736 | tf_op jit(solution)/shard_map/ppermute | solution.py:19
  4.2 7.9 %collective-permute-start.2 = (bf16[2,256,256]{2,1,0:T(8,128)(2,1)S(1)}, bf16[2,256,256]{2,1,0:T(8,128)(2,1)}, u32[]{:S(2)}, u32[]{:S(2)}) collective-permute-start(bf16[2,256,256]{2,1,0:T(8,128)(2,1)S(1)} %slice.34), channel_id=1, source_target_pairs={{1,0},{2,1},{3,2},{4,3},{5,4},{6,5},{7,6},{9,8},{10,9},{11,10},{12... | collective-permute-start | bytes 786440 | tf_op jit(solution)/shard_map/ppermute | solution.py:19
  13.5 1.4 %copy-done = bf16[1,1,12,256,256]{4,3,2,1,0:T(8,128)(2,1)S(1)} copy-done((bf16[1,1,12,256,256]{4,3,2,1,0:T(8,128)(2,1)S(1)}, bf16[1,1,12,256,256]{4,3,2,1,0:T(8,128)(2,1)}, u32[]{:S(2)}) %copy-start) | copy-done | bytes 1572888
  16.8 4.0 %shard_map.122.frames.refs_9_ = bf16[12,256,256]{2,1,0:T(8,128)(2,1)S(1)} custom-call(bf16[12,256,256]{2,1,0:T(8,128)(2,1)S(1)} %bitcast.8, bf16[256,256]{1,0:T(8,128)(2,1)S(1)} %copy-done.1, bf16[256,256]{1,0:T(8,128)(2,1)S(1)} %copy-done.2), custom_call_target="tpu_custom_call" | custom-call | flops 805306368 | bytes 3145728 | tf_op jit(solution)/shard_map/pallas_call | solution.py:372
  21.2 12.3 %collective-permute-start.3 = (bf16[2,256,256]{2,1,0:T(8,128)(2,1)}, bf16[2,256,256]{2,1,0:T(8,128)(2,1)S(1)}, u32[]{:S(2)}, u32[]{:S(2)}) collective-permute-start(bf16[2,256,256]{2,1,0:T(8,128)(2,1)} %collective-permute-done.2.refs_4_), channel_id=1, source_target_pairs={{8,0},{16,8},{24,16},{32,24},{40,32},{48,40},{56,48},{64,56},{72,6... | collective-permute-start | bytes 786440 | tf_op jit(solution)/shard_map/ppermute | solution.py:19
  33.5 1.1 copy-done.12
  34.7 4.8 %shard_map.123 = (f32[2,256,768]{2,1,0:T(8,128)S(1)}, bf16[2,256,768]{2,1,0:T(8,128)(2,1)S(1)}, f32[2,2,512,128]{3,2,1,0:T(8,128)S(1)}, f32[2,2,256,256]{3,2,1,0:T(8,128)S(1)}) custom-call(s32[12,2]{1,0:T(8,128)S(1)} %copy.13.pos.refs_0_, s32[1]{0:T(128)} %bitcast.6.cnt, bf16[2,256,1024]{2,1,0:T(8,128)(2,1)S(1)} %copy-done.3, ...), custom_call_target="tpu_custom_call" | custom-call | flops 9663676416 | bytes 12582912 | tf_op jit(solution)/shard_map/pallas_call | solution.py:398
  40.4 1.2 copy-done.6
  41.6 3.1 %shard_map.124 = (f32[2,256,256]{2,1,0:T(8,128)S(1)}, bf16[2,256,512]{2,1,0:T(8,128)(2,1)S(1)}, bf16[2,256,256]{2,1,0:T(8,128)(2,1)S(1)}, f32[2,2,256,256]{3,2,1,0:T(8,128)S(1)}) custom-call(s32[12,2]{1,0:T(8,128)S(1)} %copy.13.pos.refs_0_, s32[1]{0:T(128)} %bitcast.7.refs_1_, bf16[2,256,1024]{2,1,0:T(8,128)(2,1)S(1)} %copy-done.3, ...), custom_call_target="tpu_custom_call" | custom-call | flops 3221225472 | bytes 12582912 | tf_op jit(solution)/shard_map/pallas_call | solution.py:414
  46.3 5.1 %collective-permute-start.6 = (bf16[512,256]{1,0:T(8,128)(2,1)}, bf16[512,256]{1,0:T(8,128)(2,1)}, u32[]{:S(2)}, u32[]{:S(2)}) collective-permute-start(bf16[512,256]{1,0:T(8,128)(2,1)} %dynamic-slice_convert_fusion), channel_id=1, source_target_pairs={{0,8},{8,0},{16,24},{24,16},{32,40},{40,32},{48,56},{56,48},{64,72... | collective-permute-start | bytes 786440 | tf_op jit(solution)/shard_map/ppermute | solution.py:35
  51.4 1.5 %collective-permute-done.6 = bf16[512,256]{1,0:T(8,128)(2,1)} collective-permute-done((bf16[512,256]{1,0:T(8,128)(2,1)}, bf16[512,256]{1,0:T(8,128)(2,1)}, u32[]{:S(2)}, u32[]{:S(2)}) %collective-permute-start.6) | collective-permute-done | bytes 262176 | tf_op jit(solution)/shard_map/ppermute | solution.py:35
  54.7 1.3 collective-permute-start.7
  56.0 4.1 %collective-permute-start.8 = (bf16[128,256]{1,0:T(8,128)(2,1)S(1)}, bf16[128,256]{1,0:T(8,128)(2,1)S(1)}, u32[]{:S(2)}, u32[]{:S(2)}) collective-permute-start(bf16[128,256]{1,0:T(8,128)(2,1)S(1)} %get-tuple-element.34), channel_id=1, source_target_pairs={{0,128},{8,136},{16,144},{24,152},{32,160},{40,168},{48,176},{56,1... | collective-permute-start | bytes 196616 | tf_op jit(solution)/shard_map/ppermute | solution.py:35
  60.1 2.9 %collective-permute-done.8 = bf16[128,256]{1,0:T(8,128)(2,1)S(1)} collective-permute-done((bf16[128,256]{1,0:T(8,128)(2,1)S(1)}, bf16[128,256]{1,0:T(8,128)(2,1)S(1)}, u32[]{:S(2)}, u32[]{:S(2)}) %collective-permute-start.8) | collective-permute-done | bytes 65568 | tf_op jit(solution)/shard_map/ppermute | solution.py:35
  63.0 1.5 %collective-permute-done.9 = bf16[128,256]{1,0:T(8,128)(2,1)S(1)} collective-permute-done((bf16[128,256]{1,0:T(8,128)(2,1)S(1)}, bf16[128,256]{1,0:T(8,128)(2,1)S(1)}, u32[]{:S(2)}, u32[]{:S(2)}) %collective-permute-start.9) | collective-permute-done | bytes 65568 | tf_op jit(solution)/shard_map/ppermute | solution.py:35
  65.5 8.6 %collective-permute-start.10 = (bf16[128,256]{1,0:T(8,128)(2,1)S(1)}, bf16[128,256]{1,0:T(8,128)(2,1)S(1)}, u32[]{:S(2)}, u32[]{:S(2)}) collective-permute-start(bf16[128,256]{1,0:T(8,128)(2,1)S(1)} %add_convert_fusion.4), channel_id=1, source_target_pairs={{0,2},{1,3},{2,0},{3,1},{4,6},{5,7},{6,4},{7,5},{8,10},{9,11},{10,... | collective-permute-start | bytes 196616 | tf_op jit(solution)/shard_map/ppermute | solution.py:35
  74.1 1.3 collective-permute-start.12
  75.7 3.0 %collective-permute-done.11 = bf16[128,256]{1,0:T(8,128)(2,1)S(1)} collective-permute-done((bf16[128,256]{1,0:T(8,128)(2,1)S(1)}, bf16[128,256]{1,0:T(8,128)(2,1)S(1)}, u32[]{:S(2)}, u32[]{:S(2)}) %collective-permute-start.11) | collective-permute-done | bytes 65568 | tf_op jit(solution)/shard_map/ppermute | solution.py:35
  78.8 3.5 %collective-permute-start.13 = (bf16[128,256]{1,0:T(8,128)(2,1)S(1)}, bf16[128,256]{1,0:T(8,128)(2,1)S(1)}, u32[]{:S(2)}, u32[]{:S(2)}) collective-permute-start(bf16[128,256]{1,0:T(8,128)(2,1)S(1)} %add_convert_fusion.3), channel_id=1, source_target_pairs={{0,16},{8,24},{16,0},{24,8},{32,48},{40,56},{48,32},{56,40},{64,80... | collective-permute-start | bytes 196616 | tf_op jit(solution)/shard_map/ppermute | solution.py:35
  82.2 5.7 %collective-permute-start.14 = (bf16[128,256]{1,0:T(8,128)(2,1)S(1)}, bf16[128,256]{1,0:T(8,128)(2,1)S(1)}, u32[]{:S(2)}, u32[]{:S(2)}) collective-permute-start(bf16[128,256]{1,0:T(8,128)(2,1)S(1)} %add_convert_fusion.3), channel_id=1, source_target_pairs={{0,32},{8,40},{16,48},{24,56},{32,0},{40,8},{48,16},{56,24},{64,96... | collective-permute-start | bytes 196616 | tf_op jit(solution)/shard_map/ppermute | solution.py:35
  88.0 7.0 %collective-permute-start.4 = (bf16[2,256,512]{2,1,0:T(8,128)(2,1)}, bf16[2,256,512]{2,1,0:T(8,128)(2,1)S(1)}, u32[]{:S(2)}, u32[]{:S(2)}) collective-permute-start(bf16[2,256,512]{2,1,0:T(8,128)(2,1)} %copy-done.8), channel_id=1, source_target_pairs={{0,8},{8,16},{16,24},{24,32},{32,40},{40,48},{48,56},{56,64},{64,7... | collective-permute-start | bytes 1572872 | tf_op jit(solution)/shard_map/ppermute | solution.py:19
  95.2 3.9 %collective-permute-start.1 = (bf16[2,256,768]{2,1,0:T(8,128)(2,1)}, bf16[2,256,768]{2,1,0:T(8,128)(2,1)S(1)}, u32[]{:S(2)}, u32[]{:S(2)}) collective-permute-start(bf16[2,256,768]{2,1,0:T(8,128)(2,1)} %copy-done.7), channel_id=1, source_target_pairs={{0,8},{8,16},{16,24},{24,32},{32,40},{40,48},{48,56},{56,64},{64,7... | collective-permute-start | bytes 2359304 | tf_op jit(solution)/shard_map/ppermute | solution.py:19
  99.1 3.3 %collective-permute-done.16 = bf16[128,256]{1,0:T(8,128)(2,1)S(1)} collective-permute-done((bf16[128,256]{1,0:T(8,128)(2,1)S(1)}, bf16[128,256]{1,0:T(8,128)(2,1)S(1)}, u32[]{:S(2)}, u32[]{:S(2)}) %collective-permute-start.16) | collective-permute-done | bytes 65568 | tf_op jit(solution)/shard_map/ppermute | solution.py:35
  103.1 1.2 collective-permute-done.4
  104.4 3.4 %collective-permute-start.5 = (bf16[2,256,256]{2,1,0:T(8,128)(2,1)S(1)}, bf16[2,256,256]{2,1,0:T(8,128)(2,1)S(1)}, u32[]{:S(2)}, u32[]{:S(2)}) collective-permute-start(bf16[2,256,256]{2,1,0:T(8,128)(2,1)S(1)} %get-tuple-element.35), channel_id=1, source_target_pairs={{0,1},{1,2},{2,3},{3,4},{4,5},{5,6},{6,7},{8,9},{9,10},{10,11},{11... | collective-permute-start | bytes 786440 | tf_op jit(solution)/shard_map/ppermute | solution.py:19
  107.8 2.2 %collective-permute-start.18 = (bf16[128,256]{1,0:T(8,128)(2,1)S(1)}, bf16[128,256]{1,0:T(8,128)(2,1)S(1)}, u32[]{:S(2)}, u32[]{:S(2)}) collective-permute-start(bf16[128,256]{1,0:T(8,128)(2,1)S(1)} %get-tuple-element.31), channel_id=1, source_target_pairs={{0,128},{8,136},{16,144},{24,152},{32,160},{40,168},{48,176},{56,1... | collective-permute-start | bytes 196616 | tf_op jit(solution)/shard_map/ppermute | solution.py:35
  111.1 1.5 %collective-permute-done.18 = bf16[128,256]{1,0:T(8,128)(2,1)S(1)} collective-permute-done((bf16[128,256]{1,0:T(8,128)(2,1)S(1)}, bf16[128,256]{1,0:T(8,128)(2,1)S(1)}, u32[]{:S(2)}, u32[]{:S(2)}) %collective-permute-start.18) | collective-permute-done | bytes 65568 | tf_op jit(solution)/shard_map/ppermute | solution.py:35
  112.5 1.8 %collective-permute-done.19 = bf16[128,256]{1,0:T(8,128)(2,1)S(1)} collective-permute-done((bf16[128,256]{1,0:T(8,128)(2,1)S(1)}, bf16[128,256]{1,0:T(8,128)(2,1)S(1)}, u32[]{:S(2)}, u32[]{:S(2)}) %collective-permute-start.19) | collective-permute-done | bytes 65568 | tf_op jit(solution)/shard_map/ppermute | solution.py:35
  114.4 3.8 %collective-permute-start.20 = (bf16[512,256]{1,0:T(8,128)(2,1)S(1)}, bf16[512,256]{1,0:T(8,128)(2,1)S(1)}, u32[]{:S(2)}, u32[]{:S(2)}) collective-permute-start(bf16[512,256]{1,0:T(8,128)(2,1)S(1)} %constant_dynamic-update-slice_fusion.2), channel_id=1, source_target_pairs={{0,8},{8,0},{16,24},{24,16},{32,40},{40,32},{48,56},{56,48},{64,72... | collective-permute-start | bytes 786440 | tf_op jit(solution)/shard_map/ppermute | solution.py:35
  118.2 4.9 %collective-permute-done.1 = bf16[2,256,768]{2,1,0:T(8,128)(2,1)S(1)} collective-permute-done((bf16[2,256,768]{2,1,0:T(8,128)(2,1)}, bf16[2,256,768]{2,1,0:T(8,128)(2,1)S(1)}, u32[]{:S(2)}, u32[]{:S(2)}) %collective-permute-start.1) | collective-permute-done | bytes 786464 | tf_op jit(solution)/shard_map/ppermute | solution.py:19
  123.6 4.9 %collective-permute-done.5 = bf16[2,256,256]{2,1,0:T(8,128)(2,1)S(1)} collective-permute-done((bf16[2,256,256]{2,1,0:T(8,128)(2,1)S(1)}, bf16[2,256,256]{2,1,0:T(8,128)(2,1)S(1)}, u32[]{:S(2)}, u32[]{:S(2)}) %collective-permute-start.5) | collective-permute-done | bytes 262176 | tf_op jit(solution)/shard_map/ppermute | solution.py:19
  128.7 1.2 convert.1
  (66 shorter events, 12.7 us)
Async XLA Ops:
  0.6 32.8 %collective-permute-start = (bf16[2,256,1024]{2,1,0:T(8,128)(2,1)}, bf16[2,256,1024]{2,1,0:T(8,128)(2,1)S(1)}, u32[]{:S(2)}, u32[]{:S(2)}) collective-permute-start(bf16[2,256,1024]{2,1,0:T(8,128)(2,1)} %refs_2_.1), channel_id=1, source_target_pairs={{8,0},{16,8},{24,16},{32,24},{40,32},{48,40},{56,48},{64,56},{72,6... | collective-permute-start | bytes 3145736 | tf_op jit(solution)/shard_map/ppermute | solution.py:19
  4.2 17.0 %collective-permute-start.2 = (bf16[2,256,256]{2,1,0:T(8,128)(2,1)S(1)}, bf16[2,256,256]{2,1,0:T(8,128)(2,1)}, u32[]{:S(2)}, u32[]{:S(2)}) collective-permute-start(bf16[2,256,256]{2,1,0:T(8,128)(2,1)S(1)} %slice.34), channel_id=1, source_target_pairs={{1,0},{2,1},{3,2},{4,3},{5,4},{6,5},{7,6},{9,8},{10,9},{11,10},{12... | collective-permute-start | bytes 786440 | tf_op jit(solution)/shard_map/ppermute | solution.py:19
  13.5 1.4 %copy-start = (bf16[1,1,12,256,256]{4,3,2,1,0:T(8,128)(2,1)S(1)}, bf16[1,1,12,256,256]{4,3,2,1,0:T(8,128)(2,1)}, u32[]{:S(2)}) copy-start(bf16[1,1,12,256,256]{4,3,2,1,0:T(8,128)(2,1)} %param.15) | copy-start | bytes 4718596
  16.8 16.7 %copy-start.3 = (bf16[2,256,1024]{2,1,0:T(8,128)(2,1)S(1)}, bf16[2,256,1024]{2,1,0:T(8,128)(2,1)}, u32[]{:S(2)}) copy-start(bf16[2,256,1024]{2,1,0:T(8,128)(2,1)} %refs_2_.1) | copy-start | bytes 3145732
  16.8 16.7 %copy-start.4 = (f32[2,2,256,256]{3,2,1,0:T(8,128)S(1)}, f32[2,2,256,256]{3,2,1,0:T(8,128)}, u32[]{:S(2)}) copy-start(f32[2,2,256,256]{3,2,1,0:T(8,128)} %refs_8_.1) | copy-start | bytes 3145732
  16.8 16.7 %copy-start.9 = (bf16[512,512]{1,0:T(8,128)(2,1)S(1)}, bf16[512,512]{1,0:T(8,128)(2,1)}, u32[]{:S(2)}) copy-start(bf16[512,512]{1,0:T(8,128)(2,1)} %constant.61.clone.left.refs_10_) | copy-start | bytes 1572868
  16.8 16.8 %copy-start.10 = (bf16[512,512]{1,0:T(8,128)(2,1)S(1)}, bf16[512,512]{1,0:T(8,128)(2,1)}, u32[]{:S(2)}) copy-start(bf16[512,512]{1,0:T(8,128)(2,1)} %constant.62.clone.right.refs_11_) | copy-start | bytes 1572868
  16.8 16.8 %copy-start.11 = (bf16[2,256,256]{2,1,0:T(8,128)(2,1)S(1)}, bf16[2,256,256]{2,1,0:T(8,128)(2,1)}, u32[]{:S(2)}) copy-start(bf16[2,256,256]{2,1,0:T(8,128)(2,1)} %constant.63.clone.gl.refs_12_) | copy-start | bytes 786436
  21.2 19.2 %collective-permute-start.3 = (bf16[2,256,256]{2,1,0:T(8,128)(2,1)}, bf16[2,256,256]{2,1,0:T(8,128)(2,1)S(1)}, u32[]{:S(2)}, u32[]{:S(2)}) collective-permute-start(bf16[2,256,256]{2,1,0:T(8,128)(2,1)} %collective-permute-done.2.refs_4_), channel_id=1, source_target_pairs={{8,0},{16,8},{24,16},{32,24},{40,32},{48,40},{56,48},{64,56},{72,6... | collective-permute-start | bytes 786440 | tf_op jit(solution)/shard_map/ppermute | solution.py:19
  33.5 6.0 %copy-start.5 = (bf16[2,256,1024]{2,1,0:T(8,128)(2,1)}, bf16[2,256,1024]{2,1,0:T(8,128)(2,1)S(1)}, u32[]{:S(2)}) copy-start(bf16[2,256,1024]{2,1,0:T(8,128)(2,1)S(1)} %collective-permute-done.below.refs_3_) | copy-start | bytes 3145732
  33.5 1.1 copy-start.12
  34.7 5.7 %copy-start.13 = (bf16[2,256,256]{2,1,0:T(8,128)(2,1)S(1)}, bf16[2,256,256]{2,1,0:T(8,128)(2,1)}, u32[]{:S(2)}) copy-start(bf16[2,256,256]{2,1,0:T(8,128)(2,1)} %constant.64.clone.gr.refs_13_) | copy-start | bytes 786436
  40.4 1.2 copy-start.6
  46.3 6.6 %collective-permute-start.6 = (bf16[512,256]{1,0:T(8,128)(2,1)}, bf16[512,256]{1,0:T(8,128)(2,1)}, u32[]{:S(2)}, u32[]{:S(2)}) collective-permute-start(bf16[512,256]{1,0:T(8,128)(2,1)} %dynamic-slice_convert_fusion), channel_id=1, source_target_pairs={{0,8},{8,0},{16,24},{24,16},{32,40},{40,32},{48,56},{56,48},{64,72... | collective-permute-start | bytes 786440 | tf_op jit(solution)/shard_map/ppermute | solution.py:35
  54.7 5.4 %collective-permute-start.7 = (bf16[128,256]{1,0:T(8,128)(2,1)S(1)}, bf16[128,256]{1,0:T(8,128)(2,1)S(1)}, u32[]{:S(2)}, u32[]{:S(2)}) collective-permute-start(bf16[128,256]{1,0:T(8,128)(2,1)S(1)} %get-tuple-element.32), channel_id=1, source_target_pairs={{0,64},{8,72},{16,80},{24,88},{32,96},{40,104},{48,112},{56,120},{... | collective-permute-start | bytes 196616 | tf_op jit(solution)/shard_map/ppermute | solution.py:35
  56.0 7.1 %collective-permute-start.8 = (bf16[128,256]{1,0:T(8,128)(2,1)S(1)}, bf16[128,256]{1,0:T(8,128)(2,1)S(1)}, u32[]{:S(2)}, u32[]{:S(2)}) collective-permute-start(bf16[128,256]{1,0:T(8,128)(2,1)S(1)} %get-tuple-element.34), channel_id=1, source_target_pairs={{0,128},{8,136},{16,144},{24,152},{32,160},{40,168},{48,176},{56,1... | collective-permute-start | bytes 196616 | tf_op jit(solution)/shard_map/ppermute | solution.py:35
  60.1 4.5 %collective-permute-start.9 = (bf16[128,256]{1,0:T(8,128)(2,1)S(1)}, bf16[128,256]{1,0:T(8,128)(2,1)S(1)}, u32[]{:S(2)}, u32[]{:S(2)}) collective-permute-start(bf16[128,256]{1,0:T(8,128)(2,1)S(1)} %get-tuple-element.33), channel_id=1, source_target_pairs={{0,192},{8,200},{16,208},{24,216},{32,224},{40,232},{48,240},{56,2... | collective-permute-start | bytes 196616 | tf_op jit(solution)/shard_map/ppermute | solution.py:35
  65.5 10.3 %collective-permute-start.10 = (bf16[128,256]{1,0:T(8,128)(2,1)S(1)}, bf16[128,256]{1,0:T(8,128)(2,1)S(1)}, u32[]{:S(2)}, u32[]{:S(2)}) collective-permute-start(bf16[128,256]{1,0:T(8,128)(2,1)S(1)} %add_convert_fusion.4), channel_id=1, source_target_pairs={{0,2},{1,3},{2,0},{3,1},{4,6},{5,7},{6,4},{7,5},{8,10},{9,11},{10,... | collective-permute-start | bytes 196616 | tf_op jit(solution)/shard_map/ppermute | solution.py:35
  74.1 4.6 %collective-permute-start.11 = (bf16[128,256]{1,0:T(8,128)(2,1)S(1)}, bf16[128,256]{1,0:T(8,128)(2,1)S(1)}, u32[]{:S(2)}, u32[]{:S(2)}) collective-permute-start(bf16[128,256]{1,0:T(8,128)(2,1)S(1)} %add_convert_fusion.4), channel_id=1, source_target_pairs={{0,4},{1,5},{2,6},{3,7},{4,0},{5,1},{6,2},{7,3},{8,12},{9,13},{10,... | collective-permute-start | bytes 196616 | tf_op jit(solution)/shard_map/ppermute | solution.py:35
  74.1 4.6 %collective-permute-start.12 = (bf16[128,256]{1,0:T(8,128)(2,1)S(1)}, bf16[128,256]{1,0:T(8,128)(2,1)S(1)}, u32[]{:S(2)}, u32[]{:S(2)}) collective-permute-start(bf16[128,256]{1,0:T(8,128)(2,1)S(1)} %add_convert_fusion.4), channel_id=1, source_target_pairs={{0,6},{1,7},{2,4},{3,5},{4,2},{5,3},{6,0},{7,1},{8,14},{9,15},{10,... | collective-permute-start | bytes 196616 | tf_op jit(solution)/shard_map/ppermute | solution.py:35
  78.8 16.3 %collective-permute-start.13 = (bf16[128,256]{1,0:T(8,128)(2,1)S(1)}, bf16[128,256]{1,0:T(8,128)(2,1)S(1)}, u32[]{:S(2)}, u32[]{:S(2)}) collective-permute-start(bf16[128,256]{1,0:T(8,128)(2,1)S(1)} %add_convert_fusion.3), channel_id=1, source_target_pairs={{0,16},{8,24},{16,0},{24,8},{32,48},{40,56},{48,32},{56,40},{64,80... | collective-permute-start | bytes 196616 | tf_op jit(solution)/shard_map/ppermute | solution.py:35
  82.2 12.8 %collective-permute-start.14 = (bf16[128,256]{1,0:T(8,128)(2,1)S(1)}, bf16[128,256]{1,0:T(8,128)(2,1)S(1)}, u32[]{:S(2)}, u32[]{:S(2)}) collective-permute-start(bf16[128,256]{1,0:T(8,128)(2,1)S(1)} %add_convert_fusion.3), channel_id=1, source_target_pairs={{0,32},{8,40},{16,48},{24,56},{32,0},{40,8},{48,16},{56,24},{64,96... | collective-permute-start | bytes 196616 | tf_op jit(solution)/shard_map/ppermute | solution.py:35
  88.0 7.1 %collective-permute-start.15 = (bf16[128,256]{1,0:T(8,128)(2,1)S(1)}, bf16[128,256]{1,0:T(8,128)(2,1)S(1)}, u32[]{:S(2)}, u32[]{:S(2)}) collective-permute-start(bf16[128,256]{1,0:T(8,128)(2,1)S(1)} %add_convert_fusion.3), channel_id=1, source_target_pairs={{0,48},{8,56},{16,32},{24,40},{32,16},{40,24},{48,0},{56,8},{64,11... | collective-permute-start | bytes 196616 | tf_op jit(solution)/shard_map/ppermute | solution.py:35
  88.0 16.3 %collective-permute-start.4 = (bf16[2,256,512]{2,1,0:T(8,128)(2,1)}, bf16[2,256,512]{2,1,0:T(8,128)(2,1)S(1)}, u32[]{:S(2)}, u32[]{:S(2)}) collective-permute-start(bf16[2,256,512]{2,1,0:T(8,128)(2,1)} %copy-done.8), channel_id=1, source_target_pairs={{0,8},{8,16},{16,24},{24,32},{32,40},{40,48},{48,56},{56,64},{64,7... | collective-permute-start | bytes 1572872 | tf_op jit(solution)/shard_map/ppermute | solution.py:19
  95.1 7.3 %collective-permute-start.16 = (bf16[128,256]{1,0:T(8,128)(2,1)S(1)}, bf16[128,256]{1,0:T(8,128)(2,1)S(1)}, u32[]{:S(2)}, u32[]{:S(2)}) collective-permute-start(bf16[128,256]{1,0:T(8,128)(2,1)S(1)} %add_convert_fusion.2), channel_id=1, source_target_pairs={{0,1},{1,0},{2,3},{3,2},{4,5},{5,4},{6,7},{7,6},{8,9},{9,8},{10,11... | collective-permute-start | bytes 196616 | tf_op jit(solution)/shard_map/ppermute | solution.py:35
  95.2 27.9 %collective-permute-start.1 = (bf16[2,256,768]{2,1,0:T(8,128)(2,1)}, bf16[2,256,768]{2,1,0:T(8,128)(2,1)S(1)}, u32[]{:S(2)}, u32[]{:S(2)}) collective-permute-start(bf16[2,256,768]{2,1,0:T(8,128)(2,1)} %copy-done.7), channel_id=1, source_target_pairs={{0,8},{8,16},{16,24},{24,32},{32,40},{40,48},{48,56},{56,64},{64,7... | collective-permute-start | bytes 2359304 | tf_op jit(solution)/shard_map/ppermute | solution.py:19
  102.4 8.6 %collective-permute-start.17 = (bf16[128,256]{1,0:T(8,128)(2,1)S(1)}, bf16[128,256]{1,0:T(8,128)(2,1)S(1)}, u32[]{:S(2)}, u32[]{:S(2)}) collective-permute-start(bf16[128,256]{1,0:T(8,128)(2,1)S(1)} %get-tuple-element.31), channel_id=1, source_target_pairs={{0,64},{8,72},{16,80},{24,88},{32,96},{40,104},{48,112},{56,120},{... | collective-permute-start | bytes 196616 | tf_op jit(solution)/shard_map/ppermute | solution.py:35
  104.4 24.1 %collective-permute-start.5 = (bf16[2,256,256]{2,1,0:T(8,128)(2,1)S(1)}, bf16[2,256,256]{2,1,0:T(8,128)(2,1)S(1)}, u32[]{:S(2)}, u32[]{:S(2)}) collective-permute-start(bf16[2,256,256]{2,1,0:T(8,128)(2,1)S(1)} %get-tuple-element.35), channel_id=1, source_target_pairs={{0,1},{1,2},{2,3},{3,4},{4,5},{5,6},{6,7},{8,9},{9,10},{10,11},{11... | collective-permute-start | bytes 786440 | tf_op jit(solution)/shard_map/ppermute | solution.py:19
  107.8 4.7 %collective-permute-start.18 = (bf16[128,256]{1,0:T(8,128)(2,1)S(1)}, bf16[128,256]{1,0:T(8,128)(2,1)S(1)}, u32[]{:S(2)}, u32[]{:S(2)}) collective-permute-start(bf16[128,256]{1,0:T(8,128)(2,1)S(1)} %get-tuple-element.31), channel_id=1, source_target_pairs={{0,128},{8,136},{16,144},{24,152},{32,160},{40,168},{48,176},{56,1... | collective-permute-start | bytes 196616 | tf_op jit(solution)/shard_map/ppermute | solution.py:35
  110.0 4.3 %collective-permute-start.19 = (bf16[128,256]{1,0:T(8,128)(2,1)S(1)}, bf16[128,256]{1,0:T(8,128)(2,1)S(1)}, u32[]{:S(2)}, u32[]{:S(2)}) collective-permute-start(bf16[128,256]{1,0:T(8,128)(2,1)S(1)} %get-tuple-element.31), channel_id=1, source_target_pairs={{0,192},{8,200},{16,208},{24,216},{32,224},{40,232},{48,240},{56,2... | collective-permute-start | bytes 196616 | tf_op jit(solution)/shard_map/ppermute | solution.py:35
  114.4 14.3 %collective-permute-start.20 = (bf16[512,256]{1,0:T(8,128)(2,1)S(1)}, bf16[512,256]{1,0:T(8,128)(2,1)S(1)}, u32[]{:S(2)}, u32[]{:S(2)}) collective-permute-start(bf16[512,256]{1,0:T(8,128)(2,1)S(1)} %constant_dynamic-update-slice_fusion.2), channel_id=1, source_target_pairs={{0,8},{8,0},{16,24},{24,16},{32,40},{40,32},{48,56},{56,48},{64,72... | collective-permute-start | bytes 786440 | tf_op jit(solution)/shard_map/ppermute | solution.py:35
  128.6 1.7 %copy-start.14 = (f32[2,256,1024]{2,1,0:T(8,128)}, f32[2,256,1024]{2,1,0:T(8,128)S(1)}, u32[]{:S(2)}) copy-start(f32[2,256,1024]{2,1,0:T(8,128)S(1)} %fusion) | copy-start | bytes 6291460
  (5 other events, 4.3 us)
where the time goes:
time: 131 us; the launch traced here: 130 us
  starting transfers between devices  74.5 us (57%)
  waiting for transfers between devices  27.3 us (21%)
  Pallas kernels  11.9 us (9%)
  local copies, waits for them, and re-layouts  11.1 us (8%)
  other arithmetic  3.91 us (3%)
  between operations  1.63 us (1%)
    ppermute x15, starting transfers between devices, partner(): lax.ppermute(v, axis, [(i, i ^ d << low) for i in range(lax.axis_size(axi...  37.4 us
    ppermute x6, starting transfers between devices, shifted(): return lax.ppermute(x, axis, pairs)  37 us
    ppermute x15, waiting for transfers between devices, partner(): lax.ppermute(v, axis, [(i, i ^ d << low) for i in range(lax.axis_size(axi...  15.9 us
    ppermute x6, waiting for transfers between devices, shifted(): return lax.ppermute(x, axis, pairs)  11.3 us
    unnamed x32, local copies, waits for them, and re-layouts  8.5 us
    pallas_call x1, Pallas kernels, body(): pl.pallas_call(inner_kernel, out_shape=(jax.ShapeDtypeStruct((2, tile_row...  4.79 us
    pallas_call x1, Pallas kernels, body(): pl.pallas_call(prep_kernel, out_shape=jax.ShapeDtypeStruct(measured.shape...  4.03 us
    pallas_call x1, Pallas kernels, body(): pl.pallas_call(lambda *refs: edge_kernel(scale, *refs), out_shape=(jax.Sh...  3.13 us
  transfers between devices with their start and end apart: 21, of which 12 were waited for; matrix products, arithmetic and copies ran while one was open for 2% of the time, Pallas kernels for 7%

commit v1 on v0

--- a/solution.py
+++ b/solution.py
@@ -20,28 +20,36 @@
 
 
 FIELDS = {
-    "core": ("row", 0, 1),
-    "zlo": ("row", 1, 2),
-    "y": ("row", 3, 2),
-    "row_hi": ("row", 1, 4),
-    "zhi": ("col", 0, 1),
-    "x": ("col", 1, 2),
-    "col": ("col", 0, 3),
+    "core": ([(1, 0)], 0),
+    "y": ([(8, 0), (16, 0), (24, 0)], 3),
+    "x": ([(0, 2), (0, 4), (0, 6)], None),
+    "z0": ([(2, 0)], None),
+    "z1": ([(4, 0)], None),
+    "z2": ([(4, 1)], None),
 }
 
 
 def partner(v, field, d):
-    axis, low, _ = FIELDS[field]
-    return lax.ppermute(v, axis, [(i, i ^ (d << low)) for i in range(lax.axis_size(axis))])
+    row, col = FIELDS[field][0][d - 1]
+    if not col:
+        return lax.ppermute(v, "row", [(i, i ^ row) for i in range(lax.axis_size("row"))])
+    if not row:
+        return lax.ppermute(v, "col", [(i, i ^ col) for i in range(lax.axis_size("col"))])
+    rows, cols = lax.axis_size("row"), lax.axis_size("col")
+    pairs = [(r * cols + c, (r ^ row) * cols + (c ^ col)) for r in range(rows) for c in range(cols)]
+    return lax.ppermute(v, ("row", "col"), pairs)
+
+
+def members(field):
+    return len(FIELDS[field][0]) + 1
 
 
 def place(field):
-    axis, low, bits = FIELDS[field]
-    return (lax.axis_index(axis) >> low) & ((1 << bits) - 1)
+    return (lax.axis_index("row") >> FIELDS[field][1]) & (members(field) - 1)
 
 
 def scatter_sum(v, field, dtype):
-    n = 1 << FIELDS[field][2]
+    n = members(field)
     g = place(field)
     k = v.shape[0] // n
     total = lax.dynamic_slice_in_dim(v, g * k, k, 0)
@@ -55,7 +63,7 @@
 
 
 def full_sum(v, field, dtype):
-    n = 1 << FIELDS[field][2]
+    n = members(field)
     sent = v.astype(dtype)
     parts = [sent.astype(f32)] + [partner(sent, field, d).astype(f32) for d in range(1, n)]
     while len(parts) > 1:
@@ -64,7 +72,7 @@
 
 
 def gather(v, field, dtype):
-    n = 1 << FIELDS[field][2]
+    n = members(field)
     g = place(field)
     k = v.shape[0]
     sent = v.astype(dtype)
@@ -77,17 +85,18 @@
 
 
 PLAN = (
-    (scatter_sum, "core", bf16),
     (scatter_sum, "y", bf16),
     (full_sum, "x", bf16),
-    (full_sum, "zlo", bf16),
-    (full_sum, "zhi", bf16),
+    (full_sum, "z0", bf16),
+    (full_sum, "z1", bf16),
+    (full_sum, "z2", bf16),
     (gather, "y", bf16),
     (gather, "core", bf16),
 )
 
 
-def reduce_all(v):
+def reduce_all(keep, send):
+    v = keep + partner(send, "core", 1).astype(f32)
     for step, field, dtype in PLAN:
         v = step(v, field, dtype)
     return v.astype(f32)
@@ -303,15 +312,32 @@
                 ].astype(dst.dtype)
 
 
+def fetch(sources, targets, sems):
+    copies = [pltpu.make_async_copy(s, d, sems.at[k]) for k, (s, d) in enumerate(zip(sources, targets))]
+    for copy in copies:
+        copy.start()
+    return copies
+
+
 def inner_kernel(
-    pos, cnt, own, below, probe, frames, left, right, gl, gr,
+    pos, cnt, own_hbm, below_hbm, probe_hbm, frames_hbm, left_hbm, right_hbm, gl_hbm, gr_hbm,
     g_own, g_below, carry, p_out,
-    ext, gext, *scratch,
+    own, below, probe, frames, left, right, gl, gr, sems, ext, gext, *scratch,
 ):
+    copies = fetch(
+        (own_hbm, below_hbm, probe_hbm, left_hbm, right_hbm, gl_hbm, gr_hbm, frames_hbm),
+        (own, below, probe, left, right, gl, gr, frames),
+        sems,
+    )
     n = probe.shape[-1]
     tr, tc = own.shape[1:]
     inner = tc - n
-    fill(ext, ((own, 0, tc, 0, 0), (below, 0, tc, tr, 0)))
+    copies[0].wait()
+    fill(ext, ((own, 0, tc, 0, 0),))
+    copies[1].wait()
+    fill(ext, ((below, 0, tc, tr, 0),))
+    for copy in copies[2:]:
+        copy.wait()
 
     def clear():
         gext[...] = jnp.zeros_like(gext)
@@ -328,19 +354,31 @@
 
 
 def edge_kernel(
-    scale, pos, cnt, own, below, strip, corner, carry, p_in, probe, frames, left, right, gl, gr,
-    g_own, g_rows, g_strip, p_out,
-    ext, gext, *scratch,
+    scale, pos, cnt, core, own_hbm, below_hbm, strip_hbm, corner_hbm, carry_hbm, p_hbm, probe_hbm, frames_hbm,
+    left_hbm, right_hbm, gl_hbm, gr_hbm,
+    g_own, g_rows, g_strip, p_keep, p_send,
+    own, below, strip, corner, carry, p_in, probe, frames, left, right, gl, gr, sems, p_out, ext, gext, *scratch,
 ):
     n = probe.shape[-1]
-    tr, tc = own.shape[1:]
+    tr, tc = own_hbm.shape[1:]
     inner = tc - n
-    fill(
-        ext,
-        ((own, inner, tc, 0, 0), (below, inner, tc, tr, 0), (strip, 0, n, 0, n), (corner, 0, n, tr, n)),
-    )
+    copies = fetch(
+        (
+            own_hbm.at[:, :, inner:tc], below_hbm.at[:, :, inner:tc], strip_hbm, corner_hbm, probe_hbm,
+            left_hbm, right_hbm, gl_hbm, gr_hbm, frames_hbm, p_hbm, carry_hbm,
+        ),
+        (own, below, strip, corner, probe, left, right, gl, gr, frames, p_in, carry),
+        sems,
+    )
+    for copy in copies[:4]:
+        copy.wait()
+    fill(ext, ((own, 0, n, 0, 0), (below, 0, n, tr, 0), (strip, 0, n, 0, n), (corner, 0, n, tr, n)))
+    for copy in copies[4:10]:
+        copy.wait()
 
     def clear():
+        for copy in copies[10:]:
+            copy.wait()
         p_out[...] = p_in[...]
         for p in range(2):
             for b in range(n // 128):
@@ -351,7 +389,8 @@
         pos, cnt, lambda c: c >= inner, inner // 128, 2 * n // 128, clear, probe, frames,
         (left, right, gl, gr), p_out, ext, gext, *scratch,
     )
-    p_out[...] = p_out[...] * scale
+    p_keep[...] = p_out[core[0]] * scale
+    p_send[...] = (p_out[1 - core[0]] * scale).astype(bf16)
     drain(gext, ((g_own, 0, n, 0, 0), (g_rows, 0, 2 * n, tr, 0), (g_strip, 0, n, 0, n)))
 
 
@@ -361,8 +400,10 @@
     slots = measured.shape[2]
     left, right, gl, gr, perm, perm_t = tables(size)
     vmem = pl.BlockSpec(memory_space=pltpu.VMEM)
+    stay = pl.BlockSpec(memory_space=pl.ANY)
     smem = pl.BlockSpec(memory_space=pltpu.SMEM)
     pos, cnt = positions[0, 0], counts[0]
+    core = (lax.axis_index("row") & 1).astype(jnp.int32).reshape(1)
     inner = tile_cols - size
     rows = tile_rows + size
 
@@ -394,7 +435,8 @@
             pltpu.SMEM((slots,), jnp.int32),
         ]
 
-    params = pltpu.CompilerParams(vmem_limit_bytes=32 * 2**20)
+    fixed = [pltpu.VMEM(x.shape, x.dtype) for x in (probe, frames, left, right, gl, gr)]
+    params = pltpu.CompilerParams(vmem_limit_bytes=60 * 2**20)
     g_main, g_band, carry, p_part = pl.pallas_call(
         inner_kernel,
         out_shape=(
@@ -403,34 +445,51 @@
             jax.ShapeDtypeStruct((2, size // 128, rows, 128), f32),
             jax.ShapeDtypeStruct(probe.shape, f32),
         ),
-        in_specs=[smem, smem] + [vmem] * 8,
+        in_specs=[smem, smem] + [stay] * 8,
         out_specs=[vmem] * 4,
-        scratch_shapes=scratch(tile_cols // 128),
+        scratch_shapes=[
+            pltpu.VMEM((2, tile_rows, tile_cols), bf16),
+            pltpu.VMEM((2, size, tile_cols), bf16),
+        ]
+        + fixed
+        + [pltpu.SemaphoreType.DMA((8,))]
+        + scratch(tile_cols // 128),
         compiler_params=params,
         cost_estimate=pl.CostEstimate(flops=9 * 2**30, bytes_accessed=12 * 2**20, transcendentals=0),
     )(pos, cnt, object_field, below, probe, frames, left, right, gl, gr)
     total = slots * lax.axis_size("row") * lax.axis_size("col")
     scale = 1.0 / math.sqrt(total)
-    g_right, g_rows, g_strip, p_sum = pl.pallas_call(
+    g_right, g_rows, g_strip, p_keep, p_send = pl.pallas_call(
         lambda *refs: edge_kernel(scale, *refs),
         out_shape=(
             jax.ShapeDtypeStruct((2, tile_rows, size), f32),
             jax.ShapeDtypeStruct((2, size, 2 * size), bf16),
             jax.ShapeDtypeStruct((2, tile_rows, size), bf16),
-            jax.ShapeDtypeStruct(probe.shape, f32),
+            jax.ShapeDtypeStruct(probe.shape[1:], f32),
+            jax.ShapeDtypeStruct(probe.shape[1:], bf16),
         ),
-        in_specs=[smem, smem] + [vmem] * 12,
-        out_specs=[vmem] * 4,
-        scratch_shapes=scratch(2 * size // 128),
+        in_specs=[smem] * 3 + [stay] * 12,
+        out_specs=[vmem] * 5,
+        scratch_shapes=[
+            pltpu.VMEM((2, tile_rows, size), bf16),
+            pltpu.VMEM((2, size, size), bf16),
+            pltpu.VMEM((2, tile_rows, size), bf16),
+            pltpu.VMEM((2, size, size), bf16),
+            pltpu.VMEM((2, size // 128, rows, 128), f32),
+            pltpu.VMEM(probe.shape, f32),
+        ]
+        + fixed
+        + [pltpu.SemaphoreType.DMA((12,)), pltpu.VMEM(probe.shape, f32)]
+        + scratch(2 * size // 128),
         compiler_params=params,
         cost_estimate=pl.CostEstimate(flops=3 * 2**30, bytes_accessed=12 * 2**20, transcendentals=0),
-    )(pos, cnt, object_field, below, strip, corner, carry, p_part, probe, frames, left, right, gl, gr)
+    )(pos, cnt, core, object_field, below, strip, corner, carry, p_part, probe, frames, left, right, gl, gr)
 
     band = shifted(g_band, "row", 1)
     tail = shifted(g_rows, "row", 1)
     to_right = (g_strip.astype(f32) + tail[:, :, size:].astype(f32)).astype(bf16)
     side = shifted(to_right, "col", 1)
-    probe_grad = reduce_all(p_sum.reshape(-1, size)).reshape(probe.shape)
+    probe_grad = reduce_all(p_keep.reshape(-1, size), p_send.reshape(-1, size)).reshape(probe.shape)
     object_grad = jnp.concatenate(
         [g_main + band.astype(f32), g_right + tail[:, :, :size].astype(f32)], 2
     )

time: 131 us -> 135 us (1.031)
  Pallas kernels: 11.9 us -> 20.1 us
  local copies, waits for them, and re-layouts: 11.1 us -> 8.97 us
    pallas_call x1, Pallas kernels: 4.79 us -> 9.36 us  [body(): pl.pallas_call(inner_kernel, out_shape=(jax.ShapeDtypeStruct((2, tile_row...]
    pallas_call x1, Pallas kernels: 3.13 us -> 6.72 us  [body(): pl.pallas_call(lambda *refs: edge_kernel(scale, *refs), out_shape=(jax.Sh...]
    ppermute x15 -> x14, starting transfers between devices: 37.4 us -> 35.4 us  [the longest x10 25.5 us: partner(): lax.ppermute(v, 'row', [(i, i ^ row) for i in range(lax.axis_size('row'))])]
    unnamed x32 -> x26, local copies, waits for them, and re-layouts: 8.5 us -> 6.48 us
    ppermute x6, waiting for transfers between devices: 11.3 us -> 13 us  [shifted(): return lax.ppermute(x, axis, pairs)]
    ppermute x15 -> x14, waiting for transfers between devices: 15.9 us -> 14.6 us  [the longest x10 10.8 us: partner(): lax.ppermute(v, 'row', [(i, i ^ row) for i in range(lax.axis_size('row'))])]
  transfers between devices with their start and end apart: 21 -> 20, of which waited for: 12 -> 10; matrix products, arithmetic and copies ran while one was open for 2% -> 2% of each run, Pallas kernels for 7% -> 10%
where the time goes in v1:
time: 135 us
  starting transfers between devices  73.2 us (54%)
  waiting for transfers between devices  27.5 us (20%)
  Pallas kernels  20.1 us (15%)
  local copies, waits for them, and re-layouts  8.97 us (7%)
  other arithmetic  3.12 us (2%)
  between operations  1.63 us (1%)
    ppermute x6, starting transfers between devices, shifted(): return lax.ppermute(x, axis, pairs)  37.8 us
    ppermute x10, starting transfers between devices, partner(): lax.ppermute(v, 'row', [(i, i ^ row) for i in range(lax.axis_size('row'))])  25.5 us
    ppermute x6, waiting for transfers between devices, shifted(): return lax.ppermute(x, axis, pairs)  13 us
    ppermute x10, waiting for transfers between devices, partner(): lax.ppermute(v, 'row', [(i, i ^ row) for i in range(lax.axis_size('row'))])  10.8 us
    ppermute x3, starting transfers between devices, partner(): lax.ppermute(v, 'col', [(i, i ^ col) for i in range(lax.axis_size('col'))])  9.76 us
    pallas_call x1, Pallas kernels, body(): pl.pallas_call(inner_kernel, out_shape=(jax.ShapeDtypeStruct((2, tile_row...  9.36 us
    pallas_call x1, Pallas kernels, body(): pl.pallas_call(lambda *refs: edge_kernel(scale, *refs), out_shape=(jax.Sh...  6.72 us
    unnamed x26, local copies, waits for them, and re-layouts  6.48 us
  transfers between devices with their start and end apart: 20, of which 10 were waited for; matrix products, arithmetic and copies ran while one was open for 2% of the time, Pallas kernels for 10%

profile of v1, /device:TPU:35, one launch (start us, length us, event | category | flops | bytes accessed | tf_op | source)
XLA Modules:
  0.0 134.6 jit_solution(5785029505925422341)
XLA Ops:
  0.6 2.6 %collective-permute-start = (bf16[2,256,1024]{2,1,0:T(8,128)(2,1)}, bf16[2,256,1024]{2,1,0:T(8,128)(2,1)S(1)}, u32[]{:S(2)}, u32[]{:S(2)}) collective-permute-start(bf16[2,256,1024]{2,1,0:T(8,128)(2,1)} %refs_3_.1), channel_id=1, source_target_pairs={{8,0},{16,8},{24,16},{32,24},{40,32},{48,40},{56,48},{64,56},{72,6... | collective-permute-start | bytes 3145736 | tf_op jit(solution)/shard_map/ppermute | solution.py:19
  4.2 7.9 %collective-permute-start.2 = (bf16[2,256,256]{2,1,0:T(8,128)(2,1)S(1)}, bf16[2,256,256]{2,1,0:T(8,128)(2,1)S(1)}, u32[]{:S(2)}, u32[]{:S(2)}) collective-permute-start(bf16[2,256,256]{2,1,0:T(8,128)(2,1)S(1)} %slice.34), channel_id=1, source_target_pairs={{1,0},{2,1},{3,2},{4,3},{5,4},{6,5},{7,6},{9,8},{10,9},{11,10},{12... | collective-permute-start | bytes 786440 | tf_op jit(solution)/shard_map/ppermute | solution.py:19
  12.1 1.4 %copy.13.pos.refs_0_ = s32[12,2]{1,0:T(8,128)} copy(s32[12,2]{0,1:T(2,128)} %bitcast.13) | data formatting | bytes 192 | tf_op jit(solution)/shard_map/squeeze | solution.py:405
  14.1 1.4 %copy-done = bf16[1,1,12,256,256]{4,3,2,1,0:T(8,128)(2,1)S(1)} copy-done((bf16[1,1,12,256,256]{4,3,2,1,0:T(8,128)(2,1)S(1)}, bf16[1,1,12,256,256]{4,3,2,1,0:T(8,128)(2,1)}, u32[]{:S(2)}) %copy-start) | copy-done | bytes 1572888
  17.3 4.0 %shard_map.122.frames_hbm.refs_10_ = bf16[12,256,256]{2,1,0:T(8,128)(2,1)S(1)} custom-call(bf16[12,256,256]{2,1,0:T(8,128)(2,1)S(1)} %bitcast.11, bf16[256,256]{1,0:T(8,128)(2,1)S(1)} %copy-done.2, bf16[256,256]{1,0:T(8,128)(2,1)S(1)} %copy-done.3), custom_call_target="tpu_custom_call" | custom-call | flops 805306368 | bytes 3145728 | tf_op jit(solution)/shard_map/pallas_call | solution.py:413
  21.4 1.1 copy-done.1
  22.5 10.8 %collective-permute-start.3 = (bf16[2,256,256]{2,1,0:T(8,128)(2,1)S(1)}, bf16[2,256,256]{2,1,0:T(8,128)(2,1)S(1)}, u32[]{:S(2)}, u32[]{:S(2)}) collective-permute-start(bf16[2,256,256]{2,1,0:T(8,128)(2,1)S(1)} %collective-permute-done.2.refs_5_), channel_id=1, source_target_pairs={{8,0},{16,8},{24,16},{32,24},{40,32},{48,40},{56,48},{64,56},{72,6... | collective-permute-start | bytes 786440 | tf_op jit(solution)/shard_map/ppermute | solution.py:19
  34.3 9.4 %shard_map.123 = (f32[2,256,768]{2,1,0:T(8,128)}, bf16[2,256,768]{2,1,0:T(8,128)(2,1)}, f32[2,2,512,128]{3,2,1,0:T(8,128)}, f32[2,2,256,256]{3,2,1,0:T(8,128)}) custom-call(s32[12,2]{1,0:T(8,128)} %copy.13.pos.refs_0_, s32[1]{0:T(128)} %bitcast.9.cnt, bf16[2,256,1024]{2,1,0:T(8,128)(2,1)} %refs_3_.1, bf16[2,256,1024]{2,1,0:T(8,128)(2,1)} %copy-done.8, ...), custom_call_target="tpu_custom_call" | custom-call | flops 9663676416 | bytes 12582912 | tf_op jit(solution)/shard_map/pallas_call | solution.py:440
  44.4 6.7 %shard_map.124 = (f32[2,256,256]{2,1,0:T(8,128)}, bf16[2,256,512]{2,1,0:T(8,128)(2,1)}, bf16[2,256,256]{2,1,0:T(8,128)(2,1)}, f32[2,256,256]{2,1,0:T(8,128)}, bf16[2,256,256]{2,1,0:T(8,128)(2,1)}) custom-call(s32[12,2]{1,0:T(8,128)} %copy.13.pos.refs_0_, s32[1]{0:T(128)} %bitcast.10.refs_1_, s32[1]{0:T(128)} %bitcast.3.refs_2_, ...), custom_call_target="tpu_custom_call" | custom-call | flops 3221225472 | bytes 12582912 | tf_op jit(solution)/shard_map/pallas_call | solution.py:462
  51.2 5.1 %collective-permute-start.6 = (bf16[512,256]{1,0:T(8,128)(2,1)}, bf16[512,256]{1,0:T(8,128)(2,1)S(1)}, u32[]{:S(2)}, u32[]{:S(2)}) collective-permute-start(bf16[512,256]{1,0:T(8,128)(2,1)} %bitcast.14), channel_id=1, source_target_pairs={{0,8},{8,0},{16,24},{24,16},{32,40},{40,32},{48,56},{56,48},{64,72... | collective-permute-start | bytes 786440 | tf_op jit(solution)/shard_map/ppermute | solution.py:35
  56.3 1.4 %collective-permute-done.6 = bf16[512,256]{1,0:T(8,128)(2,1)S(1)} collective-permute-done((bf16[512,256]{1,0:T(8,128)(2,1)}, bf16[512,256]{1,0:T(8,128)(2,1)S(1)}, u32[]{:S(2)}, u32[]{:S(2)}) %collective-permute-start.6) | collective-permute-done | bytes 262176 | tf_op jit(solution)/shard_map/ppermute | solution.py:35
  57.7 1.2 bitcast_add_fusion
  58.9 1.2 collective-permute-start.7
  60.1 4.1 %collective-permute-start.8 = (bf16[128,256]{1,0:T(8,128)(2,1)S(1)}, bf16[128,256]{1,0:T(8,128)(2,1)S(1)}, u32[]{:S(2)}, u32[]{:S(2)}) collective-permute-start(bf16[128,256]{1,0:T(8,128)(2,1)S(1)} %get-tuple-element.36), channel_id=1, source_target_pairs={{0,128},{8,136},{16,144},{24,152},{32,160},{40,168},{48,176},{56,1... | collective-permute-start | bytes 196616 | tf_op jit(solution)/shard_map/ppermute | solution.py:35
  64.2 2.9 %collective-permute-done.8 = bf16[128,256]{1,0:T(8,128)(2,1)S(1)} collective-permute-done((bf16[128,256]{1,0:T(8,128)(2,1)S(1)}, bf16[128,256]{1,0:T(8,128)(2,1)S(1)}, u32[]{:S(2)}, u32[]{:S(2)}) %collective-permute-start.8) | collective-permute-done | bytes 65568 | tf_op jit(solution)/shard_map/ppermute | solution.py:35
  67.1 1.5 %collective-permute-done.9 = bf16[128,256]{1,0:T(8,128)(2,1)S(1)} collective-permute-done((bf16[128,256]{1,0:T(8,128)(2,1)S(1)}, bf16[128,256]{1,0:T(8,128)(2,1)S(1)}, u32[]{:S(2)}, u32[]{:S(2)}) %collective-permute-start.9) | collective-permute-done | bytes 65568 | tf_op jit(solution)/shard_map/ppermute | solution.py:35
  68.7 8.5 %collective-permute-start.10 = (bf16[128,256]{1,0:T(8,128)(2,1)S(1)}, bf16[128,256]{1,0:T(8,128)(2,1)S(1)}, u32[]{:S(2)}, u32[]{:S(2)}) collective-permute-start(bf16[128,256]{1,0:T(8,128)(2,1)S(1)} %add_convert_fusion.5), channel_id=1, source_target_pairs={{0,2},{1,3},{2,0},{3,1},{4,6},{5,7},{6,4},{7,5},{8,10},{9,11},{10,... | collective-permute-start | bytes 196616 | tf_op jit(solution)/shard_map/ppermute | solution.py:37
  77.2 1.3 collective-permute-start.12
  78.8 3.0 %collective-permute-done.11 = bf16[128,256]{1,0:T(8,128)(2,1)S(1)} collective-permute-done((bf16[128,256]{1,0:T(8,128)(2,1)S(1)}, bf16[128,256]{1,0:T(8,128)(2,1)S(1)}, u32[]{:S(2)}, u32[]{:S(2)}) %collective-permute-start.11) | collective-permute-done | bytes 65568 | tf_op jit(solution)/shard_map/ppermute | solution.py:37
  81.8 3.3 %collective-permute-start.13 = (bf16[128,256]{1,0:T(8,128)(2,1)S(1)}, bf16[128,256]{1,0:T(8,128)(2,1)S(1)}, u32[]{:S(2)}, u32[]{:S(2)}) collective-permute-start(bf16[128,256]{1,0:T(8,128)(2,1)S(1)} %add_convert_fusion.4), channel_id=1, source_target_pairs={{0,16},{8,24},{16,0},{24,8},{32,48},{40,56},{48,32},{56,40},{64,80... | collective-permute-start | bytes 196616 | tf_op jit(solution)/shard_map/ppermute | solution.py:35
  85.1 1.7 %collective-permute-done.13 = bf16[128,256]{1,0:T(8,128)(2,1)S(1)} collective-permute-done((bf16[128,256]{1,0:T(8,128)(2,1)S(1)}, bf16[128,256]{1,0:T(8,128)(2,1)S(1)}, u32[]{:S(2)}, u32[]{:S(2)}) %collective-permute-start.13) | collective-permute-done | bytes 65568 | tf_op jit(solution)/shard_map/ppermute | solution.py:35
  86.8 5.8 %collective-permute-start.14 = (bf16[128,256]{1,0:T(8,128)(2,1)S(1)}, bf16[128,256]{1,0:T(8,128)(2,1)S(1)}, u32[]{:S(2)}, u32[]{:S(2)}) collective-permute-start(bf16[128,256]{1,0:T(8,128)(2,1)S(1)} %add_convert_fusion.3), channel_id=1, source_target_pairs={{0,32},{8,40},{16,48},{24,56},{32,0},{40,8},{48,16},{56,24},{64,96... | collective-permute-start | bytes 196616 | tf_op jit(solution)/shard_map/ppermute | solution.py:35
  92.6 6.2 %collective-permute-start.4 = (bf16[2,256,512]{2,1,0:T(8,128)(2,1)S(1)}, bf16[2,256,512]{2,1,0:T(8,128)(2,1)S(1)}, u32[]{:S(2)}, u32[]{:S(2)}) collective-permute-start(bf16[2,256,512]{2,1,0:T(8,128)(2,1)S(1)} %copy-done.10), channel_id=1, source_target_pairs={{0,8},{8,16},{16,24},{24,32},{32,40},{40,48},{48,56},{56,64},{64,7... | collective-permute-start | bytes 1572872 | tf_op jit(solution)/shard_map/ppermute | solution.py:19
  99.0 5.1 %collective-permute-start.1 = (bf16[2,256,768]{2,1,0:T(8,128)(2,1)S(1)}, bf16[2,256,768]{2,1,0:T(8,128)(2,1)S(1)}, u32[]{:S(2)}, u32[]{:S(2)}) collective-permute-start(bf16[2,256,768]{2,1,0:T(8,128)(2,1)S(1)} %copy-done.9), channel_id=1, source_target_pairs={{0,8},{8,16},{16,24},{24,32},{32,40},{40,48},{48,56},{56,64},{64,7... | collective-permute-start | bytes 2359304 | tf_op jit(solution)/shard_map/ppermute | solution.py:19
  105.5 5.2 %collective-permute-start.5 = (bf16[2,256,256]{2,1,0:T(8,128)(2,1)S(1)}, bf16[2,256,256]{2,1,0:T(8,128)(2,1)S(1)}, u32[]{:S(2)}, u32[]{:S(2)}) collective-permute-start(bf16[2,256,256]{2,1,0:T(8,128)(2,1)S(1)} %get-tuple-element.37), channel_id=1, source_target_pairs={{0,1},{1,2},{2,3},{3,4},{4,5},{5,6},{6,7},{8,9},{9,10},{10,11},{11... | collective-permute-start | bytes 786440 | tf_op jit(solution)/shard_map/ppermute | solution.py:19
  110.7 2.2 %collective-permute-start.17 = (bf16[128,256]{1,0:T(8,128)(2,1)S(1)}, bf16[128,256]{1,0:T(8,128)(2,1)S(1)}, u32[]{:S(2)}, u32[]{:S(2)}) collective-permute-start(bf16[128,256]{1,0:T(8,128)(2,1)S(1)} %get-tuple-element.33), channel_id=1, source_target_pairs={{0,128},{8,136},{16,144},{24,152},{32,160},{40,168},{48,176},{56,1... | collective-permute-start | bytes 196616 | tf_op jit(solution)/shard_map/ppermute | solution.py:35
  112.9 1.4 %collective-permute-start.18 = (bf16[128,256]{1,0:T(8,128)(2,1)S(1)}, bf16[128,256]{1,0:T(8,128)(2,1)S(1)}, u32[]{:S(2)}, u32[]{:S(2)}) collective-permute-start(bf16[128,256]{1,0:T(8,128)(2,1)S(1)} %get-tuple-element.33), channel_id=1, source_target_pairs={{0,192},{8,200},{16,208},{24,216},{32,224},{40,232},{48,240},{56,2... | collective-permute-start | bytes 196616 | tf_op jit(solution)/shard_map/ppermute | solution.py:35
  114.3 1.1 collective-permute-done.17
  115.4 2.2 %collective-permute-done.18 = bf16[128,256]{1,0:T(8,128)(2,1)S(1)} collective-permute-done((bf16[128,256]{1,0:T(8,128)(2,1)S(1)}, bf16[128,256]{1,0:T(8,128)(2,1)S(1)}, u32[]{:S(2)}, u32[]{:S(2)}) %collective-permute-start.18) | collective-permute-done | bytes 65568 | tf_op jit(solution)/shard_map/ppermute | solution.py:35
  117.6 1.6 %collective-permute-start.19 = (bf16[512,256]{1,0:T(8,128)(2,1)S(1)}, bf16[512,256]{1,0:T(8,128)(2,1)S(1)}, u32[]{:S(2)}, u32[]{:S(2)}) collective-permute-start(bf16[512,256]{1,0:T(8,128)(2,1)S(1)} %constant_dynamic-update-slice_fusion.2), channel_id=1, source_target_pairs={{0,8},{8,0},{16,24},{24,16},{32,40},{40,32},{48,56},{56,48},{64,72... | collective-permute-start | bytes 786440 | tf_op jit(solution)/shard_map/ppermute | solution.py:35
  119.9 13.0 %collective-permute-done.5 = bf16[2,256,256]{2,1,0:T(8,128)(2,1)S(1)} collective-permute-done((bf16[2,256,256]{2,1,0:T(8,128)(2,1)S(1)}, bf16[2,256,256]{2,1,0:T(8,128)(2,1)S(1)}, u32[]{:S(2)}, u32[]{:S(2)}) %collective-permute-start.5) | collective-permute-done | bytes 262176 | tf_op jit(solution)/shard_map/ppermute | solution.py:19
  132.9 1.2 convert.1
  (58 shorter events, 7.5 us)
Async XLA Ops:
  0.6 32.7 %collective-permute-start = (bf16[2,256,1024]{2,1,0:T(8,128)(2,1)}, bf16[2,256,1024]{2,1,0:T(8,128)(2,1)S(1)}, u32[]{:S(2)}, u32[]{:S(2)}) collective-permute-start(bf16[2,256,1024]{2,1,0:T(8,128)(2,1)} %refs_3_.1), channel_id=1, source_target_pairs={{8,0},{16,8},{24,16},{32,24},{40,32},{48,40},{56,48},{64,56},{72,6... | collective-permute-start | bytes 3145736 | tf_op jit(solution)/shard_map/ppermute | solution.py:19
  4.2 18.3 %collective-permute-start.2 = (bf16[2,256,256]{2,1,0:T(8,128)(2,1)S(1)}, bf16[2,256,256]{2,1,0:T(8,128)(2,1)S(1)}, u32[]{:S(2)}, u32[]{:S(2)}) collective-permute-start(bf16[2,256,256]{2,1,0:T(8,128)(2,1)S(1)} %slice.34), channel_id=1, source_target_pairs={{1,0},{2,1},{3,2},{4,3},{5,4},{6,5},{7,6},{9,8},{10,9},{11,10},{12... | collective-permute-start | bytes 786440 | tf_op jit(solution)/shard_map/ppermute | solution.py:19
  14.1 1.4 %copy-start = (bf16[1,1,12,256,256]{4,3,2,1,0:T(8,128)(2,1)S(1)}, bf16[1,1,12,256,256]{4,3,2,1,0:T(8,128)(2,1)}, u32[]{:S(2)}) copy-start(bf16[1,1,12,256,256]{4,3,2,1,0:T(8,128)(2,1)} %param.15) | copy-start | bytes 4718596
  15.5 0.9 copy-start.2
  16.4 0.9 copy-start.3
  21.4 1.1 copy-start.1
  22.5 21.2 %copy-start.11 = (bf16[2,256,256]{2,1,0:T(8,128)(2,1)}, bf16[2,256,256]{2,1,0:T(8,128)(2,1)S(1)}, u32[]{:S(2)}) copy-start(bf16[2,256,256]{2,1,0:T(8,128)(2,1)S(1)} %collective-permute-done.2.refs_5_) | copy-start | bytes 786436
  22.5 21.2 %collective-permute-start.3 = (bf16[2,256,256]{2,1,0:T(8,128)(2,1)S(1)}, bf16[2,256,256]{2,1,0:T(8,128)(2,1)S(1)}, u32[]{:S(2)}, u32[]{:S(2)}) collective-permute-start(bf16[2,256,256]{2,1,0:T(8,128)(2,1)S(1)} %collective-permute-done.2.refs_5_), channel_id=1, source_target_pairs={{8,0},{16,8},{24,16},{32,24},{40,32},{48,40},{56,48},{64,56},{72,6... | collective-permute-start | bytes 786440 | tf_op jit(solution)/shard_map/ppermute | solution.py:19
  33.4 1.0 copy-start.8
  51.2 41.5 %copy-start.10 = (bf16[2,256,512]{2,1,0:T(8,128)(2,1)S(1)}, bf16[2,256,512]{2,1,0:T(8,128)(2,1)}, u32[]{:S(2)}) copy-start(bf16[2,256,512]{2,1,0:T(8,128)(2,1)} %get-tuple-element.28) | copy-start | bytes 1572868
  51.2 47.8 %copy-start.9 = (bf16[2,256,768]{2,1,0:T(8,128)(2,1)S(1)}, bf16[2,256,768]{2,1,0:T(8,128)(2,1)}, u32[]{:S(2)}) copy-start(bf16[2,256,768]{2,1,0:T(8,128)(2,1)} %get-tuple-element.24) | copy-start | bytes 2359300
  51.2 6.5 %collective-permute-start.6 = (bf16[512,256]{1,0:T(8,128)(2,1)}, bf16[512,256]{1,0:T(8,128)(2,1)S(1)}, u32[]{:S(2)}, u32[]{:S(2)}) collective-permute-start(bf16[512,256]{1,0:T(8,128)(2,1)} %bitcast.14), channel_id=1, source_target_pairs={{0,8},{8,0},{16,24},{24,16},{32,40},{40,32},{48,56},{56,48},{64,72... | collective-permute-start | bytes 786440 | tf_op jit(solution)/shard_map/ppermute | solution.py:35
  57.7 47.7 %copy-start.6 = (f32[2,256,256]{2,1,0:T(8,128)S(1)}, f32[2,256,256]{2,1,0:T(8,128)}, u32[]{:S(2)}) copy-start(f32[2,256,256]{2,1,0:T(8,128)} %get-tuple-element.27) | copy-start | bytes 1572868
  57.7 47.7 %copy-start.7 = (bf16[2,256,256]{2,1,0:T(8,128)(2,1)S(1)}, bf16[2,256,256]{2,1,0:T(8,128)(2,1)}, u32[]{:S(2)}) copy-start(bf16[2,256,256]{2,1,0:T(8,128)(2,1)} %get-tuple-element.29) | copy-start | bytes 786436
  58.9 5.3 %collective-permute-start.7 = (bf16[128,256]{1,0:T(8,128)(2,1)S(1)}, bf16[128,256]{1,0:T(8,128)(2,1)S(1)}, u32[]{:S(2)}, u32[]{:S(2)}) collective-permute-start(bf16[128,256]{1,0:T(8,128)(2,1)S(1)} %get-tuple-element.34), channel_id=1, source_target_pairs={{0,64},{8,72},{16,80},{24,88},{32,96},{40,104},{48,112},{56,120},{... | collective-permute-start | bytes 196616 | tf_op jit(solution)/shard_map/ppermute | solution.py:35
  60.1 7.0 %collective-permute-start.8 = (bf16[128,256]{1,0:T(8,128)(2,1)S(1)}, bf16[128,256]{1,0:T(8,128)(2,1)S(1)}, u32[]{:S(2)}, u32[]{:S(2)}) collective-permute-start(bf16[128,256]{1,0:T(8,128)(2,1)S(1)} %get-tuple-element.36), channel_id=1, source_target_pairs={{0,128},{8,136},{16,144},{24,152},{32,160},{40,168},{48,176},{56,1... | collective-permute-start | bytes 196616 | tf_op jit(solution)/shard_map/ppermute | solution.py:35
  64.2 4.5 %collective-permute-start.9 = (bf16[128,256]{1,0:T(8,128)(2,1)S(1)}, bf16[128,256]{1,0:T(8,128)(2,1)S(1)}, u32[]{:S(2)}, u32[]{:S(2)}) collective-permute-start(bf16[128,256]{1,0:T(8,128)(2,1)S(1)} %get-tuple-element.35), channel_id=1, source_target_pairs={{0,192},{8,200},{16,208},{24,216},{32,224},{40,232},{48,240},{56,2... | collective-permute-start | bytes 196616 | tf_op jit(solution)/shard_map/ppermute | solution.py:35
  68.7 10.1 %collective-permute-start.10 = (bf16[128,256]{1,0:T(8,128)(2,1)S(1)}, bf16[128,256]{1,0:T(8,128)(2,1)S(1)}, u32[]{:S(2)}, u32[]{:S(2)}) collective-permute-start(bf16[128,256]{1,0:T(8,128)(2,1)S(1)} %add_convert_fusion.5), channel_id=1, source_target_pairs={{0,2},{1,3},{2,0},{3,1},{4,6},{5,7},{6,4},{7,5},{8,10},{9,11},{10,... | collective-permute-start | bytes 196616 | tf_op jit(solution)/shard_map/ppermute | solution.py:37
  77.2 4.6 %collective-permute-start.11 = (bf16[128,256]{1,0:T(8,128)(2,1)S(1)}, bf16[128,256]{1,0:T(8,128)(2,1)S(1)}, u32[]{:S(2)}, u32[]{:S(2)}) collective-permute-start(bf16[128,256]{1,0:T(8,128)(2,1)S(1)} %add_convert_fusion.5), channel_id=1, source_target_pairs={{0,4},{1,5},{2,6},{3,7},{4,0},{5,1},{6,2},{7,3},{8,12},{9,13},{10,... | collective-permute-start | bytes 196616 | tf_op jit(solution)/shard_map/ppermute | solution.py:37
  77.2 4.6 %collective-permute-start.12 = (bf16[128,256]{1,0:T(8,128)(2,1)S(1)}, bf16[128,256]{1,0:T(8,128)(2,1)S(1)}, u32[]{:S(2)}, u32[]{:S(2)}) collective-permute-start(bf16[128,256]{1,0:T(8,128)(2,1)S(1)} %add_convert_fusion.5), channel_id=1, source_target_pairs={{0,6},{1,7},{2,4},{3,5},{4,2},{5,3},{6,0},{7,1},{8,14},{9,15},{10,... | collective-permute-start | bytes 196616 | tf_op jit(solution)/shard_map/ppermute | solution.py:37
  81.8 5.0 %collective-permute-start.13 = (bf16[128,256]{1,0:T(8,128)(2,1)S(1)}, bf16[128,256]{1,0:T(8,128)(2,1)S(1)}, u32[]{:S(2)}, u32[]{:S(2)}) collective-permute-start(bf16[128,256]{1,0:T(8,128)(2,1)S(1)} %add_convert_fusion.4), channel_id=1, source_target_pairs={{0,16},{8,24},{16,0},{24,8},{32,48},{40,56},{48,32},{56,40},{64,80... | collective-permute-start | bytes 196616 | tf_op jit(solution)/shard_map/ppermute | solution.py:35
  86.8 12.0 %collective-permute-start.14 = (bf16[128,256]{1,0:T(8,128)(2,1)S(1)}, bf16[128,256]{1,0:T(8,128)(2,1)S(1)}, u32[]{:S(2)}, u32[]{:S(2)}) collective-permute-start(bf16[128,256]{1,0:T(8,128)(2,1)S(1)} %add_convert_fusion.3), channel_id=1, source_target_pairs={{0,32},{8,40},{16,48},{24,56},{32,0},{40,8},{48,16},{56,24},{64,96... | collective-permute-start | bytes 196616 | tf_op jit(solution)/shard_map/ppermute | solution.py:35
  92.6 12.7 %collective-permute-start.4 = (bf16[2,256,512]{2,1,0:T(8,128)(2,1)S(1)}, bf16[2,256,512]{2,1,0:T(8,128)(2,1)S(1)}, u32[]{:S(2)}, u32[]{:S(2)}) collective-permute-start(bf16[2,256,512]{2,1,0:T(8,128)(2,1)S(1)} %copy-done.10), channel_id=1, source_target_pairs={{0,8},{8,16},{16,24},{24,32},{32,40},{40,48},{48,56},{56,64},{64,7... | collective-permute-start | bytes 1572872 | tf_op jit(solution)/shard_map/ppermute | solution.py:19
  98.9 5.7 %collective-permute-start.15 = (bf16[128,256]{1,0:T(8,128)(2,1)S(1)}, bf16[128,256]{1,0:T(8,128)(2,1)S(1)}, u32[]{:S(2)}, u32[]{:S(2)}) collective-permute-start(bf16[128,256]{1,0:T(8,128)(2,1)S(1)} %add_convert_fusion.2), channel_id=1, source_target_pairs={{0,33},{1,32},{2,35},{3,34},{4,37},{5,36},{6,39},{7,38},{8,41},{9,... | collective-permute-start | bytes 196616 | tf_op jit(solution)/shard_map/ppermute | solution.py:40
  99.0 20.3 %collective-permute-start.1 = (bf16[2,256,768]{2,1,0:T(8,128)(2,1)S(1)}, bf16[2,256,768]{2,1,0:T(8,128)(2,1)S(1)}, u32[]{:S(2)}, u32[]{:S(2)}) collective-permute-start(bf16[2,256,768]{2,1,0:T(8,128)(2,1)S(1)} %copy-done.9), channel_id=1, source_target_pairs={{0,8},{8,16},{16,24},{24,32},{32,40},{40,48},{48,56},{56,64},{64,7... | collective-permute-start | bytes 2359304 | tf_op jit(solution)/shard_map/ppermute | solution.py:19
  104.7 9.7 %collective-permute-start.16 = (bf16[128,256]{1,0:T(8,128)(2,1)S(1)}, bf16[128,256]{1,0:T(8,128)(2,1)S(1)}, u32[]{:S(2)}, u32[]{:S(2)}) collective-permute-start(bf16[128,256]{1,0:T(8,128)(2,1)S(1)} %get-tuple-element.33), channel_id=1, source_target_pairs={{0,64},{8,72},{16,80},{24,88},{32,96},{40,104},{48,112},{56,120},{... | collective-permute-start | bytes 196616 | tf_op jit(solution)/shard_map/ppermute | solution.py:35
  105.4 14.0 %copy-start.5 = (f32[2,256,768]{2,1,0:T(8,128)S(1)}, f32[2,256,768]{2,1,0:T(8,128)}, u32[]{:S(2)}) copy-start(f32[2,256,768]{2,1,0:T(8,128)} %get-tuple-element.23) | copy-start | bytes 4718596
  105.5 27.3 %collective-permute-start.5 = (bf16[2,256,256]{2,1,0:T(8,128)(2,1)S(1)}, bf16[2,256,256]{2,1,0:T(8,128)(2,1)S(1)}, u32[]{:S(2)}, u32[]{:S(2)}) collective-permute-start(bf16[2,256,256]{2,1,0:T(8,128)(2,1)S(1)} %get-tuple-element.37), channel_id=1, source_target_pairs={{0,1},{1,2},{2,3},{3,4},{4,5},{5,6},{6,7},{8,9},{9,10},{10,11},{11... | collective-permute-start | bytes 786440 | tf_op jit(solution)/shard_map/ppermute | solution.py:19
  110.7 4.7 %collective-permute-start.17 = (bf16[128,256]{1,0:T(8,128)(2,1)S(1)}, bf16[128,256]{1,0:T(8,128)(2,1)S(1)}, u32[]{:S(2)}, u32[]{:S(2)}) collective-permute-start(bf16[128,256]{1,0:T(8,128)(2,1)S(1)} %get-tuple-element.33), channel_id=1, source_target_pairs={{0,128},{8,136},{16,144},{24,152},{32,160},{40,168},{48,176},{56,1... | collective-permute-start | bytes 196616 | tf_op jit(solution)/shard_map/ppermute | solution.py:35
  112.9 4.7 %collective-permute-start.18 = (bf16[128,256]{1,0:T(8,128)(2,1)S(1)}, bf16[128,256]{1,0:T(8,128)(2,1)S(1)}, u32[]{:S(2)}, u32[]{:S(2)}) collective-permute-start(bf16[128,256]{1,0:T(8,128)(2,1)S(1)} %get-tuple-element.33), channel_id=1, source_target_pairs={{0,192},{8,200},{16,208},{24,216},{32,224},{40,232},{48,240},{56,2... | collective-permute-start | bytes 196616 | tf_op jit(solution)/shard_map/ppermute | solution.py:35
  117.6 15.3 %collective-permute-start.19 = (bf16[512,256]{1,0:T(8,128)(2,1)S(1)}, bf16[512,256]{1,0:T(8,128)(2,1)S(1)}, u32[]{:S(2)}, u32[]{:S(2)}) collective-permute-start(bf16[512,256]{1,0:T(8,128)(2,1)S(1)} %constant_dynamic-update-slice_fusion.2), channel_id=1, source_target_pairs={{0,8},{8,0},{16,24},{24,16},{32,40},{40,32},{48,56},{56,48},{64,72... | collective-permute-start | bytes 786440 | tf_op jit(solution)/shard_map/ppermute | solution.py:35
  132.9 1.7 %copy-start.4 = (f32[2,256,1024]{2,1,0:T(8,128)}, f32[2,256,1024]{2,1,0:T(8,128)S(1)}, u32[]{:S(2)}) copy-start(f32[2,256,1024]{2,1,0:T(8,128)S(1)} %fusion) | copy-start | bytes 6291460
  (1 other events, 0.7 us)

commit v2 on v1

--- a/solution.py
+++ b/solution.py
@@ -19,24 +19,26 @@
     return lax.ppermute(x, axis, pairs)
 
 
+Y = [(8, 0), (16, 0), (24, 0)]
+X = [(0, 2), (0, 4), (0, 6)]
 FIELDS = {
-    "core": ([(1, 0)], 0),
-    "y": ([(8, 0), (16, 0), (24, 0)], 3),
-    "x": ([(0, 2), (0, 4), (0, 6)], None),
-    "z0": ([(2, 0)], None),
-    "z1": ([(4, 0)], None),
-    "z2": ([(4, 1)], None),
+    "core": ([(1, 0)], [(1, 0)]),
+    "first": (Y, X),
+    "second": (X, Y),
+    "z0": ([(2, 0)], [(2, 0)]),
+    "z1": ([(4, 0)], [(4, 0)]),
+    "z2": ([(4, 1)], [(4, 1)]),
 }
 
 
 def partner(v, field, d):
-    row, col = FIELDS[field][0][d - 1]
-    if not col:
-        return lax.ppermute(v, "row", [(i, i ^ row) for i in range(lax.axis_size("row"))])
-    if not row:
-        return lax.ppermute(v, "col", [(i, i ^ col) for i in range(lax.axis_size("col"))])
+    masks = [masks[d - 1] for masks in FIELDS[field]]
     rows, cols = lax.axis_size("row"), lax.axis_size("col")
-    pairs = [(r * cols + c, (r ^ row) * cols + (c ^ col)) for r in range(rows) for c in range(cols)]
+    pairs = []
+    for r in range(rows):
+        for c in range(cols):
+            row, col = masks[r & 1]
+            pairs.append((r * cols + c, (r ^ row) * cols + (c ^ col)))
     return lax.ppermute(v, ("row", "col"), pairs)
 
 
@@ -45,7 +47,9 @@
 
 
 def place(field):
-    return (lax.axis_index("row") >> FIELDS[field][1]) & (members(field) - 1)
+    if field == "core":
+        return lax.axis_index("row") & 1
+    return jnp.where(lax.axis_index("row") & 1 == 0, lax.axis_index("row") >> 3, lax.axis_index("col") >> 1)
 
 
 def scatter_sum(v, field, dtype):
@@ -85,12 +89,12 @@
 
 
 PLAN = (
-    (scatter_sum, "y", bf16),
-    (full_sum, "x", bf16),
+    (scatter_sum, "first", bf16),
     (full_sum, "z0", bf16),
     (full_sum, "z1", bf16),
     (full_sum, "z2", bf16),
-    (gather, "y", bf16),
+    (full_sum, "second", bf16),
+    (gather, "first", bf16),
     (gather, "core", bf16),
 )
 
@@ -143,26 +147,39 @@
     lax.fori_loop(0, frames.shape[0], one, 0)
 
 
+def choose(pos, cnt, wanted, todo, frames_hbm, frames, sem):
+    todo[0] = 0
+
+    def pick(s, k):
+        take = wanted(pos[s, 1])
+
+        @pl.when(take)
+        def _():
+            todo[k] = s
+            pltpu.make_async_copy(frames_hbm.at[s], frames.at[s], sem.at[s]).start()
+
+        return k + take.astype(jnp.int32)
+
+    return lax.fori_loop(0, cnt[0], pick, 0)
+
+
+def await_frames(count, todo, frames_hbm, frames, sem):
+    def one(k, _):
+        s = todo[k]
+        pltpu.make_async_copy(frames_hbm.at[s], frames.at[s], sem.at[s]).wait()
+        return 0
+
+    lax.fori_loop(0, count, one, 0)
+
+
 def positions_pass(
-    pos, cnt, wanted, base, blocks, clear, probe, frames, tables, p_out,
-    ext, gext, xs, hs, sp, ws, ib, hb, eb, todo,
+    pos, count, base, blocks, clear, probe, frames, tables, p_out,
+    ext, gext, pat, xs, hs, sp, ws, ib, hb, eb, todo,
 ):
     left, right, gl, gr = tables
     n = probe.shape[-1]
     h = n // 2
     ch = 16
-    todo[0] = 0
-
-    def pick(s, k):
-        take = wanted(pos[s, 1])
-
-        @pl.when(take)
-        def _():
-            todo[k] = s
-
-        return k + take.astype(jnp.int32)
-
-    count = lax.fori_loop(0, cnt[0], pick, 0)
     last = jnp.maximum(count - 1, 0)
 
     def window(t):
@@ -180,8 +197,10 @@
             out.append(pltpu.roll(w, unshift, 1)[:, :n])
         return out
 
-    def wave_rows(win, i):
+    def wave_rows(win, slot, i):
         o = patch_rows(win, i)
+        for p in range(2):
+            pat[slot, p, i : i + ch, :] = o[p]
         for m in range(2):
             pr = probe[m, 0, i : i + ch, :]
             pi = probe[m, 1, i : i + ch, :]
@@ -195,20 +214,19 @@
     def forward_right(m, q):
         sp[m, q] = jnp.dot(hs[m], right[:, q * n : (q + 1) * n], preferred_element_type=f32)
 
-    def weigh_rows(win, i):
+    def weigh_rows(win, q, i):
         s = win[0]
         rows = i % h
         par = i // h
-        for q in range(2):
-            v = [sp[m, q, i : i + ch, :] for m in range(2)]
-            e = v[0] * v[0] + v[1] * v[1]
-            inten = e[:, :h] + e[:, h:] + 1.0
-            f = 1.0 - frames[s, i : i + ch, q * h : (q + 1) * h].astype(f32) * lax.rsqrt(inten)
-            for m in range(2):
-                for part in range(2):
-                    ws[m, par, part * h + rows : part * h + rows + ch, q * h : (q + 1) * h] = (
-                        v[m][:, part * h : (part + 1) * h] * f
-                    ).astype(bf16)
+        v = [sp[m, q, i : i + ch, :] for m in range(2)]
+        e = v[0] * v[0] + v[1] * v[1]
+        inten = e[:, :h] + e[:, h:] + 1.0
+        f = 1.0 - frames[s, i : i + ch, q * h : (q + 1) * h].astype(f32) * lax.rsqrt(inten)
+        for m in range(2):
+            for part in range(2):
+                ws[m, par, part * h + rows : part * h + rows + ch, q * h : (q + 1) * h] = (
+                    v[m][:, part * h : (part + 1) * h] * f
+                ).astype(bf16)
 
     def inverse_left(m, par):
         ib[m, par] = jnp.dot(gl[par], ws[m, par], preferred_element_type=f32)
@@ -225,13 +243,14 @@
     def inverse_right(m, q):
         eb[m, q] = jnp.dot(hb[m, q], gr[q], preferred_element_type=f32)
 
-    def add_rows(win, i0):
-      for i in range(i0, i0 + ch, 8):
-        add_some(win, i)
-
-    def add_some(win, i):
+    def add_rows(win, slot, i0):
+        for i in range(i0, i0 + ch, 8):
+            add_some(win, slot, i)
+
+    def add_some(win, slot, i):
         _, r, cb, sh, _ = win
-        ore, oim = patch_rows(win, i, 8)
+        ore = pat[slot, 0, i : i + 8, :]
+        oim = pat[slot, 1, i : i + 8, :]
         acc = None
         for m in range(2):
             e = eb[m, 0, i : i + 8, :]
@@ -263,10 +282,12 @@
     def step(t, _):
         now = window(t)
         old = window(t - 1)
+        new_slot = lax.rem(t, 2)
+        old_slot = 1 - new_slot
         for k, (m, par) in enumerate(pairs):
             inverse_left(m, par)
             for i in chunks[2 * k : 2 * k + 2]:
-                wave_rows(now, i)
+                wave_rows(now, new_slot, i)
         for m in range(2):
             for part in range(2):
                 for i in range(0, h, ch):
@@ -274,17 +295,21 @@
         for k, (m, q) in enumerate(pairs):
             inverse_right(m, q)
             for i in chunks[8 + 2 * k : 8 + 2 * k + 2]:
-                wave_rows(now, i)
+                wave_rows(now, new_slot, i)
         for k, (m, part) in enumerate(pairs):
             forward_left(m, part)
-            for i in chunks[2 * k : 2 * k + 2]:
-                add_rows(old, i)
-        for k, (m, q) in enumerate(pairs):
-            forward_right(m, q)
-            for i in chunks[8 + 2 * k : 8 + 2 * k + 2]:
-                add_rows(old, i)
+            for i in chunks[3 * k : 3 * k + 3]:
+                add_rows(old, old_slot, i)
+        for m in range(2):
+            forward_right(m, 0)
+            for i in chunks[12 + 2 * m : 12 + 2 * m + 2]:
+                add_rows(old, old_slot, i)
+        for m in range(2):
+            forward_right(m, 1)
+            for i in chunks[8 * m : 8 * m + 8]:
+                weigh_rows(now, 0, i)
         for i in chunks:
-            weigh_rows(now, i)
+            weigh_rows(now, 1, i)
 
         @pl.when(t == 0)
         def _():
@@ -322,29 +347,32 @@
 def inner_kernel(
     pos, cnt, own_hbm, below_hbm, probe_hbm, frames_hbm, left_hbm, right_hbm, gl_hbm, gr_hbm,
     g_own, g_below, carry, p_out,
-    own, below, probe, frames, left, right, gl, gr, sems, ext, gext, *scratch,
+    own, below, probe, frames, left, right, gl, gr, sems, frame_sems, ext, gext, *scratch,
 ):
     copies = fetch(
-        (own_hbm, below_hbm, probe_hbm, left_hbm, right_hbm, gl_hbm, gr_hbm, frames_hbm),
-        (own, below, probe, left, right, gl, gr, frames),
+        (own_hbm, below_hbm, probe_hbm, left_hbm, right_hbm, gl_hbm, gr_hbm),
+        (own, below, probe, left, right, gl, gr),
         sems,
     )
     n = probe.shape[-1]
     tr, tc = own.shape[1:]
     inner = tc - n
+    todo = scratch[-1]
+    count = choose(pos, cnt, lambda c: c < inner, todo, frames_hbm, frames, frame_sems)
     copies[0].wait()
     fill(ext, ((own, 0, tc, 0, 0),))
     copies[1].wait()
     fill(ext, ((below, 0, tc, tr, 0),))
     for copy in copies[2:]:
         copy.wait()
+    await_frames(count, todo, frames_hbm, frames, frame_sems)
 
     def clear():
         gext[...] = jnp.zeros_like(gext)
         p_out[...] = jnp.zeros_like(p_out)
 
     positions_pass(
-        pos, cnt, lambda c: c < inner, 0, tc // 128, clear, probe, frames, (left, right, gl, gr), p_out,
+        pos, count, 0, tc // 128, clear, probe, frames, (left, right, gl, gr), p_out,
         ext, gext, *scratch,
     )
     drain(gext, ((g_own, 0, inner, 0, 0), (g_below, 0, inner, tr, 0)))
@@ -357,7 +385,7 @@
     scale, pos, cnt, core, own_hbm, below_hbm, strip_hbm, corner_hbm, carry_hbm, p_hbm, probe_hbm, frames_hbm,
     left_hbm, right_hbm, gl_hbm, gr_hbm,
     g_own, g_rows, g_strip, p_keep, p_send,
-    own, below, strip, corner, carry, p_in, probe, frames, left, right, gl, gr, sems, p_out, ext, gext, *scratch,
+    own, below, strip, corner, carry, p_in, probe, frames, left, right, gl, gr, sems, frame_sems, p_out, ext, gext, *scratch,
 ):
     n = probe.shape[-1]
     tr, tc = own_hbm.shape[1:]
@@ -365,19 +393,22 @@
     copies = fetch(
         (
             own_hbm.at[:, :, inner:tc], below_hbm.at[:, :, inner:tc], strip_hbm, corner_hbm, probe_hbm,
-            left_hbm, right_hbm, gl_hbm, gr_hbm, frames_hbm, p_hbm, carry_hbm,
+            left_hbm, right_hbm, gl_hbm, gr_hbm, p_hbm, carry_hbm,
         ),
-        (own, below, strip, corner, probe, left, right, gl, gr, frames, p_in, carry),
+        (own, below, strip, corner, probe, left, right, gl, gr, p_in, carry),
         sems,
     )
+    todo = scratch[-1]
+    count = choose(pos, cnt, lambda c: c >= inner, todo, frames_hbm, frames, frame_sems)
     for copy in copies[:4]:
         copy.wait()
     fill(ext, ((own, 0, n, 0, 0), (below, 0, n, tr, 0), (strip, 0, n, 0, n), (corner, 0, n, tr, n)))
-    for copy in copies[4:10]:
+    for copy in copies[4:9]:
         copy.wait()
+    await_frames(count, todo, frames_hbm, frames, frame_sems)
 
     def clear():
-        for copy in copies[10:]:
+        for copy in copies[9:]:
             copy.wait()
         p_out[...] = p_in[...]
         for p in range(2):
@@ -386,7 +417,7 @@
                 gext[p, n // 128 + b] = jnp.zeros_like(gext[p, b])
 
     positions_pass(
-        pos, cnt, lambda c: c >= inner, inner // 128, 2 * n // 128, clear, probe, frames,
+        pos, count, inner // 128, 2 * n // 128, clear, probe, frames,
         (left, right, gl, gr), p_out, ext, gext, *scratch,
     )
     p_keep[...] = p_out[core[0]] * scale
@@ -425,6 +456,7 @@
         return [
             pltpu.VMEM((2, blocks, rows, 128), f32),
             pltpu.VMEM((2, blocks, rows, 128), f32),
+            pltpu.VMEM((2, 2, size, size), f32),
             pltpu.VMEM((2, 2 * size, size), bf16),
             pltpu.VMEM((2, size, 2 * size), bf16),
             pltpu.VMEM((2, 2, size, size), f32),
@@ -436,7 +468,9 @@
         ]
 
     fixed = [pltpu.VMEM(x.shape, x.dtype) for x in (probe, frames, left, right, gl, gr)]
-    params = pltpu.CompilerParams(vmem_limit_bytes=60 * 2**20)
+    params = pltpu.CompilerParams(
+        vmem_limit_bytes=60 * 2**20
+    )
     g_main, g_band, carry, p_part = pl.pallas_call(
         inner_kernel,
         out_shape=(
@@ -452,7 +486,7 @@
             pltpu.VMEM((2, size, tile_cols), bf16),
         ]
         + fixed
-        + [pltpu.SemaphoreType.DMA((8,))]
+        + [pltpu.SemaphoreType.DMA((7,)), pltpu.SemaphoreType.DMA((slots,))]
         + scratch(tile_cols // 128),
         compiler_params=params,
         cost_estimate=pl.CostEstimate(flops=9 * 2**30, bytes_accessed=12 * 2**20, transcendentals=0),
@@ -479,7 +513,7 @@
             pltpu.VMEM(probe.shape, f32),
         ]
         + fixed
-        + [pltpu.SemaphoreType.DMA((12,)), pltpu.VMEM(probe.shape, f32)]
+        + [pltpu.SemaphoreType.DMA((11,)), pltpu.SemaphoreType.DMA((slots,)), pltpu.VMEM(probe.shape, f32)]
         + scratch(2 * size // 128),
         compiler_params=params,
         cost_estimate=pl.CostEstimate(flops=3 * 2**30, bytes_accessed=12 * 2**20, transcendentals=0),

time: 135 us -> 133 us (0.985)
  starting transfers between devices: 73.2 us -> 71.8 us
    ppermute x13 -> x0, starting transfers between devices: 35.3 us -> none  [the longest x10 25.5 us: partner(): lax.ppermute(v, 'row', [(i, i ^ row) for i in range(lax.axis_size('row'))])]
    ppermute x1 -> x14, starting transfers between devices: 0.09 us -> 27.9 us  [partner(): return lax.ppermute(v, ('row', 'col'), pairs)]
    ppermute x1 -> x14, waiting for transfers between devices: 0.44 us -> 15.2 us  [partner(): return lax.ppermute(v, ('row', 'col'), pairs)]
    ppermute x13 -> x0, waiting for transfers between devices: 14.1 us -> none  [the longest x10 10.8 us: partner(): lax.ppermute(v, 'row', [(i, i ^ row) for i in range(lax.axis_size('row'))])]
    ppermute x6, starting transfers between devices: 37.8 us -> 43.9 us  [shifted(): return lax.ppermute(x, axis, pairs)]
  transfers between devices with their start and end apart: 20 -> 20, of which waited for: 10 -> 8; matrix products, arithmetic and copies ran while one was open for 2% -> 2% of each run, Pallas kernels for 10% -> 10%
where the time goes in v2:
time: 133 us; the launch traced here: 132 us
  starting transfers between devices  71.8 us (54%)
  waiting for transfers between devices  27.9 us (21%)
  Pallas kernels  19 us (14%)
  local copies, waits for them, and re-layouts  8.98 us (7%)
  other arithmetic  3.12 us (2%)
  between operations  1.67 us (1%)
    ppermute x6, starting transfers between devices, shifted(): return lax.ppermute(x, axis, pairs)  43.9 us
    ppermute x14, starting transfers between devices, partner(): return lax.ppermute(v, ('row', 'col'), pairs)  27.9 us
    ppermute x14, waiting for transfers between devices, partner(): return lax.ppermute(v, ('row', 'col'), pairs)  15.2 us
    ppermute x6, waiting for transfers between devices, shifted(): return lax.ppermute(x, axis, pairs)  12.7 us
    pallas_call x1, Pallas kernels, body(): pl.pallas_call(inner_kernel, out_shape=(jax.ShapeDtypeStruct((2, tile_row...  8.77 us
    unnamed x26, local copies, waits for them, and re-layouts  6.48 us
    pallas_call x1, Pallas kernels, body(): pl.pallas_call(lambda *refs: edge_kernel(scale, *refs), out_shape=(jax.Sh...  6.17 us
    pallas_call x1, Pallas kernels, body(): pl.pallas_call(prep_kernel, out_shape=jax.ShapeDtypeStruct(measured.shape...  4.03 us
  transfers between devices with their start and end apart: 20, of which 8 were waited for; matrix products, arithmetic and copies ran while one was open for 2% of the time, Pallas kernels for 10%

profile of v2, /device:TPU:35, one launch (start us, length us, event | category | flops | bytes accessed | tf_op | source)
XLA Modules:
  0.0 132.5 jit_solution(4736757265901093169)
XLA Ops:
  0.6 2.6 %collective-permute-start = (bf16[2,256,1024]{2,1,0:T(8,128)(2,1)}, bf16[2,256,1024]{2,1,0:T(8,128)(2,1)S(1)}, u32[]{:S(2)}, u32[]{:S(2)}) collective-permute-start(bf16[2,256,1024]{2,1,0:T(8,128)(2,1)} %refs_3_.1), channel_id=1, source_target_pairs={{8,0},{16,8},{24,16},{32,24},{40,32},{48,40},{56,48},{64,56},{72,6... | collective-permute-start | bytes 3145736 | tf_op jit(solution)/shard_map/ppermute | solution.py:19
  3.2 1.0 slice.34
  4.2 7.9 %collective-permute-start.2 = (bf16[2,256,256]{2,1,0:T(8,128)(2,1)S(1)}, bf16[2,256,256]{2,1,0:T(8,128)(2,1)S(1)}, u32[]{:S(2)}, u32[]{:S(2)}) collective-permute-start(bf16[2,256,256]{2,1,0:T(8,128)(2,1)S(1)} %slice.34), channel_id=1, source_target_pairs={{1,0},{2,1},{3,2},{4,3},{5,4},{6,5},{7,6},{9,8},{10,9},{11,10},{12... | collective-permute-start | bytes 786440 | tf_op jit(solution)/shard_map/ppermute | solution.py:19
  12.1 1.4 %copy.13.pos.refs_0_ = s32[12,2]{1,0:T(8,128)} copy(s32[12,2]{0,1:T(2,128)} %bitcast.13) | data formatting | bytes 192 | tf_op jit(solution)/shard_map/squeeze | solution.py:436
  14.1 1.4 %copy-done = bf16[1,1,12,256,256]{4,3,2,1,0:T(8,128)(2,1)S(1)} copy-done((bf16[1,1,12,256,256]{4,3,2,1,0:T(8,128)(2,1)S(1)}, bf16[1,1,12,256,256]{4,3,2,1,0:T(8,128)(2,1)}, u32[]{:S(2)}) %copy-start) | copy-done | bytes 1572888
  15.5 0.9 copy-done.2
  17.3 4.0 %shard_map.122.frames_hbm.refs_10_ = bf16[12,256,256]{2,1,0:T(8,128)(2,1)S(1)} custom-call(bf16[12,256,256]{2,1,0:T(8,128)(2,1)S(1)} %bitcast.11, bf16[256,256]{1,0:T(8,128)(2,1)S(1)} %copy-done.2, bf16[256,256]{1,0:T(8,128)(2,1)S(1)} %copy-done.3), custom_call_target="tpu_custom_call" | custom-call | flops 805306368 | bytes 3145728 | tf_op jit(solution)/shard_map/pallas_call | solution.py:444
  21.4 1.1 copy-done.1
  22.5 10.8 %collective-permute-start.3 = (bf16[2,256,256]{2,1,0:T(8,128)(2,1)S(1)}, bf16[2,256,256]{2,1,0:T(8,128)(2,1)S(1)}, u32[]{:S(2)}, u32[]{:S(2)}) collective-permute-start(bf16[2,256,256]{2,1,0:T(8,128)(2,1)S(1)} %collective-permute-done.2.refs_5_), channel_id=1, source_target_pairs={{8,0},{16,8},{24,16},{32,24},{40,32},{48,40},{56,48},{64,56},{72,6... | collective-permute-start | bytes 786440 | tf_op jit(solution)/shard_map/ppermute | solution.py:19
  33.4 1.0 copy-done.8
  34.3 8.8 %shard_map.123 = (f32[2,256,768]{2,1,0:T(8,128)}, bf16[2,256,768]{2,1,0:T(8,128)(2,1)}, f32[2,2,512,128]{3,2,1,0:T(8,128)}, f32[2,2,256,256]{3,2,1,0:T(8,128)}) custom-call(s32[12,2]{1,0:T(8,128)} %copy.13.pos.refs_0_, s32[1]{0:T(128)} %bitcast.9.cnt, bf16[2,256,1024]{2,1,0:T(8,128)(2,1)} %refs_3_.1, bf16[2,256,1024]{2,1,0:T(8,128)(2,1)} %copy-done.8, ...), custom_call_target="tpu_custom_call" | custom-call | flops 9663676416 | bytes 12582912 | tf_op jit(solution)/shard_map/pallas_call | solution.py:474
  43.8 6.2 %shard_map.124 = (f32[2,256,256]{2,1,0:T(8,128)}, bf16[2,256,512]{2,1,0:T(8,128)(2,1)}, bf16[2,256,256]{2,1,0:T(8,128)(2,1)}, f32[2,256,256]{2,1,0:T(8,128)}, bf16[2,256,256]{2,1,0:T(8,128)(2,1)}) custom-call(s32[12,2]{1,0:T(8,128)} %copy.13.pos.refs_0_, s32[1]{0:T(128)} %bitcast.10.refs_1_, s32[1]{0:T(128)} %bitcast.3.refs_2_, ...), custom_call_target="tpu_custom_call" | custom-call | flops 3221225472 | bytes 12582912 | tf_op jit(solution)/shard_map/pallas_call | solution.py:496
  50.0 5.5 %collective-permute-start.6 = (bf16[512,256]{1,0:T(8,128)(2,1)}, bf16[512,256]{1,0:T(8,128)(2,1)S(1)}, u32[]{:S(2)}, u32[]{:S(2)}) collective-permute-start(bf16[512,256]{1,0:T(8,128)(2,1)} %bitcast.14), channel_id=1, source_target_pairs={{0,8},{1,9},{2,10},{3,11},{4,12},{5,13},{6,14},{7,15},{8,0},{9,1},... | collective-permute-start | bytes 786440 | tf_op jit(solution)/shard_map/ppermute | solution.py:42
  55.5 1.4 %collective-permute-done.6 = bf16[512,256]{1,0:T(8,128)(2,1)S(1)} collective-permute-done((bf16[512,256]{1,0:T(8,128)(2,1)}, bf16[512,256]{1,0:T(8,128)(2,1)S(1)}, u32[]{:S(2)}, u32[]{:S(2)}) %collective-permute-start.6) | collective-permute-done | bytes 262176 | tf_op jit(solution)/shard_map/ppermute | solution.py:42
  56.9 1.2 bitcast_add_fusion
  58.1 10.6 %collective-permute-start.7 = (bf16[128,256]{1,0:T(8,128)(2,1)S(1)}, bf16[128,256]{1,0:T(8,128)(2,1)S(1)}, u32[]{:S(2)}, u32[]{:S(2)}) collective-permute-start(bf16[128,256]{1,0:T(8,128)(2,1)S(1)} %get-tuple-element.34), channel_id=1, source_target_pairs={{0,64},{1,65},{2,66},{3,67},{4,68},{5,69},{6,70},{7,71},{8,10},{9,... | collective-permute-start | bytes 196616 | tf_op jit(solution)/shard_map/ppermute | solution.py:42
  68.7 1.3 collective-permute-start.9
  70.3 3.0 %collective-permute-done.8 = bf16[128,256]{1,0:T(8,128)(2,1)S(1)} collective-permute-done((bf16[128,256]{1,0:T(8,128)(2,1)S(1)}, bf16[128,256]{1,0:T(8,128)(2,1)S(1)}, u32[]{:S(2)}, u32[]{:S(2)}) %collective-permute-start.8) | collective-permute-done | bytes 65568 | tf_op jit(solution)/shard_map/ppermute | solution.py:42
  73.5 3.1 %collective-permute-done.10 = bf16[128,256]{1,0:T(8,128)(2,1)S(1)} collective-permute-done((bf16[128,256]{1,0:T(8,128)(2,1)S(1)}, bf16[128,256]{1,0:T(8,128)(2,1)S(1)}, u32[]{:S(2)}, u32[]{:S(2)}) %collective-permute-start.10) | collective-permute-done | bytes 65568 | tf_op jit(solution)/shard_map/ppermute | solution.py:42
  76.6 1.0 collective-permute-start.11
  77.6 3.1 %collective-permute-done.11 = bf16[128,256]{1,0:T(8,128)(2,1)S(1)} collective-permute-done((bf16[128,256]{1,0:T(8,128)(2,1)S(1)}, bf16[128,256]{1,0:T(8,128)(2,1)S(1)}, u32[]{:S(2)}, u32[]{:S(2)}) %collective-permute-start.11) | collective-permute-done | bytes 65568 | tf_op jit(solution)/shard_map/ppermute | solution.py:42
  80.8 13.7 %collective-permute-start.4 = (bf16[2,256,512]{2,1,0:T(8,128)(2,1)S(1)}, bf16[2,256,512]{2,1,0:T(8,128)(2,1)S(1)}, u32[]{:S(2)}, u32[]{:S(2)}) collective-permute-start(bf16[2,256,512]{2,1,0:T(8,128)(2,1)S(1)} %copy-done.10), channel_id=1, source_target_pairs={{0,8},{8,16},{16,24},{24,32},{32,40},{40,48},{48,56},{56,64},{64,7... | collective-permute-start | bytes 1572872 | tf_op jit(solution)/shard_map/ppermute | solution.py:19
  94.7 1.4 %collective-permute-start.14 = (bf16[128,256]{1,0:T(8,128)(2,1)S(1)}, bf16[128,256]{1,0:T(8,128)(2,1)S(1)}, u32[]{:S(2)}, u32[]{:S(2)}) collective-permute-start(bf16[128,256]{1,0:T(8,128)(2,1)S(1)} %add_convert_fusion.2), channel_id=1, source_target_pairs={{0,4},{1,5},{2,6},{3,7},{4,0},{5,1},{6,2},{7,3},{8,136},{9,137},{1... | collective-permute-start | bytes 196616 | tf_op jit(solution)/shard_map/ppermute | solution.py:42
  96.1 2.5 %collective-permute-start.15 = (bf16[128,256]{1,0:T(8,128)(2,1)S(1)}, bf16[128,256]{1,0:T(8,128)(2,1)S(1)}, u32[]{:S(2)}, u32[]{:S(2)}) collective-permute-start(bf16[128,256]{1,0:T(8,128)(2,1)S(1)} %add_convert_fusion.2), channel_id=1, source_target_pairs={{0,6},{1,7},{2,4},{3,5},{4,2},{5,3},{6,0},{7,1},{8,200},{9,201},{1... | collective-permute-start | bytes 196616 | tf_op jit(solution)/shard_map/ppermute | solution.py:42
  98.5 6.9 %collective-permute-start.1 = (bf16[2,256,768]{2,1,0:T(8,128)(2,1)S(1)}, bf16[2,256,768]{2,1,0:T(8,128)(2,1)S(1)}, u32[]{:S(2)}, u32[]{:S(2)}) collective-permute-start(bf16[2,256,768]{2,1,0:T(8,128)(2,1)S(1)} %copy-done.9), channel_id=1, source_target_pairs={{0,8},{8,16},{16,24},{24,32},{32,40},{40,48},{48,56},{56,64},{64,7... | collective-permute-start | bytes 2359304 | tf_op jit(solution)/shard_map/ppermute | solution.py:19
  105.5 2.9 %collective-permute-start.16 = (bf16[128,256]{1,0:T(8,128)(2,1)S(1)}, bf16[128,256]{1,0:T(8,128)(2,1)S(1)}, u32[]{:S(2)}, u32[]{:S(2)}) collective-permute-start(bf16[128,256]{1,0:T(8,128)(2,1)S(1)} %get-tuple-element.33), channel_id=1, source_target_pairs={{0,64},{1,65},{2,66},{3,67},{4,68},{5,69},{6,70},{7,71},{8,10},{9,... | collective-permute-start | bytes 196616 | tf_op jit(solution)/shard_map/ppermute | solution.py:42
  108.6 2.1 %collective-permute-start.5 = (bf16[2,256,256]{2,1,0:T(8,128)(2,1)S(1)}, bf16[2,256,256]{2,1,0:T(8,128)(2,1)S(1)}, u32[]{:S(2)}, u32[]{:S(2)}) collective-permute-start(bf16[2,256,256]{2,1,0:T(8,128)(2,1)S(1)} %get-tuple-element.37), channel_id=1, source_target_pairs={{0,1},{1,2},{2,3},{3,4},{4,5},{5,6},{6,7},{8,9},{9,10},{10,11},{11... | collective-permute-start | bytes 786440 | tf_op jit(solution)/shard_map/ppermute | solution.py:19
  111.3 4.3 %collective-permute-done.17 = bf16[128,256]{1,0:T(8,128)(2,1)S(1)} collective-permute-done((bf16[128,256]{1,0:T(8,128)(2,1)S(1)}, bf16[128,256]{1,0:T(8,128)(2,1)S(1)}, u32[]{:S(2)}, u32[]{:S(2)}) %collective-permute-start.17) | collective-permute-done | bytes 65568 | tf_op jit(solution)/shard_map/ppermute | solution.py:42
  115.7 1.8 %collective-permute-start.19 = (bf16[512,256]{1,0:T(8,128)(2,1)S(1)}, bf16[512,256]{1,0:T(8,128)(2,1)S(1)}, u32[]{:S(2)}, u32[]{:S(2)}) collective-permute-start(bf16[512,256]{1,0:T(8,128)(2,1)S(1)} %constant_dynamic-update-slice_fusion.2), channel_id=1, source_target_pairs={{0,8},{1,9},{2,10},{3,11},{4,12},{5,13},{6,14},{7,15},{8,0},{9,1},... | collective-permute-start | bytes 786440 | tf_op jit(solution)/shard_map/ppermute | solution.py:42
  117.6 8.0 %collective-permute-done.1 = bf16[2,256,768]{2,1,0:T(8,128)(2,1)S(1)} collective-permute-done((bf16[2,256,768]{2,1,0:T(8,128)(2,1)S(1)}, bf16[2,256,768]{2,1,0:T(8,128)(2,1)S(1)}, u32[]{:S(2)}, u32[]{:S(2)}) %collective-permute-start.1) | collective-permute-done | bytes 786464 | tf_op jit(solution)/shard_map/ppermute | solution.py:19
  126.0 4.7 %collective-permute-done.5 = bf16[2,256,256]{2,1,0:T(8,128)(2,1)S(1)} collective-permute-done((bf16[2,256,256]{2,1,0:T(8,128)(2,1)S(1)}, bf16[2,256,256]{2,1,0:T(8,128)(2,1)S(1)}, u32[]{:S(2)}, u32[]{:S(2)}) %collective-permute-start.5) | collective-permute-done | bytes 262176 | tf_op jit(solution)/shard_map/ppermute | solution.py:19
  130.9 1.2 convert.1
  (58 shorter events, 4.4 us)
Async XLA Ops:
  0.6 32.7 %collective-permute-start = (bf16[2,256,1024]{2,1,0:T(8,128)(2,1)}, bf16[2,256,1024]{2,1,0:T(8,128)(2,1)S(1)}, u32[]{:S(2)}, u32[]{:S(2)}) collective-permute-start(bf16[2,256,1024]{2,1,0:T(8,128)(2,1)} %refs_3_.1), channel_id=1, source_target_pairs={{8,0},{16,8},{24,16},{32,24},{40,32},{48,40},{56,48},{64,56},{72,6... | collective-permute-start | bytes 3145736 | tf_op jit(solution)/shard_map/ppermute | solution.py:19
  4.2 18.3 %collective-permute-start.2 = (bf16[2,256,256]{2,1,0:T(8,128)(2,1)S(1)}, bf16[2,256,256]{2,1,0:T(8,128)(2,1)S(1)}, u32[]{:S(2)}, u32[]{:S(2)}) collective-permute-start(bf16[2,256,256]{2,1,0:T(8,128)(2,1)S(1)} %slice.34), channel_id=1, source_target_pairs={{1,0},{2,1},{3,2},{4,3},{5,4},{6,5},{7,6},{9,8},{10,9},{11,10},{12... | collective-permute-start | bytes 786440 | tf_op jit(solution)/shard_map/ppermute | solution.py:19
  14.1 1.4 %copy-start = (bf16[1,1,12,256,256]{4,3,2,1,0:T(8,128)(2,1)S(1)}, bf16[1,1,12,256,256]{4,3,2,1,0:T(8,128)(2,1)}, u32[]{:S(2)}) copy-start(bf16[1,1,12,256,256]{4,3,2,1,0:T(8,128)(2,1)} %param.15) | copy-start | bytes 4718596
  15.5 0.9 copy-start.2
  16.4 0.9 copy-start.3
  21.4 1.1 copy-start.1
  22.5 20.6 %copy-start.11 = (bf16[2,256,256]{2,1,0:T(8,128)(2,1)}, bf16[2,256,256]{2,1,0:T(8,128)(2,1)S(1)}, u32[]{:S(2)}) copy-start(bf16[2,256,256]{2,1,0:T(8,128)(2,1)S(1)} %collective-permute-done.2.refs_5_) | copy-start | bytes 786436
  22.5 20.6 %collective-permute-start.3 = (bf16[2,256,256]{2,1,0:T(8,128)(2,1)S(1)}, bf16[2,256,256]{2,1,0:T(8,128)(2,1)S(1)}, u32[]{:S(2)}, u32[]{:S(2)}) collective-permute-start(bf16[2,256,256]{2,1,0:T(8,128)(2,1)S(1)} %collective-permute-done.2.refs_5_), channel_id=1, source_target_pairs={{8,0},{16,8},{24,16},{32,24},{40,32},{48,40},{56,48},{64,56},{72,6... | collective-permute-start | bytes 786440 | tf_op jit(solution)/shard_map/ppermute | solution.py:19
  33.4 1.0 copy-start.8
  50.0 30.8 %copy-start.10 = (bf16[2,256,512]{2,1,0:T(8,128)(2,1)S(1)}, bf16[2,256,512]{2,1,0:T(8,128)(2,1)}, u32[]{:S(2)}) copy-start(bf16[2,256,512]{2,1,0:T(8,128)(2,1)} %get-tuple-element.28) | copy-start | bytes 1572868
  50.0 48.5 %copy-start.9 = (bf16[2,256,768]{2,1,0:T(8,128)(2,1)S(1)}, bf16[2,256,768]{2,1,0:T(8,128)(2,1)}, u32[]{:S(2)}) copy-start(bf16[2,256,768]{2,1,0:T(8,128)(2,1)} %get-tuple-element.24) | copy-start | bytes 2359300
  50.0 6.8 %collective-permute-start.6 = (bf16[512,256]{1,0:T(8,128)(2,1)}, bf16[512,256]{1,0:T(8,128)(2,1)S(1)}, u32[]{:S(2)}, u32[]{:S(2)}) collective-permute-start(bf16[512,256]{1,0:T(8,128)(2,1)} %bitcast.14), channel_id=1, source_target_pairs={{0,8},{1,9},{2,10},{3,11},{4,12},{5,13},{6,14},{7,15},{8,0},{9,1},... | collective-permute-start | bytes 786440 | tf_op jit(solution)/shard_map/ppermute | solution.py:42
  56.9 51.6 %copy-start.6 = (f32[2,256,256]{2,1,0:T(8,128)S(1)}, f32[2,256,256]{2,1,0:T(8,128)}, u32[]{:S(2)}) copy-start(f32[2,256,256]{2,1,0:T(8,128)} %get-tuple-element.27) | copy-start | bytes 1572868
  56.9 51.6 %copy-start.7 = (bf16[2,256,256]{2,1,0:T(8,128)(2,1)S(1)}, bf16[2,256,256]{2,1,0:T(8,128)(2,1)}, u32[]{:S(2)}) copy-start(bf16[2,256,256]{2,1,0:T(8,128)(2,1)} %get-tuple-element.29) | copy-start | bytes 786436
  58.1 12.3 %collective-permute-start.7 = (bf16[128,256]{1,0:T(8,128)(2,1)S(1)}, bf16[128,256]{1,0:T(8,128)(2,1)S(1)}, u32[]{:S(2)}, u32[]{:S(2)}) collective-permute-start(bf16[128,256]{1,0:T(8,128)(2,1)S(1)} %get-tuple-element.34), channel_id=1, source_target_pairs={{0,64},{1,65},{2,66},{3,67},{4,68},{5,69},{6,70},{7,71},{8,10},{9,... | collective-permute-start | bytes 196616 | tf_op jit(solution)/shard_map/ppermute | solution.py:42
  68.7 4.6 %collective-permute-start.8 = (bf16[128,256]{1,0:T(8,128)(2,1)S(1)}, bf16[128,256]{1,0:T(8,128)(2,1)S(1)}, u32[]{:S(2)}, u32[]{:S(2)}) collective-permute-start(bf16[128,256]{1,0:T(8,128)(2,1)S(1)} %get-tuple-element.36), channel_id=1, source_target_pairs={{0,128},{1,129},{2,130},{3,131},{4,132},{5,133},{6,134},{7,135},{8... | collective-permute-start | bytes 196616 | tf_op jit(solution)/shard_map/ppermute | solution.py:42
  68.7 4.6 %collective-permute-start.9 = (bf16[128,256]{1,0:T(8,128)(2,1)S(1)}, bf16[128,256]{1,0:T(8,128)(2,1)S(1)}, u32[]{:S(2)}, u32[]{:S(2)}) collective-permute-start(bf16[128,256]{1,0:T(8,128)(2,1)S(1)} %get-tuple-element.35), channel_id=1, source_target_pairs={{0,192},{1,193},{2,194},{3,195},{4,196},{5,197},{6,198},{7,199},{8... | collective-permute-start | bytes 196616 | tf_op jit(solution)/shard_map/ppermute | solution.py:42
  73.4 3.2 %collective-permute-start.10 = (bf16[128,256]{1,0:T(8,128)(2,1)S(1)}, bf16[128,256]{1,0:T(8,128)(2,1)S(1)}, u32[]{:S(2)}, u32[]{:S(2)}) collective-permute-start(bf16[128,256]{1,0:T(8,128)(2,1)S(1)} %add_convert_fusion.5), channel_id=1, source_target_pairs={{0,16},{1,17},{2,18},{3,19},{4,20},{5,21},{6,22},{7,23},{8,24},{9,... | collective-permute-start | bytes 196616 | tf_op jit(solution)/shard_map/ppermute | solution.py:42
  76.6 4.1 %collective-permute-start.11 = (bf16[128,256]{1,0:T(8,128)(2,1)S(1)}, bf16[128,256]{1,0:T(8,128)(2,1)S(1)}, u32[]{:S(2)}, u32[]{:S(2)}) collective-permute-start(bf16[128,256]{1,0:T(8,128)(2,1)S(1)} %add_convert_fusion.4), channel_id=1, source_target_pairs={{0,32},{1,33},{2,34},{3,35},{4,36},{5,37},{6,38},{7,39},{8,40},{9,... | collective-permute-start | bytes 196616 | tf_op jit(solution)/shard_map/ppermute | solution.py:42
  80.7 13.8 %collective-permute-start.12 = (bf16[128,256]{1,0:T(8,128)(2,1)S(1)}, bf16[128,256]{1,0:T(8,128)(2,1)S(1)}, u32[]{:S(2)}, u32[]{:S(2)}) collective-permute-start(bf16[128,256]{1,0:T(8,128)(2,1)S(1)} %add_convert_fusion.3), channel_id=1, source_target_pairs={{0,33},{1,32},{2,35},{3,34},{4,37},{5,36},{6,39},{7,38},{8,41},{9,... | collective-permute-start | bytes 196616 | tf_op jit(solution)/shard_map/ppermute | solution.py:42
  80.8 27.6 %collective-permute-start.4 = (bf16[2,256,512]{2,1,0:T(8,128)(2,1)S(1)}, bf16[2,256,512]{2,1,0:T(8,128)(2,1)S(1)}, u32[]{:S(2)}, u32[]{:S(2)}) collective-permute-start(bf16[2,256,512]{2,1,0:T(8,128)(2,1)S(1)} %copy-done.10), channel_id=1, source_target_pairs={{0,8},{8,16},{16,24},{24,32},{32,40},{40,48},{48,56},{56,64},{64,7... | collective-permute-start | bytes 1572872 | tf_op jit(solution)/shard_map/ppermute | solution.py:19
  94.6 10.8 %collective-permute-start.13 = (bf16[128,256]{1,0:T(8,128)(2,1)S(1)}, bf16[128,256]{1,0:T(8,128)(2,1)S(1)}, u32[]{:S(2)}, u32[]{:S(2)}) collective-permute-start(bf16[128,256]{1,0:T(8,128)(2,1)S(1)} %add_convert_fusion.2), channel_id=1, source_target_pairs={{0,2},{1,3},{2,0},{3,1},{4,6},{5,7},{6,4},{7,5},{8,72},{9,73},{10,... | collective-permute-start | bytes 196616 | tf_op jit(solution)/shard_map/ppermute | solution.py:42
  94.7 10.7 %collective-permute-start.14 = (bf16[128,256]{1,0:T(8,128)(2,1)S(1)}, bf16[128,256]{1,0:T(8,128)(2,1)S(1)}, u32[]{:S(2)}, u32[]{:S(2)}) collective-permute-start(bf16[128,256]{1,0:T(8,128)(2,1)S(1)} %add_convert_fusion.2), channel_id=1, source_target_pairs={{0,4},{1,5},{2,6},{3,7},{4,0},{5,1},{6,2},{7,3},{8,136},{9,137},{1... | collective-permute-start | bytes 196616 | tf_op jit(solution)/shard_map/ppermute | solution.py:42
  96.1 9.4 %collective-permute-start.15 = (bf16[128,256]{1,0:T(8,128)(2,1)S(1)}, bf16[128,256]{1,0:T(8,128)(2,1)S(1)}, u32[]{:S(2)}, u32[]{:S(2)}) collective-permute-start(bf16[128,256]{1,0:T(8,128)(2,1)S(1)} %add_convert_fusion.2), channel_id=1, source_target_pairs={{0,6},{1,7},{2,4},{3,5},{4,2},{5,3},{6,0},{7,1},{8,200},{9,201},{1... | collective-permute-start | bytes 196616 | tf_op jit(solution)/shard_map/ppermute | solution.py:42
  98.5 27.0 %collective-permute-start.1 = (bf16[2,256,768]{2,1,0:T(8,128)(2,1)S(1)}, bf16[2,256,768]{2,1,0:T(8,128)(2,1)S(1)}, u32[]{:S(2)}, u32[]{:S(2)}) collective-permute-start(bf16[2,256,768]{2,1,0:T(8,128)(2,1)S(1)} %copy-done.9), channel_id=1, source_target_pairs={{0,8},{8,16},{16,24},{24,32},{32,40},{40,48},{48,56},{56,64},{64,7... | collective-permute-start | bytes 2359304 | tf_op jit(solution)/shard_map/ppermute | solution.py:19
  105.5 5.8 %collective-permute-start.16 = (bf16[128,256]{1,0:T(8,128)(2,1)S(1)}, bf16[128,256]{1,0:T(8,128)(2,1)S(1)}, u32[]{:S(2)}, u32[]{:S(2)}) collective-permute-start(bf16[128,256]{1,0:T(8,128)(2,1)S(1)} %get-tuple-element.33), channel_id=1, source_target_pairs={{0,64},{1,65},{2,66},{3,67},{4,68},{5,69},{6,70},{7,71},{8,10},{9,... | collective-permute-start | bytes 196616 | tf_op jit(solution)/shard_map/ppermute | solution.py:42
  108.5 17.1 %copy-start.5 = (f32[2,256,768]{2,1,0:T(8,128)S(1)}, f32[2,256,768]{2,1,0:T(8,128)}, u32[]{:S(2)}) copy-start(f32[2,256,768]{2,1,0:T(8,128)} %get-tuple-element.23) | copy-start | bytes 4718596
  108.6 22.2 %collective-permute-start.5 = (bf16[2,256,256]{2,1,0:T(8,128)(2,1)S(1)}, bf16[2,256,256]{2,1,0:T(8,128)(2,1)S(1)}, u32[]{:S(2)}, u32[]{:S(2)}) collective-permute-start(bf16[2,256,256]{2,1,0:T(8,128)(2,1)S(1)} %get-tuple-element.37), channel_id=1, source_target_pairs={{0,1},{1,2},{2,3},{3,4},{4,5},{5,6},{6,7},{8,9},{9,10},{10,11},{11... | collective-permute-start | bytes 786440 | tf_op jit(solution)/shard_map/ppermute | solution.py:19
  110.6 5.0 %collective-permute-start.17 = (bf16[128,256]{1,0:T(8,128)(2,1)S(1)}, bf16[128,256]{1,0:T(8,128)(2,1)S(1)}, u32[]{:S(2)}, u32[]{:S(2)}) collective-permute-start(bf16[128,256]{1,0:T(8,128)(2,1)S(1)} %get-tuple-element.33), channel_id=1, source_target_pairs={{0,128},{1,129},{2,130},{3,131},{4,132},{5,133},{6,134},{7,135},{8... | collective-permute-start | bytes 196616 | tf_op jit(solution)/shard_map/ppermute | solution.py:42
  110.7 4.9 %collective-permute-start.18 = (bf16[128,256]{1,0:T(8,128)(2,1)S(1)}, bf16[128,256]{1,0:T(8,128)(2,1)S(1)}, u32[]{:S(2)}, u32[]{:S(2)}) collective-permute-start(bf16[128,256]{1,0:T(8,128)(2,1)S(1)} %get-tuple-element.33), channel_id=1, source_target_pairs={{0,192},{1,193},{2,194},{3,195},{4,196},{5,197},{6,198},{7,199},{8... | collective-permute-start | bytes 196616 | tf_op jit(solution)/shard_map/ppermute | solution.py:42
  115.7 15.2 %collective-permute-start.19 = (bf16[512,256]{1,0:T(8,128)(2,1)S(1)}, bf16[512,256]{1,0:T(8,128)(2,1)S(1)}, u32[]{:S(2)}, u32[]{:S(2)}) collective-permute-start(bf16[512,256]{1,0:T(8,128)(2,1)S(1)} %constant_dynamic-update-slice_fusion.2), channel_id=1, source_target_pairs={{0,8},{1,9},{2,10},{3,11},{4,12},{5,13},{6,14},{7,15},{8,0},{9,1},... | collective-permute-start | bytes 786440 | tf_op jit(solution)/shard_map/ppermute | solution.py:42
  130.8 1.7 %copy-start.4 = (f32[2,256,1024]{2,1,0:T(8,128)}, f32[2,256,1024]{2,1,0:T(8,128)S(1)}, u32[]{:S(2)}) copy-start(f32[2,256,1024]{2,1,0:T(8,128)S(1)} %fusion) | copy-start | bytes 6291460
  (1 other events, 0.7 us)

commit v3 on v2

--- a/solution.py
+++ b/solution.py
@@ -279,7 +279,34 @@
     chunks = list(range(0, n, ch))
     pairs = [(m, k) for m in range(2) for k in range(2)]
 
-    def step(t, _):
+    def front(t):
+        now = window(t)
+        slot = lax.rem(t, 2)
+        for i in chunks:
+            wave_rows(now, slot, i)
+        for m, part in pairs:
+            forward_left(m, part)
+        for q in range(2):
+            for m in range(2):
+                forward_right(m, q)
+            for i in chunks:
+                weigh_rows(now, q, i)
+
+    def rear(t):
+        old = window(t)
+        slot = lax.rem(t, 2)
+        for m in range(2):
+            for par in range(2):
+                inverse_left(m, par)
+            for part in range(2):
+                for i in range(0, h, ch):
+                    join_rows(m, part, i)
+            for q in range(2):
+                inverse_right(m, q)
+        for i in chunks:
+            add_rows(old, slot, i)
+
+    def both(t, _):
         now = window(t)
         old = window(t - 1)
         new_slot = lax.rem(t, 2)
@@ -310,14 +337,18 @@
                 weigh_rows(now, 0, i)
         for i in chunks:
             weigh_rows(now, 1, i)
-
-        @pl.when(t == 0)
-        def _():
-            clear()
-
         return 0
 
-    lax.fori_loop(0, count + 1, step, 0)
+    @pl.when(count > 0)
+    def _():
+        front(0)
+
+    clear()
+    lax.fori_loop(1, count, both, 0)
+
+    @pl.when(count > 0)
+    def _():
+        rear(count - 1)
 
 
 def fill(ext, sources):

time: 133 us -> 131 us (0.985)
  Pallas kernels: 19 us -> 17.2 us
  transfers between devices with their start and end apart: 20 -> 20, of which waited for: 8 -> 8; matrix products, arithmetic and copies ran while one was open for 2% -> 2% of each run, Pallas kernels for 10% -> 9%
where the time goes in v3:
time: 131 us
  starting transfers between devices  71.4 us (55%)
  waiting for transfers between devices  28.2 us (22%)
  Pallas kernels  17.2 us (13%)
  local copies, waits for them, and re-layouts  8.98 us (7%)
  other arithmetic  3.12 us (2%)
  between operations  1.67 us (1%)
    ppermute x6, starting transfers between devices, shifted(): return lax.ppermute(x, axis, pairs)  43.9 us
    ppermute x14, starting transfers between devices, partner(): return lax.ppermute(v, ('row', 'col'), pairs)  27.5 us
    ppermute x14, waiting for transfers between devices, partner(): return lax.ppermute(v, ('row', 'col'), pairs)  15.4 us
    ppermute x6, waiting for transfers between devices, shifted(): return lax.ppermute(x, axis, pairs)  12.8 us
    pallas_call x1, Pallas kernels, body(): pl.pallas_call(inner_kernel, out_shape=(jax.ShapeDtypeStruct((2, tile_row...  7.78 us
    unnamed x26, local copies, waits for them, and re-layouts  6.48 us
    pallas_call x1, Pallas kernels, body(): pl.pallas_call(lambda *refs: edge_kernel(scale, *refs), out_shape=(jax.Sh...  5.35 us
    pallas_call x1, Pallas kernels, body(): pl.pallas_call(prep_kernel, out_shape=jax.ShapeDtypeStruct(measured.shape...  4.03 us
  transfers between devices with their start and end apart: 20, of which 8 were waited for; matrix products, arithmetic and copies ran while one was open for 2% of the time, Pallas kernels for 9%

profile of v3, /device:TPU:35, one launch (start us, length us, event | category | flops | bytes accessed | tf_op | source)
XLA Modules:
  0.0 130.5 jit_solution(8406021406678155486)
XLA Ops:
  0.6 2.6 %collective-permute-start = (bf16[2,256,1024]{2,1,0:T(8,128)(2,1)}, bf16[2,256,1024]{2,1,0:T(8,128)(2,1)S(1)}, u32[]{:S(2)}, u32[]{:S(2)}) collective-permute-start(bf16[2,256,1024]{2,1,0:T(8,128)(2,1)} %refs_3_.1), channel_id=1, source_target_pairs={{8,0},{16,8},{24,16},{32,24},{40,32},{48,40},{56,48},{64,56},{72,6... | collective-permute-start | bytes 3145736 | tf_op jit(solution)/shard_map/ppermute | solution.py:19
  3.2 1.0 slice.34
  4.2 7.9 %collective-permute-start.2 = (bf16[2,256,256]{2,1,0:T(8,128)(2,1)S(1)}, bf16[2,256,256]{2,1,0:T(8,128)(2,1)S(1)}, u32[]{:S(2)}, u32[]{:S(2)}) collective-permute-start(bf16[2,256,256]{2,1,0:T(8,128)(2,1)S(1)} %slice.34), channel_id=1, source_target_pairs={{1,0},{2,1},{3,2},{4,3},{5,4},{6,5},{7,6},{9,8},{10,9},{11,10},{12... | collective-permute-start | bytes 786440 | tf_op jit(solution)/shard_map/ppermute | solution.py:19
  12.1 1.4 %copy.13.pos.refs_0_ = s32[12,2]{1,0:T(8,128)} copy(s32[12,2]{0,1:T(2,128)} %bitcast.13) | data formatting | bytes 192 | tf_op jit(solution)/shard_map/squeeze | solution.py:467
  14.1 1.4 %copy-done = bf16[1,1,12,256,256]{4,3,2,1,0:T(8,128)(2,1)S(1)} copy-done((bf16[1,1,12,256,256]{4,3,2,1,0:T(8,128)(2,1)S(1)}, bf16[1,1,12,256,256]{4,3,2,1,0:T(8,128)(2,1)}, u32[]{:S(2)}) %copy-start) | copy-done | bytes 1572888
  15.5 0.9 copy-done.2
  16.4 0.9 copy-done.3
  17.3 4.0 %shard_map.122.frames_hbm.refs_10_ = bf16[12,256,256]{2,1,0:T(8,128)(2,1)S(1)} custom-call(bf16[12,256,256]{2,1,0:T(8,128)(2,1)S(1)} %bitcast.11, bf16[256,256]{1,0:T(8,128)(2,1)S(1)} %copy-done.2, bf16[256,256]{1,0:T(8,128)(2,1)S(1)} %copy-done.3), custom_call_target="tpu_custom_call" | custom-call | flops 805306368 | bytes 3145728 | tf_op jit(solution)/shard_map/pallas_call | solution.py:475
  21.4 1.1 copy-done.1
  22.5 10.8 %collective-permute-start.3 = (bf16[2,256,256]{2,1,0:T(8,128)(2,1)S(1)}, bf16[2,256,256]{2,1,0:T(8,128)(2,1)S(1)}, u32[]{:S(2)}, u32[]{:S(2)}) collective-permute-start(bf16[2,256,256]{2,1,0:T(8,128)(2,1)S(1)} %collective-permute-done.2.refs_5_), channel_id=1, source_target_pairs={{8,0},{16,8},{24,16},{32,24},{40,32},{48,40},{56,48},{64,56},{72,6... | collective-permute-start | bytes 786440 | tf_op jit(solution)/shard_map/ppermute | solution.py:19
  33.4 1.0 copy-done.8
  34.3 7.8 %shard_map.123 = (f32[2,256,768]{2,1,0:T(8,128)}, bf16[2,256,768]{2,1,0:T(8,128)(2,1)}, f32[2,2,512,128]{3,2,1,0:T(8,128)}, f32[2,2,256,256]{3,2,1,0:T(8,128)}) custom-call(s32[12,2]{1,0:T(8,128)} %copy.13.pos.refs_0_, s32[1]{0:T(128)} %bitcast.9.cnt, bf16[2,256,1024]{2,1,0:T(8,128)(2,1)} %refs_3_.1, bf16[2,256,1024]{2,1,0:T(8,128)(2,1)} %copy-done.8, ...), custom_call_target="tpu_custom_call" | custom-call | flops 9663676416 | bytes 12582912 | tf_op jit(solution)/shard_map/pallas_call | solution.py:505
  42.9 5.3 %shard_map.124 = (f32[2,256,256]{2,1,0:T(8,128)}, bf16[2,256,512]{2,1,0:T(8,128)(2,1)}, bf16[2,256,256]{2,1,0:T(8,128)(2,1)}, f32[2,256,256]{2,1,0:T(8,128)}, bf16[2,256,256]{2,1,0:T(8,128)(2,1)}) custom-call(s32[12,2]{1,0:T(8,128)} %copy.13.pos.refs_0_, s32[1]{0:T(128)} %bitcast.10.refs_1_, s32[1]{0:T(128)} %bitcast.3.refs_2_, ...), custom_call_target="tpu_custom_call" | custom-call | flops 3221225472 | bytes 12582912 | tf_op jit(solution)/shard_map/pallas_call | solution.py:527
  48.2 5.2 %collective-permute-start.6 = (bf16[512,256]{1,0:T(8,128)(2,1)}, bf16[512,256]{1,0:T(8,128)(2,1)S(1)}, u32[]{:S(2)}, u32[]{:S(2)}) collective-permute-start(bf16[512,256]{1,0:T(8,128)(2,1)} %bitcast.14), channel_id=1, source_target_pairs={{0,8},{1,9},{2,10},{3,11},{4,12},{5,13},{6,14},{7,15},{8,0},{9,1},... | collective-permute-start | bytes 786440 | tf_op jit(solution)/shard_map/ppermute | solution.py:42
  53.4 1.4 %collective-permute-done.6 = bf16[512,256]{1,0:T(8,128)(2,1)S(1)} collective-permute-done((bf16[512,256]{1,0:T(8,128)(2,1)}, bf16[512,256]{1,0:T(8,128)(2,1)S(1)}, u32[]{:S(2)}, u32[]{:S(2)}) %collective-permute-start.6) | collective-permute-done | bytes 262176 | tf_op jit(solution)/shard_map/ppermute | solution.py:42
  54.8 1.2 bitcast_add_fusion
  56.0 10.7 %collective-permute-start.7 = (bf16[128,256]{1,0:T(8,128)(2,1)S(1)}, bf16[128,256]{1,0:T(8,128)(2,1)S(1)}, u32[]{:S(2)}, u32[]{:S(2)}) collective-permute-start(bf16[128,256]{1,0:T(8,128)(2,1)S(1)} %get-tuple-element.34), channel_id=1, source_target_pairs={{0,64},{1,65},{2,66},{3,67},{4,68},{5,69},{6,70},{7,71},{8,10},{9,... | collective-permute-start | bytes 196616 | tf_op jit(solution)/shard_map/ppermute | solution.py:42
  66.7 1.3 collective-permute-start.9
  68.4 3.0 %collective-permute-done.8 = bf16[128,256]{1,0:T(8,128)(2,1)S(1)} collective-permute-done((bf16[128,256]{1,0:T(8,128)(2,1)S(1)}, bf16[128,256]{1,0:T(8,128)(2,1)S(1)}, u32[]{:S(2)}, u32[]{:S(2)}) %collective-permute-start.8) | collective-permute-done | bytes 65568 | tf_op jit(solution)/shard_map/ppermute | solution.py:42
  71.5 3.1 %collective-permute-done.10 = bf16[128,256]{1,0:T(8,128)(2,1)S(1)} collective-permute-done((bf16[128,256]{1,0:T(8,128)(2,1)S(1)}, bf16[128,256]{1,0:T(8,128)(2,1)S(1)}, u32[]{:S(2)}, u32[]{:S(2)}) %collective-permute-start.10) | collective-permute-done | bytes 65568 | tf_op jit(solution)/shard_map/ppermute | solution.py:42
  75.5 3.2 %collective-permute-done.11 = bf16[128,256]{1,0:T(8,128)(2,1)S(1)} collective-permute-done((bf16[128,256]{1,0:T(8,128)(2,1)S(1)}, bf16[128,256]{1,0:T(8,128)(2,1)S(1)}, u32[]{:S(2)}, u32[]{:S(2)}) %collective-permute-start.11) | collective-permute-done | bytes 65568 | tf_op jit(solution)/shard_map/ppermute | solution.py:42
  79.0 13.7 %collective-permute-start.4 = (bf16[2,256,512]{2,1,0:T(8,128)(2,1)S(1)}, bf16[2,256,512]{2,1,0:T(8,128)(2,1)S(1)}, u32[]{:S(2)}, u32[]{:S(2)}) collective-permute-start(bf16[2,256,512]{2,1,0:T(8,128)(2,1)S(1)} %copy-done.10), channel_id=1, source_target_pairs={{0,8},{8,16},{16,24},{24,32},{32,40},{40,48},{48,56},{56,64},{64,7... | collective-permute-start | bytes 1572872 | tf_op jit(solution)/shard_map/ppermute | solution.py:19
  92.8 1.4 %collective-permute-start.14 = (bf16[128,256]{1,0:T(8,128)(2,1)S(1)}, bf16[128,256]{1,0:T(8,128)(2,1)S(1)}, u32[]{:S(2)}, u32[]{:S(2)}) collective-permute-start(bf16[128,256]{1,0:T(8,128)(2,1)S(1)} %add_convert_fusion.2), channel_id=1, source_target_pairs={{0,4},{1,5},{2,6},{3,7},{4,0},{5,1},{6,2},{7,3},{8,136},{9,137},{1... | collective-permute-start | bytes 196616 | tf_op jit(solution)/shard_map/ppermute | solution.py:42
  94.2 2.5 %collective-permute-start.15 = (bf16[128,256]{1,0:T(8,128)(2,1)S(1)}, bf16[128,256]{1,0:T(8,128)(2,1)S(1)}, u32[]{:S(2)}, u32[]{:S(2)}) collective-permute-start(bf16[128,256]{1,0:T(8,128)(2,1)S(1)} %add_convert_fusion.2), channel_id=1, source_target_pairs={{0,6},{1,7},{2,4},{3,5},{4,2},{5,3},{6,0},{7,1},{8,200},{9,201},{1... | collective-permute-start | bytes 196616 | tf_op jit(solution)/shard_map/ppermute | solution.py:42
  96.7 6.9 %collective-permute-start.1 = (bf16[2,256,768]{2,1,0:T(8,128)(2,1)S(1)}, bf16[2,256,768]{2,1,0:T(8,128)(2,1)S(1)}, u32[]{:S(2)}, u32[]{:S(2)}) collective-permute-start(bf16[2,256,768]{2,1,0:T(8,128)(2,1)S(1)} %copy-done.9), channel_id=1, source_target_pairs={{0,8},{8,16},{16,24},{24,32},{32,40},{40,48},{48,56},{56,64},{64,7... | collective-permute-start | bytes 2359304 | tf_op jit(solution)/shard_map/ppermute | solution.py:19
  103.7 2.9 %collective-permute-start.16 = (bf16[128,256]{1,0:T(8,128)(2,1)S(1)}, bf16[128,256]{1,0:T(8,128)(2,1)S(1)}, u32[]{:S(2)}, u32[]{:S(2)}) collective-permute-start(bf16[128,256]{1,0:T(8,128)(2,1)S(1)} %get-tuple-element.33), channel_id=1, source_target_pairs={{0,64},{1,65},{2,66},{3,67},{4,68},{5,69},{6,70},{7,71},{8,10},{9,... | collective-permute-start | bytes 196616 | tf_op jit(solution)/shard_map/ppermute | solution.py:42
  106.7 2.1 %collective-permute-start.5 = (bf16[2,256,256]{2,1,0:T(8,128)(2,1)S(1)}, bf16[2,256,256]{2,1,0:T(8,128)(2,1)S(1)}, u32[]{:S(2)}, u32[]{:S(2)}) collective-permute-start(bf16[2,256,256]{2,1,0:T(8,128)(2,1)S(1)} %get-tuple-element.37), channel_id=1, source_target_pairs={{0,1},{1,2},{2,3},{3,4},{4,5},{5,6},{6,7},{8,9},{9,10},{10,11},{11... | collective-permute-start | bytes 786440 | tf_op jit(solution)/shard_map/ppermute | solution.py:19
  109.5 4.3 %collective-permute-done.17 = bf16[128,256]{1,0:T(8,128)(2,1)S(1)} collective-permute-done((bf16[128,256]{1,0:T(8,128)(2,1)S(1)}, bf16[128,256]{1,0:T(8,128)(2,1)S(1)}, u32[]{:S(2)}, u32[]{:S(2)}) %collective-permute-start.17) | collective-permute-done | bytes 65568 | tf_op jit(solution)/shard_map/ppermute | solution.py:42
  113.8 1.6 %collective-permute-start.19 = (bf16[512,256]{1,0:T(8,128)(2,1)S(1)}, bf16[512,256]{1,0:T(8,128)(2,1)S(1)}, u32[]{:S(2)}, u32[]{:S(2)}) collective-permute-start(bf16[512,256]{1,0:T(8,128)(2,1)S(1)} %constant_dynamic-update-slice_fusion.2), channel_id=1, source_target_pairs={{0,8},{1,9},{2,10},{3,11},{4,12},{5,13},{6,14},{7,15},{8,0},{9,1},... | collective-permute-start | bytes 786440 | tf_op jit(solution)/shard_map/ppermute | solution.py:42
  115.5 8.2 %collective-permute-done.1 = bf16[2,256,768]{2,1,0:T(8,128)(2,1)S(1)} collective-permute-done((bf16[2,256,768]{2,1,0:T(8,128)(2,1)S(1)}, bf16[2,256,768]{2,1,0:T(8,128)(2,1)S(1)}, u32[]{:S(2)}, u32[]{:S(2)}) %collective-permute-start.1) | collective-permute-done | bytes 786464 | tf_op jit(solution)/shard_map/ppermute | solution.py:19
  124.2 4.6 %collective-permute-done.5 = bf16[2,256,256]{2,1,0:T(8,128)(2,1)S(1)} collective-permute-done((bf16[2,256,256]{2,1,0:T(8,128)(2,1)S(1)}, bf16[2,256,256]{2,1,0:T(8,128)(2,1)S(1)}, u32[]{:S(2)}, u32[]{:S(2)}) %collective-permute-start.5) | collective-permute-done | bytes 262176 | tf_op jit(solution)/shard_map/ppermute | solution.py:19
  128.9 1.2 convert.1
  (58 shorter events, 4.5 us)
Async XLA Ops:
  0.6 32.7 %collective-permute-start = (bf16[2,256,1024]{2,1,0:T(8,128)(2,1)}, bf16[2,256,1024]{2,1,0:T(8,128)(2,1)S(1)}, u32[]{:S(2)}, u32[]{:S(2)}) collective-permute-start(bf16[2,256,1024]{2,1,0:T(8,128)(2,1)} %refs_3_.1), channel_id=1, source_target_pairs={{8,0},{16,8},{24,16},{32,24},{40,32},{48,40},{56,48},{64,56},{72,6... | collective-permute-start | bytes 3145736 | tf_op jit(solution)/shard_map/ppermute | solution.py:19
  4.2 18.3 %collective-permute-start.2 = (bf16[2,256,256]{2,1,0:T(8,128)(2,1)S(1)}, bf16[2,256,256]{2,1,0:T(8,128)(2,1)S(1)}, u32[]{:S(2)}, u32[]{:S(2)}) collective-permute-start(bf16[2,256,256]{2,1,0:T(8,128)(2,1)S(1)} %slice.34), channel_id=1, source_target_pairs={{1,0},{2,1},{3,2},{4,3},{5,4},{6,5},{7,6},{9,8},{10,9},{11,10},{12... | collective-permute-start | bytes 786440 | tf_op jit(solution)/shard_map/ppermute | solution.py:19
  14.1 1.4 %copy-start = (bf16[1,1,12,256,256]{4,3,2,1,0:T(8,128)(2,1)S(1)}, bf16[1,1,12,256,256]{4,3,2,1,0:T(8,128)(2,1)}, u32[]{:S(2)}) copy-start(bf16[1,1,12,256,256]{4,3,2,1,0:T(8,128)(2,1)} %param.15) | copy-start | bytes 4718596
  15.5 0.9 copy-start.2
  16.4 0.9 copy-start.3
  21.4 1.1 copy-start.1
  22.5 19.6 %copy-start.11 = (bf16[2,256,256]{2,1,0:T(8,128)(2,1)}, bf16[2,256,256]{2,1,0:T(8,128)(2,1)S(1)}, u32[]{:S(2)}) copy-start(bf16[2,256,256]{2,1,0:T(8,128)(2,1)S(1)} %collective-permute-done.2.refs_5_) | copy-start | bytes 786436
  22.5 19.6 %collective-permute-start.3 = (bf16[2,256,256]{2,1,0:T(8,128)(2,1)S(1)}, bf16[2,256,256]{2,1,0:T(8,128)(2,1)S(1)}, u32[]{:S(2)}, u32[]{:S(2)}) collective-permute-start(bf16[2,256,256]{2,1,0:T(8,128)(2,1)S(1)} %collective-permute-done.2.refs_5_), channel_id=1, source_target_pairs={{8,0},{16,8},{24,16},{32,24},{40,32},{48,40},{56,48},{64,56},{72,6... | collective-permute-start | bytes 786440 | tf_op jit(solution)/shard_map/ppermute | solution.py:19
  33.4 1.0 copy-start.8
  48.2 30.8 %copy-start.10 = (bf16[2,256,512]{2,1,0:T(8,128)(2,1)S(1)}, bf16[2,256,512]{2,1,0:T(8,128)(2,1)}, u32[]{:S(2)}) copy-start(bf16[2,256,512]{2,1,0:T(8,128)(2,1)} %get-tuple-element.28) | copy-start | bytes 1572868
  48.2 48.5 %copy-start.9 = (bf16[2,256,768]{2,1,0:T(8,128)(2,1)S(1)}, bf16[2,256,768]{2,1,0:T(8,128)(2,1)}, u32[]{:S(2)}) copy-start(bf16[2,256,768]{2,1,0:T(8,128)(2,1)} %get-tuple-element.24) | copy-start | bytes 2359300
  48.2 6.6 %collective-permute-start.6 = (bf16[512,256]{1,0:T(8,128)(2,1)}, bf16[512,256]{1,0:T(8,128)(2,1)S(1)}, u32[]{:S(2)}, u32[]{:S(2)}) collective-permute-start(bf16[512,256]{1,0:T(8,128)(2,1)} %bitcast.14), channel_id=1, source_target_pairs={{0,8},{1,9},{2,10},{3,11},{4,12},{5,13},{6,14},{7,15},{8,0},{9,1},... | collective-permute-start | bytes 786440 | tf_op jit(solution)/shard_map/ppermute | solution.py:42
  54.8 51.8 %copy-start.6 = (f32[2,256,256]{2,1,0:T(8,128)S(1)}, f32[2,256,256]{2,1,0:T(8,128)}, u32[]{:S(2)}) copy-start(f32[2,256,256]{2,1,0:T(8,128)} %get-tuple-element.27) | copy-start | bytes 1572868
  54.8 51.8 %copy-start.7 = (bf16[2,256,256]{2,1,0:T(8,128)(2,1)S(1)}, bf16[2,256,256]{2,1,0:T(8,128)(2,1)}, u32[]{:S(2)}) copy-start(bf16[2,256,256]{2,1,0:T(8,128)(2,1)} %get-tuple-element.29) | copy-start | bytes 786436
  56.0 12.3 %collective-permute-start.7 = (bf16[128,256]{1,0:T(8,128)(2,1)S(1)}, bf16[128,256]{1,0:T(8,128)(2,1)S(1)}, u32[]{:S(2)}, u32[]{:S(2)}) collective-permute-start(bf16[128,256]{1,0:T(8,128)(2,1)S(1)} %get-tuple-element.34), channel_id=1, source_target_pairs={{0,64},{1,65},{2,66},{3,67},{4,68},{5,69},{6,70},{7,71},{8,10},{9,... | collective-permute-start | bytes 196616 | tf_op jit(solution)/shard_map/ppermute | solution.py:42
  66.7 4.6 %collective-permute-start.8 = (bf16[128,256]{1,0:T(8,128)(2,1)S(1)}, bf16[128,256]{1,0:T(8,128)(2,1)S(1)}, u32[]{:S(2)}, u32[]{:S(2)}) collective-permute-start(bf16[128,256]{1,0:T(8,128)(2,1)S(1)} %get-tuple-element.36), channel_id=1, source_target_pairs={{0,128},{1,129},{2,130},{3,131},{4,132},{5,133},{6,134},{7,135},{8... | collective-permute-start | bytes 196616 | tf_op jit(solution)/shard_map/ppermute | solution.py:42
  66.7 4.6 %collective-permute-start.9 = (bf16[128,256]{1,0:T(8,128)(2,1)S(1)}, bf16[128,256]{1,0:T(8,128)(2,1)S(1)}, u32[]{:S(2)}, u32[]{:S(2)}) collective-permute-start(bf16[128,256]{1,0:T(8,128)(2,1)S(1)} %get-tuple-element.35), channel_id=1, source_target_pairs={{0,192},{1,193},{2,194},{3,195},{4,196},{5,197},{6,198},{7,199},{8... | collective-permute-start | bytes 196616 | tf_op jit(solution)/shard_map/ppermute | solution.py:42
  71.4 3.2 %collective-permute-start.10 = (bf16[128,256]{1,0:T(8,128)(2,1)S(1)}, bf16[128,256]{1,0:T(8,128)(2,1)S(1)}, u32[]{:S(2)}, u32[]{:S(2)}) collective-permute-start(bf16[128,256]{1,0:T(8,128)(2,1)S(1)} %add_convert_fusion.5), channel_id=1, source_target_pairs={{0,16},{1,17},{2,18},{3,19},{4,20},{5,21},{6,22},{7,23},{8,24},{9,... | collective-permute-start | bytes 196616 | tf_op jit(solution)/shard_map/ppermute | solution.py:42
  74.6 4.1 %collective-permute-start.11 = (bf16[128,256]{1,0:T(8,128)(2,1)S(1)}, bf16[128,256]{1,0:T(8,128)(2,1)S(1)}, u32[]{:S(2)}, u32[]{:S(2)}) collective-permute-start(bf16[128,256]{1,0:T(8,128)(2,1)S(1)} %add_convert_fusion.4), channel_id=1, source_target_pairs={{0,32},{1,33},{2,34},{3,35},{4,36},{5,37},{6,38},{7,39},{8,40},{9,... | collective-permute-start | bytes 196616 | tf_op jit(solution)/shard_map/ppermute | solution.py:42
  78.7 14.0 %collective-permute-start.12 = (bf16[128,256]{1,0:T(8,128)(2,1)S(1)}, bf16[128,256]{1,0:T(8,128)(2,1)S(1)}, u32[]{:S(2)}, u32[]{:S(2)}) collective-permute-start(bf16[128,256]{1,0:T(8,128)(2,1)S(1)} %add_convert_fusion.3), channel_id=1, source_target_pairs={{0,33},{1,32},{2,35},{3,34},{4,37},{5,36},{6,39},{7,38},{8,41},{9,... | collective-permute-start | bytes 196616 | tf_op jit(solution)/shard_map/ppermute | solution.py:42
  79.0 27.6 %collective-permute-start.4 = (bf16[2,256,512]{2,1,0:T(8,128)(2,1)S(1)}, bf16[2,256,512]{2,1,0:T(8,128)(2,1)S(1)}, u32[]{:S(2)}, u32[]{:S(2)}) collective-permute-start(bf16[2,256,512]{2,1,0:T(8,128)(2,1)S(1)} %copy-done.10), channel_id=1, source_target_pairs={{0,8},{8,16},{16,24},{24,32},{32,40},{40,48},{48,56},{56,64},{64,7... | collective-permute-start | bytes 1572872 | tf_op jit(solution)/shard_map/ppermute | solution.py:19
  92.7 10.8 %collective-permute-start.13 = (bf16[128,256]{1,0:T(8,128)(2,1)S(1)}, bf16[128,256]{1,0:T(8,128)(2,1)S(1)}, u32[]{:S(2)}, u32[]{:S(2)}) collective-permute-start(bf16[128,256]{1,0:T(8,128)(2,1)S(1)} %add_convert_fusion.2), channel_id=1, source_target_pairs={{0,2},{1,3},{2,0},{3,1},{4,6},{5,7},{6,4},{7,5},{8,72},{9,73},{10,... | collective-permute-start | bytes 196616 | tf_op jit(solution)/shard_map/ppermute | solution.py:42
  92.8 10.8 %collective-permute-start.14 = (bf16[128,256]{1,0:T(8,128)(2,1)S(1)}, bf16[128,256]{1,0:T(8,128)(2,1)S(1)}, u32[]{:S(2)}, u32[]{:S(2)}) collective-permute-start(bf16[128,256]{1,0:T(8,128)(2,1)S(1)} %add_convert_fusion.2), channel_id=1, source_target_pairs={{0,4},{1,5},{2,6},{3,7},{4,0},{5,1},{6,2},{7,3},{8,136},{9,137},{1... | collective-permute-start | bytes 196616 | tf_op jit(solution)/shard_map/ppermute | solution.py:42
  94.2 9.4 %collective-permute-start.15 = (bf16[128,256]{1,0:T(8,128)(2,1)S(1)}, bf16[128,256]{1,0:T(8,128)(2,1)S(1)}, u32[]{:S(2)}, u32[]{:S(2)}) collective-permute-start(bf16[128,256]{1,0:T(8,128)(2,1)S(1)} %add_convert_fusion.2), channel_id=1, source_target_pairs={{0,6},{1,7},{2,4},{3,5},{4,2},{5,3},{6,0},{7,1},{8,200},{9,201},{1... | collective-permute-start | bytes 196616 | tf_op jit(solution)/shard_map/ppermute | solution.py:42
  96.7 27.0 %collective-permute-start.1 = (bf16[2,256,768]{2,1,0:T(8,128)(2,1)S(1)}, bf16[2,256,768]{2,1,0:T(8,128)(2,1)S(1)}, u32[]{:S(2)}, u32[]{:S(2)}) collective-permute-start(bf16[2,256,768]{2,1,0:T(8,128)(2,1)S(1)} %copy-done.9), channel_id=1, source_target_pairs={{0,8},{8,16},{16,24},{24,32},{32,40},{40,48},{48,56},{56,64},{64,7... | collective-permute-start | bytes 2359304 | tf_op jit(solution)/shard_map/ppermute | solution.py:19
  103.7 5.8 %collective-permute-start.16 = (bf16[128,256]{1,0:T(8,128)(2,1)S(1)}, bf16[128,256]{1,0:T(8,128)(2,1)S(1)}, u32[]{:S(2)}, u32[]{:S(2)}) collective-permute-start(bf16[128,256]{1,0:T(8,128)(2,1)S(1)} %get-tuple-element.33), channel_id=1, source_target_pairs={{0,64},{1,65},{2,66},{3,67},{4,68},{5,69},{6,70},{7,71},{8,10},{9,... | collective-permute-start | bytes 196616 | tf_op jit(solution)/shard_map/ppermute | solution.py:42
  106.6 17.1 %copy-start.5 = (f32[2,256,768]{2,1,0:T(8,128)S(1)}, f32[2,256,768]{2,1,0:T(8,128)}, u32[]{:S(2)}) copy-start(f32[2,256,768]{2,1,0:T(8,128)} %get-tuple-element.23) | copy-start | bytes 4718596
  106.7 22.1 %collective-permute-start.5 = (bf16[2,256,256]{2,1,0:T(8,128)(2,1)S(1)}, bf16[2,256,256]{2,1,0:T(8,128)(2,1)S(1)}, u32[]{:S(2)}, u32[]{:S(2)}) collective-permute-start(bf16[2,256,256]{2,1,0:T(8,128)(2,1)S(1)} %get-tuple-element.37), channel_id=1, source_target_pairs={{0,1},{1,2},{2,3},{3,4},{4,5},{5,6},{6,7},{8,9},{9,10},{10,11},{11... | collective-permute-start | bytes 786440 | tf_op jit(solution)/shard_map/ppermute | solution.py:19
  108.8 5.0 %collective-permute-start.17 = (bf16[128,256]{1,0:T(8,128)(2,1)S(1)}, bf16[128,256]{1,0:T(8,128)(2,1)S(1)}, u32[]{:S(2)}, u32[]{:S(2)}) collective-permute-start(bf16[128,256]{1,0:T(8,128)(2,1)S(1)} %get-tuple-element.33), channel_id=1, source_target_pairs={{0,128},{1,129},{2,130},{3,131},{4,132},{5,133},{6,134},{7,135},{8... | collective-permute-start | bytes 196616 | tf_op jit(solution)/shard_map/ppermute | solution.py:42
  108.9 4.9 %collective-permute-start.18 = (bf16[128,256]{1,0:T(8,128)(2,1)S(1)}, bf16[128,256]{1,0:T(8,128)(2,1)S(1)}, u32[]{:S(2)}, u32[]{:S(2)}) collective-permute-start(bf16[128,256]{1,0:T(8,128)(2,1)S(1)} %get-tuple-element.33), channel_id=1, source_target_pairs={{0,192},{1,193},{2,194},{3,195},{4,196},{5,197},{6,198},{7,199},{8... | collective-permute-start | bytes 196616 | tf_op jit(solution)/shard_map/ppermute | solution.py:42
  113.8 15.0 %collective-permute-start.19 = (bf16[512,256]{1,0:T(8,128)(2,1)S(1)}, bf16[512,256]{1,0:T(8,128)(2,1)S(1)}, u32[]{:S(2)}, u32[]{:S(2)}) collective-permute-start(bf16[512,256]{1,0:T(8,128)(2,1)S(1)} %constant_dynamic-update-slice_fusion.2), channel_id=1, source_target_pairs={{0,8},{1,9},{2,10},{3,11},{4,12},{5,13},{6,14},{7,15},{8,0},{9,1},... | collective-permute-start | bytes 786440 | tf_op jit(solution)/shard_map/ppermute | solution.py:42
  128.9 1.7 %copy-start.4 = (f32[2,256,1024]{2,1,0:T(8,128)}, f32[2,256,1024]{2,1,0:T(8,128)S(1)}, u32[]{:S(2)}) copy-start(f32[2,256,1024]{2,1,0:T(8,128)S(1)} %fusion) | copy-start | bytes 6291460
  (1 other events, 0.7 us)

commit v4 on v3

--- a/solution.py
+++ b/solution.py
@@ -375,10 +375,17 @@
     return copies
 
 
+def send_out(source, target, sem):
+    copy = pltpu.make_async_copy(source, target, sem)
+    copy.start()
+    return copy
+
+
 def inner_kernel(
     pos, cnt, own_hbm, below_hbm, probe_hbm, frames_hbm, left_hbm, right_hbm, gl_hbm, gr_hbm,
-    g_own, g_below, carry, p_out,
-    own, below, probe, frames, left, right, gl, gr, sems, frame_sems, ext, gext, *scratch,
+    g_own_hbm, g_below_hbm, carry_hbm, p_hbm,
+    own, below, probe, frames, left, right, gl, gr, sems, frame_sems, out_sems, g_own, g_below, p_out,
+    ext, gext, *scratch,
 ):
     copies = fetch(
         (own_hbm, below_hbm, probe_hbm, left_hbm, right_hbm, gl_hbm, gr_hbm),
@@ -406,17 +413,23 @@
         pos, count, 0, tc // 128, clear, probe, frames, (left, right, gl, gr), p_out,
         ext, gext, *scratch,
     )
-    drain(gext, ((g_own, 0, inner, 0, 0), (g_below, 0, inner, tr, 0)))
+    done = [send_out(p_out, p_hbm, out_sems.at[0])]
     for p in range(2):
-        for b in range(n // 128):
-            carry[p, b] = gext[p, inner // 128 + b]
+        done.append(send_out(gext.at[p, pl.ds(inner // 128, n // 128)], carry_hbm.at[p], out_sems.at[1 + p]))
+    drain(gext, ((g_below, 0, inner, tr, 0),))
+    done.append(send_out(g_below, g_below_hbm, out_sems.at[3]))
+    drain(gext, ((g_own, 0, inner, 0, 0),))
+    done.append(send_out(g_own, g_own_hbm, out_sems.at[4]))
+    for copy in done:
+        copy.wait()
 
 
 def edge_kernel(
     scale, pos, cnt, core, own_hbm, below_hbm, strip_hbm, corner_hbm, carry_hbm, p_hbm, probe_hbm, frames_hbm,
     left_hbm, right_hbm, gl_hbm, gr_hbm,
-    g_own, g_rows, g_strip, p_keep, p_send,
-    own, below, strip, corner, carry, p_in, probe, frames, left, right, gl, gr, sems, frame_sems, p_out, ext, gext, *scratch,
+    g_own_hbm, g_rows_hbm, g_strip_hbm, p_keep_hbm, p_send_hbm,
+    own, below, strip, corner, carry, p_in, probe, frames, left, right, gl, gr, sems, frame_sems, out_sems,
+    g_own, g_rows, g_strip, p_keep, p_send, p_out, ext, gext, *scratch,
 ):
     n = probe.shape[-1]
     tr, tc = own_hbm.shape[1:]
@@ -451,9 +464,18 @@
         pos, count, inner // 128, 2 * n // 128, clear, probe, frames,
         (left, right, gl, gr), p_out, ext, gext, *scratch,
     )
+    p_send[...] = (p_out[1 - core[0]] * scale).astype(bf16)
+    done = [send_out(p_send, p_send_hbm, out_sems.at[0])]
     p_keep[...] = p_out[core[0]] * scale
-    p_send[...] = (p_out[1 - core[0]] * scale).astype(bf16)
-    drain(gext, ((g_own, 0, n, 0, 0), (g_rows, 0, 2 * n, tr, 0), (g_strip, 0, n, 0, n)))
+    done.append(send_out(p_keep, p_keep_hbm, out_sems.at[1]))
+    drain(gext, ((g_rows, 0, 2 * n, tr, 0),))
+    done.append(send_out(g_rows, g_rows_hbm, out_sems.at[2]))
+    drain(gext, ((g_strip, 0, n, 0, n),))
+    done.append(send_out(g_strip, g_strip_hbm, out_sems.at[3]))
+    drain(gext, ((g_own, 0, n, 0, 0),))
+    done.append(send_out(g_own, g_own_hbm, out_sems.at[4]))
+    for copy in done:
+        copy.wait()
 
 
 def body(object_field, probe, measured, positions, counts):
@@ -511,13 +533,18 @@
             jax.ShapeDtypeStruct(probe.shape, f32),
         ),
         in_specs=[smem, smem] + [stay] * 8,
-        out_specs=[vmem] * 4,
+        out_specs=[stay] * 4,
         scratch_shapes=[
             pltpu.VMEM((2, tile_rows, tile_cols), bf16),
             pltpu.VMEM((2, size, tile_cols), bf16),
         ]
         + fixed
-        + [pltpu.SemaphoreType.DMA((7,)), pltpu.SemaphoreType.DMA((slots,))]
+        + [pltpu.SemaphoreType.DMA((k,)) for k in (7, slots, 5)]
+        + [
+            pltpu.VMEM((2, tile_rows, inner), f32),
+            pltpu.VMEM((2, size, inner), bf16),
+            pltpu.VMEM(probe.shape, f32),
+        ]
         + scratch(tile_cols // 128),
         compiler_params=params,
         cost_estimate=pl.CostEstimate(flops=9 * 2**30, bytes_accessed=12 * 2**20, transcendentals=0),
@@ -534,7 +561,7 @@
             jax.ShapeDtypeStruct(probe.shape[1:], bf16),
         ),
         in_specs=[smem] * 3 + [stay] * 12,
-        out_specs=[vmem] * 5,
+        out_specs=[stay] * 5,
         scratch_shapes=[
             pltpu.VMEM((2, tile_rows, size), bf16),
             pltpu.VMEM((2, size, size), bf16),
@@ -544,7 +571,15 @@
             pltpu.VMEM(probe.shape, f32),
         ]
         + fixed
-        + [pltpu.SemaphoreType.DMA((11,)), pltpu.SemaphoreType.DMA((slots,)), pltpu.VMEM(probe.shape, f32)]
+        + [pltpu.SemaphoreType.DMA((k,)) for k in (11, slots, 5)]
+        + [
+            pltpu.VMEM((2, tile_rows, size), f32),
+            pltpu.VMEM((2, size, 2 * size), bf16),
+            pltpu.VMEM((2, tile_rows, size), bf16),
+            pltpu.VMEM(probe.shape[1:], f32),
+            pltpu.VMEM(probe.shape[1:], bf16),
+            pltpu.VMEM(probe.shape, f32),
+        ]
         + scratch(2 * size // 128),
         compiler_params=params,
         cost_estimate=pl.CostEstimate(flops=3 * 2**30, bytes_accessed=12 * 2**20, transcendentals=0),
@@ -555,8 +590,9 @@
     to_right = (g_strip.astype(f32) + tail[:, :, size:].astype(f32)).astype(bf16)
     side = shifted(to_right, "col", 1)
     probe_grad = reduce_all(p_keep.reshape(-1, size), p_send.reshape(-1, size)).reshape(probe.shape)
+    main = g_main + band.astype(f32)
     object_grad = jnp.concatenate(
-        [g_main + band.astype(f32), g_right + tail[:, :, :size].astype(f32)], 2
+        [main, g_right + tail[:, :, :size].astype(f32)], 2
     )
     object_grad = object_grad.at[:, :, :size].add(side.astype(f32))
     return (object_grad, probe_grad)

time: 131 us -> 131 us (level)
  no operation moved by 1% of the time
where the time goes in v4:
time: 131 us; the launch traced here: 130 us
  starting transfers between devices  71.4 us (55%)
  waiting for transfers between devices  28.2 us (22%)
  Pallas kernels  17.1 us (13%)
  local copies, waits for them, and re-layouts  8.98 us (7%)
  other arithmetic  3.12 us (2%)
  between operations  1.67 us (1%)
    ppermute x6, starting transfers between devices, shifted(): return lax.ppermute(x, axis, pairs)  43.9 us
    ppermute x14, starting transfers between devices, partner(): return lax.ppermute(v, ('row', 'col'), pairs)  27.5 us
    ppermute x14, waiting for transfers between devices, partner(): return lax.ppermute(v, ('row', 'col'), pairs)  15.4 us
    ppermute x6, waiting for transfers between devices, shifted(): return lax.ppermute(x, axis, pairs)  12.8 us
    pallas_call x1, Pallas kernels, body(): pl.pallas_call(inner_kernel, out_shape=(jax.ShapeDtypeStruct((2, tile_row...  7.75 us
    unnamed x26, local copies, waits for them, and re-layouts  6.48 us
    pallas_call x1, Pallas kernels, body(): pl.pallas_call(lambda *refs: edge_kernel(scale, *refs), out_shape=(jax.Sh...  5.3 us
    pallas_call x1, Pallas kernels, body(): pl.pallas_call(prep_kernel, out_shape=jax.ShapeDtypeStruct(measured.shape...  4.03 us
  transfers between devices with their start and end apart: 20, of which 8 were waited for; matrix products, arithmetic and copies ran while one was open for 2% of the time, Pallas kernels for 9%

profile of v4, /device:TPU:35, one launch (start us, length us, event | category | flops | bytes accessed | tf_op | source)
XLA Modules:
  0.0 130.5 jit_solution(6397623926210614324)
XLA Ops:
  0.6 2.6 %collective-permute-start = (bf16[2,256,1024]{2,1,0:T(8,128)(2,1)}, bf16[2,256,1024]{2,1,0:T(8,128)(2,1)S(1)}, u32[]{:S(2)}, u32[]{:S(2)}) collective-permute-start(bf16[2,256,1024]{2,1,0:T(8,128)(2,1)} %refs_3_.1), channel_id=1, source_target_pairs={{8,0},{16,8},{24,16},{32,24},{40,32},{48,40},{56,48},{64,56},{72,6... | collective-permute-start | bytes 3145736 | tf_op jit(solution)/shard_map/ppermute | solution.py:19
  3.2 1.0 slice.34
  4.2 7.9 %collective-permute-start.2 = (bf16[2,256,256]{2,1,0:T(8,128)(2,1)S(1)}, bf16[2,256,256]{2,1,0:T(8,128)(2,1)S(1)}, u32[]{:S(2)}, u32[]{:S(2)}) collective-permute-start(bf16[2,256,256]{2,1,0:T(8,128)(2,1)S(1)} %slice.34), channel_id=1, source_target_pairs={{1,0},{2,1},{3,2},{4,3},{5,4},{6,5},{7,6},{9,8},{10,9},{11,10},{12... | collective-permute-start | bytes 786440 | tf_op jit(solution)/shard_map/ppermute | solution.py:19
  12.1 1.4 %copy.13.pos.refs_0_ = s32[12,2]{1,0:T(8,128)} copy(s32[12,2]{0,1:T(2,128)} %bitcast.13) | data formatting | bytes 192 | tf_op jit(solution)/shard_map/squeeze | solution.py:489
  14.1 1.4 %copy-done = bf16[1,1,12,256,256]{4,3,2,1,0:T(8,128)(2,1)S(1)} copy-done((bf16[1,1,12,256,256]{4,3,2,1,0:T(8,128)(2,1)S(1)}, bf16[1,1,12,256,256]{4,3,2,1,0:T(8,128)(2,1)}, u32[]{:S(2)}) %copy-start) | copy-done | bytes 1572888
  15.5 0.9 copy-done.2
  16.4 0.9 copy-done.3
  17.3 4.0 %shard_map.122.frames_hbm.refs_10_ = bf16[12,256,256]{2,1,0:T(8,128)(2,1)S(1)} custom-call(bf16[12,256,256]{2,1,0:T(8,128)(2,1)S(1)} %bitcast.11, bf16[256,256]{1,0:T(8,128)(2,1)S(1)} %copy-done.2, bf16[256,256]{1,0:T(8,128)(2,1)S(1)} %copy-done.3), custom_call_target="tpu_custom_call" | custom-call | flops 805306368 | bytes 3145728 | tf_op jit(solution)/shard_map/pallas_call | solution.py:497
  21.4 1.1 copy-done.1
  22.5 10.8 %collective-permute-start.3 = (bf16[2,256,256]{2,1,0:T(8,128)(2,1)S(1)}, bf16[2,256,256]{2,1,0:T(8,128)(2,1)S(1)}, u32[]{:S(2)}, u32[]{:S(2)}) collective-permute-start(bf16[2,256,256]{2,1,0:T(8,128)(2,1)S(1)} %collective-permute-done.2.refs_5_), channel_id=1, source_target_pairs={{8,0},{16,8},{24,16},{32,24},{40,32},{48,40},{56,48},{64,56},{72,6... | collective-permute-start | bytes 786440 | tf_op jit(solution)/shard_map/ppermute | solution.py:19
  33.4 1.0 copy-done.8
  34.3 7.8 %shard_map.123 = (f32[2,256,768]{2,1,0:T(8,128)}, bf16[2,256,768]{2,1,0:T(8,128)(2,1)}, f32[2,2,512,128]{3,2,1,0:T(8,128)}, f32[2,2,256,256]{3,2,1,0:T(8,128)}) custom-call(s32[12,2]{1,0:T(8,128)} %copy.13.pos.refs_0_, s32[1]{0:T(128)} %bitcast.9.cnt, bf16[2,256,1024]{2,1,0:T(8,128)(2,1)} %refs_3_.1, bf16[2,256,1024]{2,1,0:T(8,128)(2,1)} %copy-done.8, ...), custom_call_target="tpu_custom_call" | custom-call | flops 9663676416 | bytes 12582912 | tf_op jit(solution)/shard_map/pallas_call | solution.py:527
  42.8 5.3 %shard_map.124 = (f32[2,256,256]{2,1,0:T(8,128)}, bf16[2,256,512]{2,1,0:T(8,128)(2,1)}, bf16[2,256,256]{2,1,0:T(8,128)(2,1)}, f32[2,256,256]{2,1,0:T(8,128)}, bf16[2,256,256]{2,1,0:T(8,128)(2,1)}) custom-call(s32[12,2]{1,0:T(8,128)} %copy.13.pos.refs_0_, s32[1]{0:T(128)} %bitcast.10.refs_1_, s32[1]{0:T(128)} %bitcast.3.refs_2_, ...), custom_call_target="tpu_custom_call" | custom-call | flops 3221225472 | bytes 12582912 | tf_op jit(solution)/shard_map/pallas_call | solution.py:554
  48.1 5.2 %collective-permute-start.6 = (bf16[512,256]{1,0:T(8,128)(2,1)}, bf16[512,256]{1,0:T(8,128)(2,1)S(1)}, u32[]{:S(2)}, u32[]{:S(2)}) collective-permute-start(bf16[512,256]{1,0:T(8,128)(2,1)} %bitcast.14), channel_id=1, source_target_pairs={{0,8},{1,9},{2,10},{3,11},{4,12},{5,13},{6,14},{7,15},{8,0},{9,1},... | collective-permute-start | bytes 786440 | tf_op jit(solution)/shard_map/ppermute | solution.py:42
  53.3 1.4 %collective-permute-done.6 = bf16[512,256]{1,0:T(8,128)(2,1)S(1)} collective-permute-done((bf16[512,256]{1,0:T(8,128)(2,1)}, bf16[512,256]{1,0:T(8,128)(2,1)S(1)}, u32[]{:S(2)}, u32[]{:S(2)}) %collective-permute-start.6) | collective-permute-done | bytes 262176 | tf_op jit(solution)/shard_map/ppermute | solution.py:42
  54.7 1.2 bitcast_add_fusion
  55.9 10.7 %collective-permute-start.7 = (bf16[128,256]{1,0:T(8,128)(2,1)S(1)}, bf16[128,256]{1,0:T(8,128)(2,1)S(1)}, u32[]{:S(2)}, u32[]{:S(2)}) collective-permute-start(bf16[128,256]{1,0:T(8,128)(2,1)S(1)} %get-tuple-element.34), channel_id=1, source_target_pairs={{0,64},{1,65},{2,66},{3,67},{4,68},{5,69},{6,70},{7,71},{8,10},{9,... | collective-permute-start | bytes 196616 | tf_op jit(solution)/shard_map/ppermute | solution.py:42
  66.6 1.3 collective-permute-start.9
  68.3 3.0 %collective-permute-done.8 = bf16[128,256]{1,0:T(8,128)(2,1)S(1)} collective-permute-done((bf16[128,256]{1,0:T(8,128)(2,1)S(1)}, bf16[128,256]{1,0:T(8,128)(2,1)S(1)}, u32[]{:S(2)}, u32[]{:S(2)}) %collective-permute-start.8) | collective-permute-done | bytes 65568 | tf_op jit(solution)/shard_map/ppermute | solution.py:42
  71.4 3.1 %collective-permute-done.10 = bf16[128,256]{1,0:T(8,128)(2,1)S(1)} collective-permute-done((bf16[128,256]{1,0:T(8,128)(2,1)S(1)}, bf16[128,256]{1,0:T(8,128)(2,1)S(1)}, u32[]{:S(2)}, u32[]{:S(2)}) %collective-permute-start.10) | collective-permute-done | bytes 65568 | tf_op jit(solution)/shard_map/ppermute | solution.py:42
  75.4 3.2 %collective-permute-done.11 = bf16[128,256]{1,0:T(8,128)(2,1)S(1)} collective-permute-done((bf16[128,256]{1,0:T(8,128)(2,1)S(1)}, bf16[128,256]{1,0:T(8,128)(2,1)S(1)}, u32[]{:S(2)}, u32[]{:S(2)}) %collective-permute-start.11) | collective-permute-done | bytes 65568 | tf_op jit(solution)/shard_map/ppermute | solution.py:42
  78.9 13.7 %collective-permute-start.4 = (bf16[2,256,512]{2,1,0:T(8,128)(2,1)S(1)}, bf16[2,256,512]{2,1,0:T(8,128)(2,1)S(1)}, u32[]{:S(2)}, u32[]{:S(2)}) collective-permute-start(bf16[2,256,512]{2,1,0:T(8,128)(2,1)S(1)} %copy-done.10), channel_id=1, source_target_pairs={{0,8},{8,16},{16,24},{24,32},{32,40},{40,48},{48,56},{56,64},{64,7... | collective-permute-start | bytes 1572872 | tf_op jit(solution)/shard_map/ppermute | solution.py:19
  92.8 1.4 %collective-permute-start.14 = (bf16[128,256]{1,0:T(8,128)(2,1)S(1)}, bf16[128,256]{1,0:T(8,128)(2,1)S(1)}, u32[]{:S(2)}, u32[]{:S(2)}) collective-permute-start(bf16[128,256]{1,0:T(8,128)(2,1)S(1)} %add_convert_fusion.2), channel_id=1, source_target_pairs={{0,4},{1,5},{2,6},{3,7},{4,0},{5,1},{6,2},{7,3},{8,136},{9,137},{1... | collective-permute-start | bytes 196616 | tf_op jit(solution)/shard_map/ppermute | solution.py:42
  94.1 2.5 %collective-permute-start.15 = (bf16[128,256]{1,0:T(8,128)(2,1)S(1)}, bf16[128,256]{1,0:T(8,128)(2,1)S(1)}, u32[]{:S(2)}, u32[]{:S(2)}) collective-permute-start(bf16[128,256]{1,0:T(8,128)(2,1)S(1)} %add_convert_fusion.2), channel_id=1, source_target_pairs={{0,6},{1,7},{2,4},{3,5},{4,2},{5,3},{6,0},{7,1},{8,200},{9,201},{1... | collective-permute-start | bytes 196616 | tf_op jit(solution)/shard_map/ppermute | solution.py:42
  96.6 6.9 %collective-permute-start.1 = (bf16[2,256,768]{2,1,0:T(8,128)(2,1)S(1)}, bf16[2,256,768]{2,1,0:T(8,128)(2,1)S(1)}, u32[]{:S(2)}, u32[]{:S(2)}) collective-permute-start(bf16[2,256,768]{2,1,0:T(8,128)(2,1)S(1)} %copy-done.9), channel_id=1, source_target_pairs={{0,8},{8,16},{16,24},{24,32},{32,40},{40,48},{48,56},{56,64},{64,7... | collective-permute-start | bytes 2359304 | tf_op jit(solution)/shard_map/ppermute | solution.py:19
  103.6 2.9 %collective-permute-start.16 = (bf16[128,256]{1,0:T(8,128)(2,1)S(1)}, bf16[128,256]{1,0:T(8,128)(2,1)S(1)}, u32[]{:S(2)}, u32[]{:S(2)}) collective-permute-start(bf16[128,256]{1,0:T(8,128)(2,1)S(1)} %get-tuple-element.33), channel_id=1, source_target_pairs={{0,64},{1,65},{2,66},{3,67},{4,68},{5,69},{6,70},{7,71},{8,10},{9,... | collective-permute-start | bytes 196616 | tf_op jit(solution)/shard_map/ppermute | solution.py:42
  106.7 2.1 %collective-permute-start.5 = (bf16[2,256,256]{2,1,0:T(8,128)(2,1)S(1)}, bf16[2,256,256]{2,1,0:T(8,128)(2,1)S(1)}, u32[]{:S(2)}, u32[]{:S(2)}) collective-permute-start(bf16[2,256,256]{2,1,0:T(8,128)(2,1)S(1)} %get-tuple-element.37), channel_id=1, source_target_pairs={{0,1},{1,2},{2,3},{3,4},{4,5},{5,6},{6,7},{8,9},{9,10},{10,11},{11... | collective-permute-start | bytes 786440 | tf_op jit(solution)/shard_map/ppermute | solution.py:19
  109.4 4.3 %collective-permute-done.17 = bf16[128,256]{1,0:T(8,128)(2,1)S(1)} collective-permute-done((bf16[128,256]{1,0:T(8,128)(2,1)S(1)}, bf16[128,256]{1,0:T(8,128)(2,1)S(1)}, u32[]{:S(2)}, u32[]{:S(2)}) %collective-permute-start.17) | collective-permute-done | bytes 65568 | tf_op jit(solution)/shard_map/ppermute | solution.py:42
  113.8 1.6 %collective-permute-start.19 = (bf16[512,256]{1,0:T(8,128)(2,1)S(1)}, bf16[512,256]{1,0:T(8,128)(2,1)S(1)}, u32[]{:S(2)}, u32[]{:S(2)}) collective-permute-start(bf16[512,256]{1,0:T(8,128)(2,1)S(1)} %constant_dynamic-update-slice_fusion.2), channel_id=1, source_target_pairs={{0,8},{1,9},{2,10},{3,11},{4,12},{5,13},{6,14},{7,15},{8,0},{9,1},... | collective-permute-start | bytes 786440 | tf_op jit(solution)/shard_map/ppermute | solution.py:42
  115.4 8.2 %collective-permute-done.1 = bf16[2,256,768]{2,1,0:T(8,128)(2,1)S(1)} collective-permute-done((bf16[2,256,768]{2,1,0:T(8,128)(2,1)S(1)}, bf16[2,256,768]{2,1,0:T(8,128)(2,1)S(1)}, u32[]{:S(2)}, u32[]{:S(2)}) %collective-permute-start.1) | collective-permute-done | bytes 786464 | tf_op jit(solution)/shard_map/ppermute | solution.py:19
  124.1 4.6 %collective-permute-done.5 = bf16[2,256,256]{2,1,0:T(8,128)(2,1)S(1)} collective-permute-done((bf16[2,256,256]{2,1,0:T(8,128)(2,1)S(1)}, bf16[2,256,256]{2,1,0:T(8,128)(2,1)S(1)}, u32[]{:S(2)}, u32[]{:S(2)}) %collective-permute-start.5) | collective-permute-done | bytes 262176 | tf_op jit(solution)/shard_map/ppermute | solution.py:19
  128.8 1.2 convert.1
  (58 shorter events, 4.5 us)
Async XLA Ops:
  0.6 32.7 %collective-permute-start = (bf16[2,256,1024]{2,1,0:T(8,128)(2,1)}, bf16[2,256,1024]{2,1,0:T(8,128)(2,1)S(1)}, u32[]{:S(2)}, u32[]{:S(2)}) collective-permute-start(bf16[2,256,1024]{2,1,0:T(8,128)(2,1)} %refs_3_.1), channel_id=1, source_target_pairs={{8,0},{16,8},{24,16},{32,24},{40,32},{48,40},{56,48},{64,56},{72,6... | collective-permute-start | bytes 3145736 | tf_op jit(solution)/shard_map/ppermute | solution.py:19
  4.2 18.3 %collective-permute-start.2 = (bf16[2,256,256]{2,1,0:T(8,128)(2,1)S(1)}, bf16[2,256,256]{2,1,0:T(8,128)(2,1)S(1)}, u32[]{:S(2)}, u32[]{:S(2)}) collective-permute-start(bf16[2,256,256]{2,1,0:T(8,128)(2,1)S(1)} %slice.34), channel_id=1, source_target_pairs={{1,0},{2,1},{3,2},{4,3},{5,4},{6,5},{7,6},{9,8},{10,9},{11,10},{12... | collective-permute-start | bytes 786440 | tf_op jit(solution)/shard_map/ppermute | solution.py:19
  14.1 1.4 %copy-start = (bf16[1,1,12,256,256]{4,3,2,1,0:T(8,128)(2,1)S(1)}, bf16[1,1,12,256,256]{4,3,2,1,0:T(8,128)(2,1)}, u32[]{:S(2)}) copy-start(bf16[1,1,12,256,256]{4,3,2,1,0:T(8,128)(2,1)} %param.15) | copy-start | bytes 4718596
  15.5 0.9 copy-start.2
  16.4 0.9 copy-start.3
  21.4 1.1 copy-start.1
  22.5 19.6 %copy-start.11 = (bf16[2,256,256]{2,1,0:T(8,128)(2,1)}, bf16[2,256,256]{2,1,0:T(8,128)(2,1)S(1)}, u32[]{:S(2)}) copy-start(bf16[2,256,256]{2,1,0:T(8,128)(2,1)S(1)} %collective-permute-done.2.refs_5_) | copy-start | bytes 786436
  22.5 19.6 %collective-permute-start.3 = (bf16[2,256,256]{2,1,0:T(8,128)(2,1)S(1)}, bf16[2,256,256]{2,1,0:T(8,128)(2,1)S(1)}, u32[]{:S(2)}, u32[]{:S(2)}) collective-permute-start(bf16[2,256,256]{2,1,0:T(8,128)(2,1)S(1)} %collective-permute-done.2.refs_5_), channel_id=1, source_target_pairs={{8,0},{16,8},{24,16},{32,24},{40,32},{48,40},{56,48},{64,56},{72,6... | collective-permute-start | bytes 786440 | tf_op jit(solution)/shard_map/ppermute | solution.py:19
  33.4 1.0 copy-start.8
  48.1 30.8 %copy-start.10 = (bf16[2,256,512]{2,1,0:T(8,128)(2,1)S(1)}, bf16[2,256,512]{2,1,0:T(8,128)(2,1)}, u32[]{:S(2)}) copy-start(bf16[2,256,512]{2,1,0:T(8,128)(2,1)} %get-tuple-element.28) | copy-start | bytes 1572868
  48.1 48.5 %copy-start.9 = (bf16[2,256,768]{2,1,0:T(8,128)(2,1)S(1)}, bf16[2,256,768]{2,1,0:T(8,128)(2,1)}, u32[]{:S(2)}) copy-start(bf16[2,256,768]{2,1,0:T(8,128)(2,1)} %get-tuple-element.24) | copy-start | bytes 2359300
  48.1 6.6 %collective-permute-start.6 = (bf16[512,256]{1,0:T(8,128)(2,1)}, bf16[512,256]{1,0:T(8,128)(2,1)S(1)}, u32[]{:S(2)}, u32[]{:S(2)}) collective-permute-start(bf16[512,256]{1,0:T(8,128)(2,1)} %bitcast.14), channel_id=1, source_target_pairs={{0,8},{1,9},{2,10},{3,11},{4,12},{5,13},{6,14},{7,15},{8,0},{9,1},... | collective-permute-start | bytes 786440 | tf_op jit(solution)/shard_map/ppermute | solution.py:42
  54.7 51.8 %copy-start.6 = (f32[2,256,256]{2,1,0:T(8,128)S(1)}, f32[2,256,256]{2,1,0:T(8,128)}, u32[]{:S(2)}) copy-start(f32[2,256,256]{2,1,0:T(8,128)} %get-tuple-element.27) | copy-start | bytes 1572868
  54.7 51.8 %copy-start.7 = (bf16[2,256,256]{2,1,0:T(8,128)(2,1)S(1)}, bf16[2,256,256]{2,1,0:T(8,128)(2,1)}, u32[]{:S(2)}) copy-start(bf16[2,256,256]{2,1,0:T(8,128)(2,1)} %get-tuple-element.29) | copy-start | bytes 786436
  55.9 12.4 %collective-permute-start.7 = (bf16[128,256]{1,0:T(8,128)(2,1)S(1)}, bf16[128,256]{1,0:T(8,128)(2,1)S(1)}, u32[]{:S(2)}, u32[]{:S(2)}) collective-permute-start(bf16[128,256]{1,0:T(8,128)(2,1)S(1)} %get-tuple-element.34), channel_id=1, source_target_pairs={{0,64},{1,65},{2,66},{3,67},{4,68},{5,69},{6,70},{7,71},{8,10},{9,... | collective-permute-start | bytes 196616 | tf_op jit(solution)/shard_map/ppermute | solution.py:42
  66.6 4.6 %collective-permute-start.8 = (bf16[128,256]{1,0:T(8,128)(2,1)S(1)}, bf16[128,256]{1,0:T(8,128)(2,1)S(1)}, u32[]{:S(2)}, u32[]{:S(2)}) collective-permute-start(bf16[128,256]{1,0:T(8,128)(2,1)S(1)} %get-tuple-element.36), channel_id=1, source_target_pairs={{0,128},{1,129},{2,130},{3,131},{4,132},{5,133},{6,134},{7,135},{8... | collective-permute-start | bytes 196616 | tf_op jit(solution)/shard_map/ppermute | solution.py:42
  66.6 4.6 %collective-permute-start.9 = (bf16[128,256]{1,0:T(8,128)(2,1)S(1)}, bf16[128,256]{1,0:T(8,128)(2,1)S(1)}, u32[]{:S(2)}, u32[]{:S(2)}) collective-permute-start(bf16[128,256]{1,0:T(8,128)(2,1)S(1)} %get-tuple-element.35), channel_id=1, source_target_pairs={{0,192},{1,193},{2,194},{3,195},{4,196},{5,197},{6,198},{7,199},{8... | collective-permute-start | bytes 196616 | tf_op jit(solution)/shard_map/ppermute | solution.py:42
  71.3 3.2 %collective-permute-start.10 = (bf16[128,256]{1,0:T(8,128)(2,1)S(1)}, bf16[128,256]{1,0:T(8,128)(2,1)S(1)}, u32[]{:S(2)}, u32[]{:S(2)}) collective-permute-start(bf16[128,256]{1,0:T(8,128)(2,1)S(1)} %add_convert_fusion.5), channel_id=1, source_target_pairs={{0,16},{1,17},{2,18},{3,19},{4,20},{5,21},{6,22},{7,23},{8,24},{9,... | collective-permute-start | bytes 196616 | tf_op jit(solution)/shard_map/ppermute | solution.py:42
  74.5 4.1 %collective-permute-start.11 = (bf16[128,256]{1,0:T(8,128)(2,1)S(1)}, bf16[128,256]{1,0:T(8,128)(2,1)S(1)}, u32[]{:S(2)}, u32[]{:S(2)}) collective-permute-start(bf16[128,256]{1,0:T(8,128)(2,1)S(1)} %add_convert_fusion.4), channel_id=1, source_target_pairs={{0,32},{1,33},{2,34},{3,35},{4,36},{5,37},{6,38},{7,39},{8,40},{9,... | collective-permute-start | bytes 196616 | tf_op jit(solution)/shard_map/ppermute | solution.py:42
  78.6 14.0 %collective-permute-start.12 = (bf16[128,256]{1,0:T(8,128)(2,1)S(1)}, bf16[128,256]{1,0:T(8,128)(2,1)S(1)}, u32[]{:S(2)}, u32[]{:S(2)}) collective-permute-start(bf16[128,256]{1,0:T(8,128)(2,1)S(1)} %add_convert_fusion.3), channel_id=1, source_target_pairs={{0,33},{1,32},{2,35},{3,34},{4,37},{5,36},{6,39},{7,38},{8,41},{9,... | collective-permute-start | bytes 196616 | tf_op jit(solution)/shard_map/ppermute | solution.py:42
  78.9 27.6 %collective-permute-start.4 = (bf16[2,256,512]{2,1,0:T(8,128)(2,1)S(1)}, bf16[2,256,512]{2,1,0:T(8,128)(2,1)S(1)}, u32[]{:S(2)}, u32[]{:S(2)}) collective-permute-start(bf16[2,256,512]{2,1,0:T(8,128)(2,1)S(1)} %copy-done.10), channel_id=1, source_target_pairs={{0,8},{8,16},{16,24},{24,32},{32,40},{40,48},{48,56},{56,64},{64,7... | collective-permute-start | bytes 1572872 | tf_op jit(solution)/shard_map/ppermute | solution.py:19
  92.7 10.8 %collective-permute-start.13 = (bf16[128,256]{1,0:T(8,128)(2,1)S(1)}, bf16[128,256]{1,0:T(8,128)(2,1)S(1)}, u32[]{:S(2)}, u32[]{:S(2)}) collective-permute-start(bf16[128,256]{1,0:T(8,128)(2,1)S(1)} %add_convert_fusion.2), channel_id=1, source_target_pairs={{0,2},{1,3},{2,0},{3,1},{4,6},{5,7},{6,4},{7,5},{8,72},{9,73},{10,... | collective-permute-start | bytes 196616 | tf_op jit(solution)/shard_map/ppermute | solution.py:42
  92.8 10.7 %collective-permute-start.14 = (bf16[128,256]{1,0:T(8,128)(2,1)S(1)}, bf16[128,256]{1,0:T(8,128)(2,1)S(1)}, u32[]{:S(2)}, u32[]{:S(2)}) collective-permute-start(bf16[128,256]{1,0:T(8,128)(2,1)S(1)} %add_convert_fusion.2), channel_id=1, source_target_pairs={{0,4},{1,5},{2,6},{3,7},{4,0},{5,1},{6,2},{7,3},{8,136},{9,137},{1... | collective-permute-start | bytes 196616 | tf_op jit(solution)/shard_map/ppermute | solution.py:42
  94.1 9.4 %collective-permute-start.15 = (bf16[128,256]{1,0:T(8,128)(2,1)S(1)}, bf16[128,256]{1,0:T(8,128)(2,1)S(1)}, u32[]{:S(2)}, u32[]{:S(2)}) collective-permute-start(bf16[128,256]{1,0:T(8,128)(2,1)S(1)} %add_convert_fusion.2), channel_id=1, source_target_pairs={{0,6},{1,7},{2,4},{3,5},{4,2},{5,3},{6,0},{7,1},{8,200},{9,201},{1... | collective-permute-start | bytes 196616 | tf_op jit(solution)/shard_map/ppermute | solution.py:42
  96.6 27.0 %collective-permute-start.1 = (bf16[2,256,768]{2,1,0:T(8,128)(2,1)S(1)}, bf16[2,256,768]{2,1,0:T(8,128)(2,1)S(1)}, u32[]{:S(2)}, u32[]{:S(2)}) collective-permute-start(bf16[2,256,768]{2,1,0:T(8,128)(2,1)S(1)} %copy-done.9), channel_id=1, source_target_pairs={{0,8},{8,16},{16,24},{24,32},{32,40},{40,48},{48,56},{56,64},{64,7... | collective-permute-start | bytes 2359304 | tf_op jit(solution)/shard_map/ppermute | solution.py:19
  103.6 5.8 %collective-permute-start.16 = (bf16[128,256]{1,0:T(8,128)(2,1)S(1)}, bf16[128,256]{1,0:T(8,128)(2,1)S(1)}, u32[]{:S(2)}, u32[]{:S(2)}) collective-permute-start(bf16[128,256]{1,0:T(8,128)(2,1)S(1)} %get-tuple-element.33), channel_id=1, source_target_pairs={{0,64},{1,65},{2,66},{3,67},{4,68},{5,69},{6,70},{7,71},{8,10},{9,... | collective-permute-start | bytes 196616 | tf_op jit(solution)/shard_map/ppermute | solution.py:42
  106.5 17.1 %copy-start.5 = (f32[2,256,768]{2,1,0:T(8,128)S(1)}, f32[2,256,768]{2,1,0:T(8,128)}, u32[]{:S(2)}) copy-start(f32[2,256,768]{2,1,0:T(8,128)} %get-tuple-element.23) | copy-start | bytes 4718596
  106.7 22.1 %collective-permute-start.5 = (bf16[2,256,256]{2,1,0:T(8,128)(2,1)S(1)}, bf16[2,256,256]{2,1,0:T(8,128)(2,1)S(1)}, u32[]{:S(2)}, u32[]{:S(2)}) collective-permute-start(bf16[2,256,256]{2,1,0:T(8,128)(2,1)S(1)} %get-tuple-element.37), channel_id=1, source_target_pairs={{0,1},{1,2},{2,3},{3,4},{4,5},{5,6},{6,7},{8,9},{9,10},{10,11},{11... | collective-permute-start | bytes 786440 | tf_op jit(solution)/shard_map/ppermute | solution.py:19
  108.7 5.0 %collective-permute-start.17 = (bf16[128,256]{1,0:T(8,128)(2,1)S(1)}, bf16[128,256]{1,0:T(8,128)(2,1)S(1)}, u32[]{:S(2)}, u32[]{:S(2)}) collective-permute-start(bf16[128,256]{1,0:T(8,128)(2,1)S(1)} %get-tuple-element.33), channel_id=1, source_target_pairs={{0,128},{1,129},{2,130},{3,131},{4,132},{5,133},{6,134},{7,135},{8... | collective-permute-start | bytes 196616 | tf_op jit(solution)/shard_map/ppermute | solution.py:42
  108.8 4.9 %collective-permute-start.18 = (bf16[128,256]{1,0:T(8,128)(2,1)S(1)}, bf16[128,256]{1,0:T(8,128)(2,1)S(1)}, u32[]{:S(2)}, u32[]{:S(2)}) collective-permute-start(bf16[128,256]{1,0:T(8,128)(2,1)S(1)} %get-tuple-element.33), channel_id=1, source_target_pairs={{0,192},{1,193},{2,194},{3,195},{4,196},{5,197},{6,198},{7,199},{8... | collective-permute-start | bytes 196616 | tf_op jit(solution)/shard_map/ppermute | solution.py:42
  113.8 15.0 %collective-permute-start.19 = (bf16[512,256]{1,0:T(8,128)(2,1)S(1)}, bf16[512,256]{1,0:T(8,128)(2,1)S(1)}, u32[]{:S(2)}, u32[]{:S(2)}) collective-permute-start(bf16[512,256]{1,0:T(8,128)(2,1)S(1)} %constant_dynamic-update-slice_fusion.2), channel_id=1, source_target_pairs={{0,8},{1,9},{2,10},{3,11},{4,12},{5,13},{6,14},{7,15},{8,0},{9,1},... | collective-permute-start | bytes 786440 | tf_op jit(solution)/shard_map/ppermute | solution.py:42
  128.8 1.7 %copy-start.4 = (f32[2,256,1024]{2,1,0:T(8,128)}, f32[2,256,1024]{2,1,0:T(8,128)S(1)}, u32[]{:S(2)}) copy-start(f32[2,256,1024]{2,1,0:T(8,128)S(1)} %fusion) | copy-start | bytes 6291460
  (1 other events, 0.7 us)

commit v5 on v4

--- a/solution.py
+++ b/solution.py
@@ -425,7 +425,7 @@
 
 
 def edge_kernel(
-    scale, pos, cnt, core, own_hbm, below_hbm, strip_hbm, corner_hbm, carry_hbm, p_hbm, probe_hbm, frames_hbm,
+    scale, pos, cnt, core, own_hbm, below_hbm, strip_hbm, corner_hbm, carry_hbm, p_hbm, band_hbm, probe_hbm, frames_hbm,
     left_hbm, right_hbm, gl_hbm, gr_hbm,
     g_own_hbm, g_rows_hbm, g_strip_hbm, p_keep_hbm, p_send_hbm,
     own, below, strip, corner, carry, p_in, probe, frames, left, right, gl, gr, sems, frame_sems, out_sems,
@@ -437,9 +437,9 @@
     copies = fetch(
         (
             own_hbm.at[:, :, inner:tc], below_hbm.at[:, :, inner:tc], strip_hbm, corner_hbm, probe_hbm,
-            left_hbm, right_hbm, gl_hbm, gr_hbm, p_hbm, carry_hbm,
+            left_hbm, right_hbm, gl_hbm, gr_hbm, p_hbm, carry_hbm, band_hbm,
         ),
-        (own, below, strip, corner, probe, left, right, gl, gr, p_in, carry),
+        (own, below, strip, corner, probe, left, right, gl, gr, p_in, carry, g_rows.at[:, :, pl.ds(0, inner)]),
         sems,
     )
     todo = scratch[-1]
@@ -468,7 +468,7 @@
     done = [send_out(p_send, p_send_hbm, out_sems.at[0])]
     p_keep[...] = p_out[core[0]] * scale
     done.append(send_out(p_keep, p_keep_hbm, out_sems.at[1]))
-    drain(gext, ((g_rows, 0, 2 * n, tr, 0),))
+    drain(gext, ((g_rows, inner, 2 * n, tr, 0),))
     done.append(send_out(g_rows, g_rows_hbm, out_sems.at[2]))
     drain(gext, ((g_strip, 0, n, 0, n),))
     done.append(send_out(g_strip, g_strip_hbm, out_sems.at[3]))
@@ -489,7 +489,7 @@
     pos, cnt = positions[0, 0], counts[0]
     core = (lax.axis_index("row") & 1).astype(jnp.int32).reshape(1)
     inner = tile_cols - size
-    rows = tile_rows + size
+    rows, cols = tile_rows + size, tile_cols + size
 
     below = shifted(object_field, "row", -1)
     strip = shifted(object_field[:, :, :size], "col", -1)
@@ -555,12 +555,12 @@
         lambda *refs: edge_kernel(scale, *refs),
         out_shape=(
             jax.ShapeDtypeStruct((2, tile_rows, size), f32),
-            jax.ShapeDtypeStruct((2, size, 2 * size), bf16),
+            jax.ShapeDtypeStruct((2, size, cols), bf16),
             jax.ShapeDtypeStruct((2, tile_rows, size), bf16),
             jax.ShapeDtypeStruct(probe.shape[1:], f32),
             jax.ShapeDtypeStruct(probe.shape[1:], bf16),
         ),
-        in_specs=[smem] * 3 + [stay] * 12,
+        in_specs=[smem] * 3 + [stay] * 13,
         out_specs=[stay] * 5,
         scratch_shapes=[
             pltpu.VMEM((2, tile_rows, size), bf16),
@@ -571,10 +571,10 @@
             pltpu.VMEM(probe.shape, f32),
         ]
         + fixed
-        + [pltpu.SemaphoreType.DMA((k,)) for k in (11, slots, 5)]
+        + [pltpu.SemaphoreType.DMA((k,)) for k in (12, slots, 5)]
         + [
             pltpu.VMEM((2, tile_rows, size), f32),
-            pltpu.VMEM((2, size, 2 * size), bf16),
+            pltpu.VMEM((2, size, cols), bf16),
             pltpu.VMEM((2, tile_rows, size), bf16),
             pltpu.VMEM(probe.shape[1:], f32),
             pltpu.VMEM(probe.shape[1:], bf16),
@@ -583,17 +583,13 @@
         + scratch(2 * size // 128),
         compiler_params=params,
         cost_estimate=pl.CostEstimate(flops=3 * 2**30, bytes_accessed=12 * 2**20, transcendentals=0),
-    )(pos, cnt, core, object_field, below, strip, corner, carry, p_part, probe, frames, left, right, gl, gr)
-
-    band = shifted(g_band, "row", 1)
+    )(pos, cnt, core, object_field, below, strip, corner, carry, p_part, g_band, probe, frames, left, right, gl, gr)
+
     tail = shifted(g_rows, "row", 1)
-    to_right = (g_strip.astype(f32) + tail[:, :, size:].astype(f32)).astype(bf16)
+    to_right = (g_strip.astype(f32) + tail[:, :, tile_cols:].astype(f32)).astype(bf16)
     side = shifted(to_right, "col", 1)
     probe_grad = reduce_all(p_keep.reshape(-1, size), p_send.reshape(-1, size)).reshape(probe.shape)
-    main = g_main + band.astype(f32)
-    object_grad = jnp.concatenate(
-        [main, g_right + tail[:, :, :size].astype(f32)], 2
-    )
+    object_grad = jnp.concatenate([g_main, g_right], 2) + tail[:, :, :tile_cols].astype(f32)
     object_grad = object_grad.at[:, :, :size].add(side.astype(f32))
     return (object_grad, probe_grad)
 
@@ -606,6 +602,4 @@
         P("row", "col", None, None),
         P("row", "col"),
     )
-    return jax.shard_map(
-        body, mesh=mesh, in_specs=placed, out_specs=(P(None, "row", "col"), P()), check_vma=False
-    )
+    return jax.shard_map(body, mesh=mesh, in_specs=placed, out_specs=(P(None, "row", "col"), P()), check_vma=False)

time: 131 us -> 140 us (1.069)
  the two profiles are of different devices: /device:TPU:35 before, /device:TPU:2 now
where the time goes in v5:
time: 140 us; the launch traced here: 139 us
  starting transfers between devices  70.1 us (50%)
  waiting for transfers between devices  36.1 us (26%)
  Pallas kernels  17.5 us (12%)
  local copies, waits for them, and re-layouts  10.8 us (8%)
  other arithmetic  2.78 us (2%)
  between operations  1.57 us (1%)
    ppermute x14, starting transfers between devices, partner(): return lax.ppermute(v, ('row', 'col'), pairs)  49.9 us
    ppermute x14, waiting for transfers between devices, partner(): return lax.ppermute(v, ('row', 'col'), pairs)  28.2 us
    ppermute x5, starting transfers between devices, shifted(): return lax.ppermute(x, axis, pairs)  20.2 us
    ppermute x5, waiting for transfers between devices, shifted(): return lax.ppermute(x, axis, pairs)  7.93 us
    pallas_call x1, Pallas kernels, body(): pl.pallas_call(inner_kernel, out_shape=(jax.ShapeDtypeStruct((2, tile_row...  7.72 us
    unnamed x22, local copies, waits for them, and re-layouts  7.33 us
    pallas_call x1, Pallas kernels, body(): pl.pallas_call(lambda *refs: edge_kernel(scale, *refs), out_shape=(jax.Sh...  5.71 us
    pallas_call x1, Pallas kernels, body(): pl.pallas_call(prep_kernel, out_shape=jax.ShapeDtypeStruct(measured.shape...  4.04 us
  transfers between devices with their start and end apart: 19, of which 12 were waited for; matrix products, arithmetic and copies ran while one was open for 3% of the time, Pallas kernels for 8%

profile of v5, /device:TPU:2, one launch (start us, length us, event | category | flops | bytes accessed | tf_op | source)
XLA Modules:
  0.0 138.8 jit_solution(12383113285960843455)
XLA Ops:
  0.6 1.3 collective-permute-start
  2.9 9.1 %collective-permute-start.1 = (bf16[2,256,256]{2,1,0:T(8,128)(2,1)S(1)}, bf16[2,256,256]{2,1,0:T(8,128)(2,1)S(1)}, u32[]{:S(2)}, u32[]{:S(2)}) collective-permute-start(bf16[2,256,256]{2,1,0:T(8,128)(2,1)S(1)} %slice.33), channel_id=1, source_target_pairs={{1,0},{2,1},{3,2},{4,3},{5,4},{6,5},{7,6},{9,8},{10,9},{11,10},{12... | collective-permute-start | bytes 786440 | tf_op jit(solution)/shard_map/ppermute | solution.py:19
  12.0 1.4 copy.13.pos.refs_0_
  14.0 1.4 %copy-done = bf16[1,1,12,256,256]{4,3,2,1,0:T(8,128)(2,1)S(1)} copy-done((bf16[1,1,12,256,256]{4,3,2,1,0:T(8,128)(2,1)S(1)}, bf16[1,1,12,256,256]{4,3,2,1,0:T(8,128)(2,1)}, u32[]{:S(2)}) %copy-start) | copy-done | bytes 1572888
  17.2 4.0 %shard_map.122.frames_hbm.refs_11_ = bf16[12,256,256]{2,1,0:T(8,128)(2,1)S(1)} custom-call(bf16[12,256,256]{2,1,0:T(8,128)(2,1)S(1)} %bitcast.11, bf16[256,256]{1,0:T(8,128)(2,1)S(1)} %copy-done.2, bf16[256,256]{1,0:T(8,128)(2,1)S(1)} %copy-done.3), custom_call_target="tpu_custom_call" | custom-call | flops 805306368 | bytes 3145728 | tf_op jit(solution)/shard_map/pallas_call | solution.py:497
  21.3 1.1 copy-done.1
  22.4 1.3 collective-permute-start.2
  24.7 7.7 %shard_map.123 = (f32[2,256,768]{2,1,0:T(8,128)}, bf16[2,256,768]{2,1,0:T(8,128)(2,1)}, f32[2,2,512,128]{3,2,1,0:T(8,128)}, f32[2,2,256,256]{3,2,1,0:T(8,128)}) custom-call(s32[12,2]{1,0:T(8,128)} %copy.13.pos.refs_0_, s32[1]{0:T(128)} %bitcast.9.cnt, bf16[2,256,1024]{2,1,0:T(8,128)(2,1)} %refs_3_.1, bf16[2,256,1024]{2,1,0:T(8,128)(2,1)} %copy-done.8, ...), custom_call_target="tpu_custom_call" | custom-call | flops 9663676416 | bytes 12582912 | tf_op jit(solution)/shard_map/pallas_call | solution.py:527
  33.1 5.7 %shard_map.124 = (f32[2,256,256]{2,1,0:T(8,128)}, bf16[2,256,1280]{2,1,0:T(8,128)(2,1)}, bf16[2,256,256]{2,1,0:T(8,128)(2,1)}, f32[2,256,256]{2,1,0:T(8,128)}, bf16[2,256,256]{2,1,0:T(8,128)(2,1)}) custom-call(s32[12,2]{1,0:T(8,128)} %copy.13.pos.refs_0_, s32[1]{0:T(128)} %bitcast.10.refs_1_, s32[1]{0:T(128)} %bitcast.3.refs_2_, ...), custom_call_target="tpu_custom_call" | custom-call | flops 3221225472 | bytes 12582912 | tf_op jit(solution)/shard_map/pallas_call | solution.py:554
  38.9 9.9 %collective-permute-start.5 = (bf16[512,256]{1,0:T(8,128)(2,1)}, bf16[512,256]{1,0:T(8,128)(2,1)S(1)}, u32[]{:S(2)}, u32[]{:S(2)}) collective-permute-start(bf16[512,256]{1,0:T(8,128)(2,1)} %bitcast.14), channel_id=1, source_target_pairs={{0,8},{1,9},{2,10},{3,11},{4,12},{5,13},{6,14},{7,15},{8,0},{9,1},... | collective-permute-start | bytes 786440 | tf_op jit(solution)/shard_map/ppermute | solution.py:42
  48.8 1.4 collective-permute-done.5
  50.2 1.1 bitcast_add_fusion
  51.3 6.4 %collective-permute-start.6 = (bf16[128,256]{1,0:T(8,128)(2,1)S(1)}, bf16[128,256]{1,0:T(8,128)(2,1)S(1)}, u32[]{:S(2)}, u32[]{:S(2)}) collective-permute-start(bf16[128,256]{1,0:T(8,128)(2,1)S(1)} %get-tuple-element.34), channel_id=1, source_target_pairs={{0,64},{1,65},{2,66},{3,67},{4,68},{5,69},{6,70},{7,71},{8,10},{9,... | collective-permute-start | bytes 196616 | tf_op jit(solution)/shard_map/ppermute | solution.py:42
  57.6 5.2 %collective-permute-start.7 = (bf16[128,256]{1,0:T(8,128)(2,1)S(1)}, bf16[128,256]{1,0:T(8,128)(2,1)S(1)}, u32[]{:S(2)}, u32[]{:S(2)}) collective-permute-start(bf16[128,256]{1,0:T(8,128)(2,1)S(1)} %get-tuple-element.36), channel_id=1, source_target_pairs={{0,128},{1,129},{2,130},{3,131},{4,132},{5,133},{6,134},{7,135},{8... | collective-permute-start | bytes 196616 | tf_op jit(solution)/shard_map/ppermute | solution.py:42
  62.9 2.9 %collective-permute-done.7 = bf16[128,256]{1,0:T(8,128)(2,1)S(1)} collective-permute-done((bf16[128,256]{1,0:T(8,128)(2,1)S(1)}, bf16[128,256]{1,0:T(8,128)(2,1)S(1)}, u32[]{:S(2)}, u32[]{:S(2)}) %collective-permute-start.7) | collective-permute-done | bytes 65568 | tf_op jit(solution)/shard_map/ppermute | solution.py:42
  65.8 2.5 %collective-permute-done.8 = bf16[128,256]{1,0:T(8,128)(2,1)S(1)} collective-permute-done((bf16[128,256]{1,0:T(8,128)(2,1)S(1)}, bf16[128,256]{1,0:T(8,128)(2,1)S(1)}, u32[]{:S(2)}, u32[]{:S(2)}) %collective-permute-start.8) | collective-permute-done | bytes 65568 | tf_op jit(solution)/shard_map/ppermute | solution.py:42
  68.9 3.8 %collective-permute-done.9 = bf16[128,256]{1,0:T(8,128)(2,1)S(1)} collective-permute-done((bf16[128,256]{1,0:T(8,128)(2,1)S(1)}, bf16[128,256]{1,0:T(8,128)(2,1)S(1)}, u32[]{:S(2)}, u32[]{:S(2)}) %collective-permute-start.9) | collective-permute-done | bytes 65568 | tf_op jit(solution)/shard_map/ppermute | solution.py:42
  72.7 13.7 %collective-permute-start.10 = (bf16[128,256]{1,0:T(8,128)(2,1)S(1)}, bf16[128,256]{1,0:T(8,128)(2,1)S(1)}, u32[]{:S(2)}, u32[]{:S(2)}) collective-permute-start(bf16[128,256]{1,0:T(8,128)(2,1)S(1)} %add_convert_fusion.4), channel_id=1, source_target_pairs={{0,32},{1,33},{2,34},{3,35},{4,36},{5,37},{6,38},{7,39},{8,40},{9,... | collective-permute-start | bytes 196616 | tf_op jit(solution)/shard_map/ppermute | solution.py:42
  86.4 2.2 %collective-permute-done.10 = bf16[128,256]{1,0:T(8,128)(2,1)S(1)} collective-permute-done((bf16[128,256]{1,0:T(8,128)(2,1)S(1)}, bf16[128,256]{1,0:T(8,128)(2,1)S(1)}, u32[]{:S(2)}, u32[]{:S(2)}) %collective-permute-start.10) | collective-permute-done | bytes 65568 | tf_op jit(solution)/shard_map/ppermute | solution.py:42
  89.0 1.4 collective-permute-start.3
  90.4 5.0 %collective-permute-done.11 = bf16[128,256]{1,0:T(8,128)(2,1)S(1)} collective-permute-done((bf16[128,256]{1,0:T(8,128)(2,1)S(1)}, bf16[128,256]{1,0:T(8,128)(2,1)S(1)}, u32[]{:S(2)}, u32[]{:S(2)}) %collective-permute-start.11) | collective-permute-done | bytes 65568 | tf_op jit(solution)/shard_map/ppermute | solution.py:42
  95.5 2.9 %collective-permute-start.12 = (bf16[128,256]{1,0:T(8,128)(2,1)S(1)}, bf16[128,256]{1,0:T(8,128)(2,1)S(1)}, u32[]{:S(2)}, u32[]{:S(2)}) collective-permute-start(bf16[128,256]{1,0:T(8,128)(2,1)S(1)} %add_convert_fusion.2), channel_id=1, source_target_pairs={{0,2},{1,3},{2,0},{3,1},{4,6},{5,7},{6,4},{7,5},{8,72},{9,73},{10,... | collective-permute-start | bytes 196616 | tf_op jit(solution)/shard_map/ppermute | solution.py:42
  98.3 1.6 %collective-permute-start.14 = (bf16[128,256]{1,0:T(8,128)(2,1)S(1)}, bf16[128,256]{1,0:T(8,128)(2,1)S(1)}, u32[]{:S(2)}, u32[]{:S(2)}) collective-permute-start(bf16[128,256]{1,0:T(8,128)(2,1)S(1)} %add_convert_fusion.2), channel_id=1, source_target_pairs={{0,6},{1,7},{2,4},{3,5},{4,2},{5,3},{6,0},{7,1},{8,200},{9,201},{1... | collective-permute-start | bytes 196616 | tf_op jit(solution)/shard_map/ppermute | solution.py:42
  100.6 3.5 %collective-permute-done.13 = bf16[128,256]{1,0:T(8,128)(2,1)S(1)} collective-permute-done((bf16[128,256]{1,0:T(8,128)(2,1)S(1)}, bf16[128,256]{1,0:T(8,128)(2,1)S(1)}, u32[]{:S(2)}, u32[]{:S(2)}) %collective-permute-start.13) | collective-permute-done | bytes 65568 | tf_op jit(solution)/shard_map/ppermute | solution.py:42
  104.8 2.0 %collective-permute-start.16 = (bf16[128,256]{1,0:T(8,128)(2,1)S(1)}, bf16[128,256]{1,0:T(8,128)(2,1)S(1)}, u32[]{:S(2)}, u32[]{:S(2)}) collective-permute-start(bf16[128,256]{1,0:T(8,128)(2,1)S(1)} %get-tuple-element.33), channel_id=1, source_target_pairs={{0,128},{1,129},{2,130},{3,131},{4,132},{5,133},{6,134},{7,135},{8... | collective-permute-start | bytes 196616 | tf_op jit(solution)/shard_map/ppermute | solution.py:42
  106.8 2.1 %collective-permute-start.17 = (bf16[128,256]{1,0:T(8,128)(2,1)S(1)}, bf16[128,256]{1,0:T(8,128)(2,1)S(1)}, u32[]{:S(2)}, u32[]{:S(2)}) collective-permute-start(bf16[128,256]{1,0:T(8,128)(2,1)S(1)} %get-tuple-element.33), channel_id=1, source_target_pairs={{0,192},{1,193},{2,194},{3,195},{4,196},{5,197},{6,198},{7,199},{8... | collective-permute-start | bytes 196616 | tf_op jit(solution)/shard_map/ppermute | solution.py:42
  109.5 4.3 %collective-permute-done.16 = bf16[128,256]{1,0:T(8,128)(2,1)S(1)} collective-permute-done((bf16[128,256]{1,0:T(8,128)(2,1)S(1)}, bf16[128,256]{1,0:T(8,128)(2,1)S(1)}, u32[]{:S(2)}, u32[]{:S(2)}) %collective-permute-start.16) | collective-permute-done | bytes 65568 | tf_op jit(solution)/shard_map/ppermute | solution.py:42
  113.8 4.7 %collective-permute-start.18 = (bf16[512,256]{1,0:T(8,128)(2,1)S(1)}, bf16[512,256]{1,0:T(8,128)(2,1)}, u32[]{:S(2)}, u32[]{:S(2)}) collective-permute-start(bf16[512,256]{1,0:T(8,128)(2,1)S(1)} %constant_dynamic-update-slice_fusion.2), channel_id=1, source_target_pairs={{0,8},{1,9},{2,10},{3,11},{4,12},{5,13},{6,14},{7,15},{8,0},{9,1},... | collective-permute-start | bytes 786440 | tf_op jit(solution)/shard_map/ppermute | solution.py:42
  118.6 1.2 collective-permute-done.18
  121.9 7.1 %collective-permute-start.4 = (bf16[2,256,256]{2,1,0:T(8,128)(2,1)S(1)}, bf16[2,256,256]{2,1,0:T(8,128)(2,1)S(1)}, u32[]{:S(2)}, u32[]{:S(2)}) collective-permute-start(bf16[2,256,256]{2,1,0:T(8,128)(2,1)S(1)} %add_convert_fusion), channel_id=1, source_target_pairs={{0,1},{1,2},{2,3},{3,4},{4,5},{5,6},{6,7},{8,9},{9,10},{10,11},{11... | collective-permute-start | bytes 786440 | tf_op jit(solution)/shard_map/ppermute | solution.py:19
  129.4 7.9 %collective-permute-done.4 = bf16[2,256,256]{2,1,0:T(8,128)(2,1)S(1)} collective-permute-done((bf16[2,256,256]{2,1,0:T(8,128)(2,1)S(1)}, bf16[2,256,256]{2,1,0:T(8,128)(2,1)S(1)}, u32[]{:S(2)}, u32[]{:S(2)}) %collective-permute-start.4) | collective-permute-done | bytes 262176 | tf_op jit(solution)/shard_map/ppermute | solution.py:19
  137.4 1.3 copy-done.4
  (51 shorter events, 9.9 us)
Async XLA Ops:
  0.6 23.1 %collective-permute-start = (bf16[2,256,1024]{2,1,0:T(8,128)(2,1)}, bf16[2,256,1024]{2,1,0:T(8,128)(2,1)S(1)}, u32[]{:S(2)}, u32[]{:S(2)}) collective-permute-start(bf16[2,256,1024]{2,1,0:T(8,128)(2,1)} %refs_3_.1), channel_id=1, source_target_pairs={{8,0},{16,8},{24,16},{32,24},{40,32},{48,40},{56,48},{64,56},{72,6... | collective-permute-start | bytes 3145736 | tf_op jit(solution)/shard_map/ppermute | solution.py:19
  2.9 19.5 %collective-permute-start.1 = (bf16[2,256,256]{2,1,0:T(8,128)(2,1)S(1)}, bf16[2,256,256]{2,1,0:T(8,128)(2,1)S(1)}, u32[]{:S(2)}, u32[]{:S(2)}) collective-permute-start(bf16[2,256,256]{2,1,0:T(8,128)(2,1)S(1)} %slice.33), channel_id=1, source_target_pairs={{1,0},{2,1},{3,2},{4,3},{5,4},{6,5},{7,6},{9,8},{10,9},{11,10},{12... | collective-permute-start | bytes 786440 | tf_op jit(solution)/shard_map/ppermute | solution.py:19
  14.0 1.4 %copy-start = (bf16[1,1,12,256,256]{4,3,2,1,0:T(8,128)(2,1)S(1)}, bf16[1,1,12,256,256]{4,3,2,1,0:T(8,128)(2,1)}, u32[]{:S(2)}) copy-start(bf16[1,1,12,256,256]{4,3,2,1,0:T(8,128)(2,1)} %param.15) | copy-start | bytes 4718596
  15.4 0.9 copy-start.2
  16.3 0.9 copy-start.3
  21.3 1.1 copy-start.1
  22.4 10.0 %copy-start.9 = (bf16[2,256,256]{2,1,0:T(8,128)(2,1)}, bf16[2,256,256]{2,1,0:T(8,128)(2,1)S(1)}, u32[]{:S(2)}) copy-start(bf16[2,256,256]{2,1,0:T(8,128)(2,1)S(1)} %collective-permute-done.1.refs_5_) | copy-start | bytes 786436
  22.4 10.0 %collective-permute-start.2 = (bf16[2,256,256]{2,1,0:T(8,128)(2,1)S(1)}, bf16[2,256,256]{2,1,0:T(8,128)(2,1)S(1)}, u32[]{:S(2)}, u32[]{:S(2)}) collective-permute-start(bf16[2,256,256]{2,1,0:T(8,128)(2,1)S(1)} %collective-permute-done.1.refs_5_), channel_id=1, source_target_pairs={{8,0},{16,8},{24,16},{32,24},{40,32},{48,40},{56,48},{64,56},{72,6... | collective-permute-start | bytes 786440 | tf_op jit(solution)/shard_map/ppermute | solution.py:19
  23.7 1.0 copy-start.8
  32.4 0.7 copy-start.10
  38.9 11.3 %collective-permute-start.5 = (bf16[512,256]{1,0:T(8,128)(2,1)}, bf16[512,256]{1,0:T(8,128)(2,1)S(1)}, u32[]{:S(2)}, u32[]{:S(2)}) collective-permute-start(bf16[512,256]{1,0:T(8,128)(2,1)} %bitcast.14), channel_id=1, source_target_pairs={{0,8},{1,9},{2,10},{3,11},{4,12},{5,13},{6,14},{7,15},{8,0},{9,1},... | collective-permute-start | bytes 786440 | tf_op jit(solution)/shard_map/ppermute | solution.py:42
  51.3 11.6 %collective-permute-start.6 = (bf16[128,256]{1,0:T(8,128)(2,1)S(1)}, bf16[128,256]{1,0:T(8,128)(2,1)S(1)}, u32[]{:S(2)}, u32[]{:S(2)}) collective-permute-start(bf16[128,256]{1,0:T(8,128)(2,1)S(1)} %get-tuple-element.34), channel_id=1, source_target_pairs={{0,64},{1,65},{2,66},{3,67},{4,68},{5,69},{6,70},{7,71},{8,10},{9,... | collective-permute-start | bytes 196616 | tf_op jit(solution)/shard_map/ppermute | solution.py:42
  57.6 8.1 %collective-permute-start.7 = (bf16[128,256]{1,0:T(8,128)(2,1)S(1)}, bf16[128,256]{1,0:T(8,128)(2,1)S(1)}, u32[]{:S(2)}, u32[]{:S(2)}) collective-permute-start(bf16[128,256]{1,0:T(8,128)(2,1)S(1)} %get-tuple-element.36), channel_id=1, source_target_pairs={{0,128},{1,129},{2,130},{3,131},{4,132},{5,133},{6,134},{7,135},{8... | collective-permute-start | bytes 196616 | tf_op jit(solution)/shard_map/ppermute | solution.py:42
  62.9 5.5 %collective-permute-start.8 = (bf16[128,256]{1,0:T(8,128)(2,1)S(1)}, bf16[128,256]{1,0:T(8,128)(2,1)S(1)}, u32[]{:S(2)}, u32[]{:S(2)}) collective-permute-start(bf16[128,256]{1,0:T(8,128)(2,1)S(1)} %get-tuple-element.35), channel_id=1, source_target_pairs={{0,192},{1,193},{2,194},{3,195},{4,196},{5,197},{6,198},{7,199},{8... | collective-permute-start | bytes 196616 | tf_op jit(solution)/shard_map/ppermute | solution.py:42
  68.4 4.4 %collective-permute-start.9 = (bf16[128,256]{1,0:T(8,128)(2,1)S(1)}, bf16[128,256]{1,0:T(8,128)(2,1)S(1)}, u32[]{:S(2)}, u32[]{:S(2)}) collective-permute-start(bf16[128,256]{1,0:T(8,128)(2,1)S(1)} %add_convert_fusion.5), channel_id=1, source_target_pairs={{0,16},{1,17},{2,18},{3,19},{4,20},{5,21},{6,22},{7,23},{8,24},{9,... | collective-permute-start | bytes 196616 | tf_op jit(solution)/shard_map/ppermute | solution.py:42
  72.7 15.9 %collective-permute-start.10 = (bf16[128,256]{1,0:T(8,128)(2,1)S(1)}, bf16[128,256]{1,0:T(8,128)(2,1)S(1)}, u32[]{:S(2)}, u32[]{:S(2)}) collective-permute-start(bf16[128,256]{1,0:T(8,128)(2,1)S(1)} %add_convert_fusion.4), channel_id=1, source_target_pairs={{0,32},{1,33},{2,34},{3,35},{4,36},{5,37},{6,38},{7,39},{8,40},{9,... | collective-permute-start | bytes 196616 | tf_op jit(solution)/shard_map/ppermute | solution.py:42
  88.7 6.7 %collective-permute-start.11 = (bf16[128,256]{1,0:T(8,128)(2,1)S(1)}, bf16[128,256]{1,0:T(8,128)(2,1)S(1)}, u32[]{:S(2)}, u32[]{:S(2)}) collective-permute-start(bf16[128,256]{1,0:T(8,128)(2,1)S(1)} %add_convert_fusion.3), channel_id=1, source_target_pairs={{0,33},{1,32},{2,35},{3,34},{4,37},{5,36},{6,39},{7,38},{8,41},{9,... | collective-permute-start | bytes 196616 | tf_op jit(solution)/shard_map/ppermute | solution.py:42
  89.0 32.8 %collective-permute-start.3 = (bf16[2,256,1280]{2,1,0:T(8,128)(2,1)}, bf16[2,256,1280]{2,1,0:T(8,128)(2,1)S(1)}, u32[]{:S(2)}, u32[]{:S(2)}) collective-permute-start(bf16[2,256,1280]{2,1,0:T(8,128)(2,1)} %get-tuple-element.28), channel_id=1, source_target_pairs={{0,8},{8,16},{16,24},{24,32},{32,40},{40,48},{48,56},{56,64},{64,7... | collective-permute-start | bytes 3932168 | tf_op jit(solution)/shard_map/ppermute | solution.py:19
  95.4 26.4 %copy-start.7 = (bf16[2,256,256]{2,1,0:T(8,128)(2,1)S(1)}, bf16[2,256,256]{2,1,0:T(8,128)(2,1)}, u32[]{:S(2)}) copy-start(bf16[2,256,256]{2,1,0:T(8,128)(2,1)} %get-tuple-element.29) | copy-start | bytes 786436
  95.5 5.1 %collective-permute-start.12 = (bf16[128,256]{1,0:T(8,128)(2,1)S(1)}, bf16[128,256]{1,0:T(8,128)(2,1)S(1)}, u32[]{:S(2)}, u32[]{:S(2)}) collective-permute-start(bf16[128,256]{1,0:T(8,128)(2,1)S(1)} %add_convert_fusion.2), channel_id=1, source_target_pairs={{0,2},{1,3},{2,0},{3,1},{4,6},{5,7},{6,4},{7,5},{8,72},{9,73},{10,... | collective-permute-start | bytes 196616 | tf_op jit(solution)/shard_map/ppermute | solution.py:42
  98.3 5.8 %collective-permute-start.13 = (bf16[128,256]{1,0:T(8,128)(2,1)S(1)}, bf16[128,256]{1,0:T(8,128)(2,1)S(1)}, u32[]{:S(2)}, u32[]{:S(2)}) collective-permute-start(bf16[128,256]{1,0:T(8,128)(2,1)S(1)} %add_convert_fusion.2), channel_id=1, source_target_pairs={{0,4},{1,5},{2,6},{3,7},{4,0},{5,1},{6,2},{7,3},{8,136},{9,137},{1... | collective-permute-start | bytes 196616 | tf_op jit(solution)/shard_map/ppermute | solution.py:42
  98.3 5.8 %collective-permute-start.14 = (bf16[128,256]{1,0:T(8,128)(2,1)S(1)}, bf16[128,256]{1,0:T(8,128)(2,1)S(1)}, u32[]{:S(2)}, u32[]{:S(2)}) collective-permute-start(bf16[128,256]{1,0:T(8,128)(2,1)S(1)} %add_convert_fusion.2), channel_id=1, source_target_pairs={{0,6},{1,7},{2,4},{3,5},{4,2},{5,3},{6,0},{7,1},{8,200},{9,201},{1... | collective-permute-start | bytes 196616 | tf_op jit(solution)/shard_map/ppermute | solution.py:42
  104.2 5.3 %collective-permute-start.15 = (bf16[128,256]{1,0:T(8,128)(2,1)S(1)}, bf16[128,256]{1,0:T(8,128)(2,1)S(1)}, u32[]{:S(2)}, u32[]{:S(2)}) collective-permute-start(bf16[128,256]{1,0:T(8,128)(2,1)S(1)} %get-tuple-element.33), channel_id=1, source_target_pairs={{0,64},{1,65},{2,66},{3,67},{4,68},{5,69},{6,70},{7,71},{8,10},{9,... | collective-permute-start | bytes 196616 | tf_op jit(solution)/shard_map/ppermute | solution.py:42
  104.8 8.9 %collective-permute-start.16 = (bf16[128,256]{1,0:T(8,128)(2,1)S(1)}, bf16[128,256]{1,0:T(8,128)(2,1)S(1)}, u32[]{:S(2)}, u32[]{:S(2)}) collective-permute-start(bf16[128,256]{1,0:T(8,128)(2,1)S(1)} %get-tuple-element.33), channel_id=1, source_target_pairs={{0,128},{1,129},{2,130},{3,131},{4,132},{5,133},{6,134},{7,135},{8... | collective-permute-start | bytes 196616 | tf_op jit(solution)/shard_map/ppermute | solution.py:42
  106.8 7.0 %collective-permute-start.17 = (bf16[128,256]{1,0:T(8,128)(2,1)S(1)}, bf16[128,256]{1,0:T(8,128)(2,1)S(1)}, u32[]{:S(2)}, u32[]{:S(2)}) collective-permute-start(bf16[128,256]{1,0:T(8,128)(2,1)S(1)} %get-tuple-element.33), channel_id=1, source_target_pairs={{0,192},{1,193},{2,194},{3,195},{4,196},{5,197},{6,198},{7,199},{8... | collective-permute-start | bytes 196616 | tf_op jit(solution)/shard_map/ppermute | solution.py:42
  109.5 19.6 %copy-start.5 = (f32[2,256,768]{2,1,0:T(8,128)S(1)}, f32[2,256,768]{2,1,0:T(8,128)}, u32[]{:S(2)}) copy-start(f32[2,256,768]{2,1,0:T(8,128)} %get-tuple-element.23) | copy-start | bytes 4718596
  113.8 6.0 %collective-permute-start.18 = (bf16[512,256]{1,0:T(8,128)(2,1)S(1)}, bf16[512,256]{1,0:T(8,128)(2,1)}, u32[]{:S(2)}, u32[]{:S(2)}) collective-permute-start(bf16[512,256]{1,0:T(8,128)(2,1)S(1)} %constant_dynamic-update-slice_fusion.2), channel_id=1, source_target_pairs={{0,8},{1,9},{2,10},{3,11},{4,12},{5,13},{6,14},{7,15},{8,0},{9,1},... | collective-permute-start | bytes 786440 | tf_op jit(solution)/shard_map/ppermute | solution.py:42
  118.5 10.6 %copy-start.6 = (f32[2,256,256]{2,1,0:T(8,128)S(1)}, f32[2,256,256]{2,1,0:T(8,128)}, u32[]{:S(2)}) copy-start(f32[2,256,256]{2,1,0:T(8,128)} %get-tuple-element.27) | copy-start | bytes 1572868
  121.9 15.4 %collective-permute-start.4 = (bf16[2,256,256]{2,1,0:T(8,128)(2,1)S(1)}, bf16[2,256,256]{2,1,0:T(8,128)(2,1)S(1)}, u32[]{:S(2)}, u32[]{:S(2)}) collective-permute-start(bf16[2,256,256]{2,1,0:T(8,128)(2,1)S(1)} %add_convert_fusion), channel_id=1, source_target_pairs={{0,1},{1,2},{2,3},{3,4},{4,5},{5,6},{6,7},{8,9},{9,10},{10,11},{11... | collective-permute-start | bytes 786440 | tf_op jit(solution)/shard_map/ppermute | solution.py:19
  137.4 1.3 copy-start.4

commit v6 on v5

--- a/solution.py
+++ b/solution.py
@@ -381,27 +381,28 @@
     return copy
 
 
-def inner_kernel(
-    pos, cnt, own_hbm, below_hbm, probe_hbm, frames_hbm, left_hbm, right_hbm, gl_hbm, gr_hbm,
-    g_own_hbm, g_below_hbm, carry_hbm, p_hbm,
-    own, below, probe, frames, left, right, gl, gr, sems, frame_sems, out_sems, g_own, g_below, p_out,
-    ext, gext, *scratch,
+def tile_kernel(
+    scale, pos, cnt, core, own_hbm, below_hbm, strip_hbm, corner_hbm, probe_hbm, frames_hbm,
+    left_hbm, right_hbm, gl_hbm, gr_hbm,
+    g_own_hbm, g_rows_hbm, g_strip_hbm, p_keep_hbm, p_send_hbm,
+    own, below, strip, corner, probe, frames, left, right, gl, gr, sems, frame_sems, out_sems,
+    g_own, g_rows, g_strip, p_keep, p_send, p_out, ext, gext, *scratch,
 ):
     copies = fetch(
-        (own_hbm, below_hbm, probe_hbm, left_hbm, right_hbm, gl_hbm, gr_hbm),
-        (own, below, probe, left, right, gl, gr),
+        (own_hbm, below_hbm, strip_hbm, corner_hbm, probe_hbm, left_hbm, right_hbm, gl_hbm, gr_hbm),
+        (own, below, strip, corner, probe, left, right, gl, gr),
         sems,
     )
     n = probe.shape[-1]
     tr, tc = own.shape[1:]
-    inner = tc - n
     todo = scratch[-1]
-    count = choose(pos, cnt, lambda c: c < inner, todo, frames_hbm, frames, frame_sems)
+    count = choose(pos, cnt, lambda c: c >= 0, todo, frames_hbm, frames, frame_sems)
     copies[0].wait()
     fill(ext, ((own, 0, tc, 0, 0),))
-    copies[1].wait()
-    fill(ext, ((below, 0, tc, tr, 0),))
-    for copy in copies[2:]:
+    for copy in copies[1:4]:
+        copy.wait()
+    fill(ext, ((below, 0, tc, tr, 0), (strip, 0, n, 0, tc), (corner, 0, n, tr, tc)))
+    for copy in copies[4:]:
         copy.wait()
     await_frames(count, todo, frames_hbm, frames, frame_sems)
 
@@ -410,69 +411,18 @@
         p_out[...] = jnp.zeros_like(p_out)
 
     positions_pass(
-        pos, count, 0, tc // 128, clear, probe, frames, (left, right, gl, gr), p_out,
+        pos, count, 0, (tc + n) // 128, clear, probe, frames, (left, right, gl, gr), p_out,
         ext, gext, *scratch,
-    )
-    done = [send_out(p_out, p_hbm, out_sems.at[0])]
-    for p in range(2):
-        done.append(send_out(gext.at[p, pl.ds(inner // 128, n // 128)], carry_hbm.at[p], out_sems.at[1 + p]))
-    drain(gext, ((g_below, 0, inner, tr, 0),))
-    done.append(send_out(g_below, g_below_hbm, out_sems.at[3]))
-    drain(gext, ((g_own, 0, inner, 0, 0),))
-    done.append(send_out(g_own, g_own_hbm, out_sems.at[4]))
-    for copy in done:
-        copy.wait()
-
-
-def edge_kernel(
-    scale, pos, cnt, core, own_hbm, below_hbm, strip_hbm, corner_hbm, carry_hbm, p_hbm, band_hbm, probe_hbm, frames_hbm,
-    left_hbm, right_hbm, gl_hbm, gr_hbm,
-    g_own_hbm, g_rows_hbm, g_strip_hbm, p_keep_hbm, p_send_hbm,
-    own, below, strip, corner, carry, p_in, probe, frames, left, right, gl, gr, sems, frame_sems, out_sems,
-    g_own, g_rows, g_strip, p_keep, p_send, p_out, ext, gext, *scratch,
-):
-    n = probe.shape[-1]
-    tr, tc = own_hbm.shape[1:]
-    inner = tc - n
-    copies = fetch(
-        (
-            own_hbm.at[:, :, inner:tc], below_hbm.at[:, :, inner:tc], strip_hbm, corner_hbm, probe_hbm,
-            left_hbm, right_hbm, gl_hbm, gr_hbm, p_hbm, carry_hbm, band_hbm,
-        ),
-        (own, below, strip, corner, probe, left, right, gl, gr, p_in, carry, g_rows.at[:, :, pl.ds(0, inner)]),
-        sems,
-    )
-    todo = scratch[-1]
-    count = choose(pos, cnt, lambda c: c >= inner, todo, frames_hbm, frames, frame_sems)
-    for copy in copies[:4]:
-        copy.wait()
-    fill(ext, ((own, 0, n, 0, 0), (below, 0, n, tr, 0), (strip, 0, n, 0, n), (corner, 0, n, tr, n)))
-    for copy in copies[4:9]:
-        copy.wait()
-    await_frames(count, todo, frames_hbm, frames, frame_sems)
-
-    def clear():
-        for copy in copies[9:]:
-            copy.wait()
-        p_out[...] = p_in[...]
-        for p in range(2):
-            for b in range(n // 128):
-                gext[p, b] = carry[p, b]
-                gext[p, n // 128 + b] = jnp.zeros_like(gext[p, b])
-
-    positions_pass(
-        pos, count, inner // 128, 2 * n // 128, clear, probe, frames,
-        (left, right, gl, gr), p_out, ext, gext, *scratch,
     )
     p_send[...] = (p_out[1 - core[0]] * scale).astype(bf16)
     done = [send_out(p_send, p_send_hbm, out_sems.at[0])]
     p_keep[...] = p_out[core[0]] * scale
     done.append(send_out(p_keep, p_keep_hbm, out_sems.at[1]))
-    drain(gext, ((g_rows, inner, 2 * n, tr, 0),))
+    drain(gext, ((g_rows, 0, tc + n, tr, 0),))
     done.append(send_out(g_rows, g_rows_hbm, out_sems.at[2]))
-    drain(gext, ((g_strip, 0, n, 0, n),))
+    drain(gext, ((g_strip, 0, n, 0, tc),))
     done.append(send_out(g_strip, g_strip_hbm, out_sems.at[3]))
-    drain(gext, ((g_own, 0, n, 0, 0),))
+    drain(gext, ((g_own, 0, tc, 0, 0),))
     done.append(send_out(g_own, g_own_hbm, out_sems.at[4]))
     for copy in done:
         copy.wait()
@@ -488,7 +438,6 @@
     smem = pl.BlockSpec(memory_space=pltpu.SMEM)
     pos, cnt = positions[0, 0], counts[0]
     core = (lax.axis_index("row") & 1).astype(jnp.int32).reshape(1)
-    inner = tile_cols - size
     rows, cols = tile_rows + size, tile_cols + size
 
     below = shifted(object_field, "row", -1)
@@ -524,72 +473,45 @@
     params = pltpu.CompilerParams(
         vmem_limit_bytes=60 * 2**20
     )
-    g_main, g_band, carry, p_part = pl.pallas_call(
-        inner_kernel,
-        out_shape=(
-            jax.ShapeDtypeStruct((2, tile_rows, inner), f32),
-            jax.ShapeDtypeStruct((2, size, inner), bf16),
-            jax.ShapeDtypeStruct((2, size // 128, rows, 128), f32),
-            jax.ShapeDtypeStruct(probe.shape, f32),
-        ),
-        in_specs=[smem, smem] + [stay] * 8,
-        out_specs=[stay] * 4,
-        scratch_shapes=[
-            pltpu.VMEM((2, tile_rows, tile_cols), bf16),
-            pltpu.VMEM((2, size, tile_cols), bf16),
-        ]
-        + fixed
-        + [pltpu.SemaphoreType.DMA((k,)) for k in (7, slots, 5)]
-        + [
-            pltpu.VMEM((2, tile_rows, inner), f32),
-            pltpu.VMEM((2, size, inner), bf16),
-            pltpu.VMEM(probe.shape, f32),
-        ]
-        + scratch(tile_cols // 128),
-        compiler_params=params,
-        cost_estimate=pl.CostEstimate(flops=9 * 2**30, bytes_accessed=12 * 2**20, transcendentals=0),
-    )(pos, cnt, object_field, below, probe, frames, left, right, gl, gr)
     total = slots * lax.axis_size("row") * lax.axis_size("col")
     scale = 1.0 / math.sqrt(total)
-    g_right, g_rows, g_strip, p_keep, p_send = pl.pallas_call(
-        lambda *refs: edge_kernel(scale, *refs),
+    g_own, g_rows, g_strip, p_keep, p_send = pl.pallas_call(
+        lambda *refs: tile_kernel(scale, *refs),
         out_shape=(
-            jax.ShapeDtypeStruct((2, tile_rows, size), f32),
+            jax.ShapeDtypeStruct((2, tile_rows, tile_cols), f32),
             jax.ShapeDtypeStruct((2, size, cols), bf16),
             jax.ShapeDtypeStruct((2, tile_rows, size), bf16),
             jax.ShapeDtypeStruct(probe.shape[1:], f32),
             jax.ShapeDtypeStruct(probe.shape[1:], bf16),
         ),
-        in_specs=[smem] * 3 + [stay] * 13,
+        in_specs=[smem] * 3 + [stay] * 10,
         out_specs=[stay] * 5,
         scratch_shapes=[
+            pltpu.VMEM((2, tile_rows, tile_cols), bf16),
+            pltpu.VMEM((2, size, tile_cols), bf16),
             pltpu.VMEM((2, tile_rows, size), bf16),
             pltpu.VMEM((2, size, size), bf16),
-            pltpu.VMEM((2, tile_rows, size), bf16),
-            pltpu.VMEM((2, size, size), bf16),
-            pltpu.VMEM((2, size // 128, rows, 128), f32),
-            pltpu.VMEM(probe.shape, f32),
         ]
         + fixed
-        + [pltpu.SemaphoreType.DMA((k,)) for k in (12, slots, 5)]
+        + [pltpu.SemaphoreType.DMA((k,)) for k in (9, slots, 5)]
         + [
-            pltpu.VMEM((2, tile_rows, size), f32),
+            pltpu.VMEM((2, tile_rows, tile_cols), f32),
             pltpu.VMEM((2, size, cols), bf16),
             pltpu.VMEM((2, tile_rows, size), bf16),
             pltpu.VMEM(probe.shape[1:], f32),
             pltpu.VMEM(probe.shape[1:], bf16),
             pltpu.VMEM(probe.shape, f32),
         ]
-        + scratch(2 * size // 128),
+        + scratch(cols // 128),
         compiler_params=params,
-        cost_estimate=pl.CostEstimate(flops=3 * 2**30, bytes_accessed=12 * 2**20, transcendentals=0),
-    )(pos, cnt, core, object_field, below, strip, corner, carry, p_part, g_band, probe, frames, left, right, gl, gr)
+        cost_estimate=pl.CostEstimate(flops=slots * 2**30, bytes_accessed=16 * 2**20, transcendentals=0),
+    )(pos, cnt, core, object_field, below, strip, corner, probe, frames, left, right, gl, gr)
 
     tail = shifted(g_rows, "row", 1)
     to_right = (g_strip.astype(f32) + tail[:, :, tile_cols:].astype(f32)).astype(bf16)
     side = shifted(to_right, "col", 1)
     probe_grad = reduce_all(p_keep.reshape(-1, size), p_send.reshape(-1, size)).reshape(probe.shape)
-    object_grad = jnp.concatenate([g_main, g_right], 2) + tail[:, :, :tile_cols].astype(f32)
+    object_grad = g_own + tail[:, :, :tile_cols].astype(f32)
     object_grad = object_grad.at[:, :, :size].add(side.astype(f32))
     return (object_grad, probe_grad)
 
@@ -602,4 +524,6 @@
         P("row", "col", None, None),
         P("row", "col"),
     )
-    return jax.shard_map(body, mesh=mesh, in_specs=placed, out_specs=(P(None, "row", "col"), P()), check_vma=False)
+    return jax.shard_map(
+        body, mesh=mesh, in_specs=placed, out_specs=(P(None, "row", "col"), P()), check_vma=False
+    )

time: 140 us -> 146 us (1.043)
  Pallas kernels: 17.5 us -> 12.2 us
  waiting for transfers between devices: 36.1 us -> 40.9 us
  starting transfers between devices: 70.1 us -> 73.8 us
  local copies, waits for them, and re-layouts: 10.8 us -> 13.7 us
    ppermute x5, waiting for transfers between devices: 7.93 us -> 15.4 us  [shifted(): return lax.ppermute(x, axis, pairs)]
    pallas_call x2 -> x1, Pallas kernels: 13.4 us -> 8.17 us  [body(): pl.pallas_call(lambda *refs: tile_kernel(scale, *refs), out_shape=(jax.Sh...]
    ppermute x14, waiting for transfers between devices: 28.2 us -> 25.5 us  [partner(): return lax.ppermute(v, ('row', 'col'), pairs)]
    ppermute x14, starting transfers between devices: 49.9 us -> 52 us  [partner(): return lax.ppermute(v, ('row', 'col'), pairs)]
    dynamic_update_slice x4, local copies, waits for them, and re-layouts: 1 us -> 2.87 us  [gather(): out = lax.dynamic_update_slice_in_dim(out, got[d - 1], (g ^ d) * k, 0)]
    ppermute x5, starting transfers between devices: 20.2 us -> 21.8 us  [shifted(): return lax.ppermute(x, axis, pairs)]
    unnamed x22 -> x20, local copies, waits for them, and re-layouts: 7.33 us -> 6.75 us
  transfers between devices with their start and end apart: 19 -> 19, of which waited for: 12 -> 13; matrix products, arithmetic and copies ran while one was open for 3% -> 6% of each run, Pallas kernels for 8% -> 3%
where the time goes in v6:
time: 146 us
  starting transfers between devices  73.8 us (51%)
  waiting for transfers between devices  40.9 us (28%)
  local copies, waits for them, and re-layouts  13.7 us (9%)
  Pallas kernels  12.2 us (8%)
  other arithmetic  3.4 us (2%)
  between operations  1.48 us (1%)
    ppermute x14, starting transfers between devices, partner(): return lax.ppermute(v, ('row', 'col'), pairs)  52 us
    ppermute x14, waiting for transfers between devices, partner(): return lax.ppermute(v, ('row', 'col'), pairs)  25.5 us
    ppermute x5, starting transfers between devices, shifted(): return lax.ppermute(x, axis, pairs)  21.8 us
    ppermute x5, waiting for transfers between devices, shifted(): return lax.ppermute(x, axis, pairs)  15.4 us
    pallas_call x1, Pallas kernels, body(): pl.pallas_call(lambda *refs: tile_kernel(scale, *refs), out_shape=(jax.Sh...  8.17 us
    unnamed x20, local copies, waits for them, and re-layouts  6.75 us
    pallas_call x1, Pallas kernels, body(): pl.pallas_call(prep_kernel, out_shape=jax.ShapeDtypeStruct(measured.shape...  4.03 us
  transfers between devices with their start and end apart: 19, of which 13 were waited for; matrix products, arithmetic and copies ran while one was open for 6% of the time, Pallas kernels for 3%

profile of v6, /device:TPU:2, one launch (start us, length us, event | category | flops | bytes accessed | tf_op | source)
XLA Modules:
  0.0 145.5 jit_solution(7686181073666893782)
XLA Ops:
  0.6 1.3 collective-permute-start
  2.9 9.1 %collective-permute-start.1 = (bf16[2,256,256]{2,1,0:T(8,128)(2,1)S(1)}, bf16[2,256,256]{2,1,0:T(8,128)(2,1)S(1)}, u32[]{:S(2)}, u32[]{:S(2)}) collective-permute-start(bf16[2,256,256]{2,1,0:T(8,128)(2,1)S(1)} %slice.33), channel_id=1, source_target_pairs={{1,0},{2,1},{3,2},{4,3},{5,4},{6,5},{7,6},{9,8},{10,9},{11,10},{12... | collective-permute-start | bytes 786440 | tf_op jit(solution)/shard_map/ppermute | solution.py:19
  12.0 7.7 %collective-permute-done.1.refs_5_ = bf16[2,256,256]{2,1,0:T(8,128)(2,1)S(1)} collective-permute-done((bf16[2,256,256]{2,1,0:T(8,128)(2,1)S(1)}, bf16[2,256,256]{2,1,0:T(8,128)(2,1)S(1)}, u32[]{:S(2)}, u32[]{:S(2)}) %collective-permute-start.1) | collective-permute-done | bytes 262176 | tf_op jit(solution)/shard_map/ppermute | solution.py:19
  19.7 1.3 collective-permute-start.2
  21.0 1.4 copy.13.refs_0_
  23.0 1.4 copy-done
  26.2 4.0 %shard_map.122.refs_8_ = bf16[12,256,256]{2,1,0:T(8,128)(2,1)S(1)} custom-call(bf16[12,256,256]{2,1,0:T(8,128)(2,1)S(1)} %bitcast.10, bf16[256,256]{1,0:T(8,128)(2,1)S(1)} %copy-done.2, bf16[256,256]{1,0:T(8,128)(2,1)S(1)} %copy-done.3), custom_call_target="tpu_custom_call" | custom-call | flops 805306368 | bytes 3145728 | tf_op jit(solution)/shard_map/pallas_call | solution.py:446
  30.3 1.2 copy-done.1
  32.5 8.2 %shard_map.123 = (f32[2,256,1024]{2,1,0:T(8,128)}, bf16[2,256,1280]{2,1,0:T(8,128)(2,1)}, bf16[2,256,256]{2,1,0:T(8,128)(2,1)}, f32[2,256,256]{2,1,0:T(8,128)}, bf16[2,256,256]{2,1,0:T(8,128)(2,1)}) custom-call(s32[12,2]{1,0:T(8,128)} %copy.13.refs_0_, s32[1]{0:T(128)} %bitcast.9.refs_1_, s32[1]{0:T(128)} %bitcast.2.refs_2_, bf16[2,256,1024]{2,1,0:T(8,128)(2,1)} %refs_3_.1, ...), custom_call_target="tpu_custom_call" | custom-call | flops 12884901888 | bytes 16777216 | tf_op jit(solution)/shard_map/pallas_call | solution.py:478
  40.7 10.5 %collective-permute-start.5 = (bf16[512,256]{1,0:T(8,128)(2,1)}, bf16[512,256]{1,0:T(8,128)(2,1)S(1)}, u32[]{:S(2)}, u32[]{:S(2)}) collective-permute-start(bf16[512,256]{1,0:T(8,128)(2,1)} %bitcast.13), channel_id=1, source_target_pairs={{0,8},{1,9},{2,10},{3,11},{4,12},{5,13},{6,14},{7,15},{8,0},{9,1},... | collective-permute-start | bytes 786440 | tf_op jit(solution)/shard_map/ppermute | solution.py:42
  51.2 1.4 collective-permute-done.5
  52.5 1.1 bitcast_add_fusion
  53.7 11.8 %collective-permute-start.8 = (bf16[128,256]{1,0:T(8,128)(2,1)S(1)}, bf16[128,256]{1,0:T(8,128)(2,1)S(1)}, u32[]{:S(2)}, u32[]{:S(2)}) collective-permute-start(bf16[128,256]{1,0:T(8,128)(2,1)S(1)} %get-tuple-element.27), channel_id=1, source_target_pairs={{0,192},{1,193},{2,194},{3,195},{4,196},{5,197},{6,198},{7,199},{8... | collective-permute-start | bytes 196616 | tf_op jit(solution)/shard_map/ppermute | solution.py:42
  66.5 1.6 %collective-permute-done.8 = bf16[128,256]{1,0:T(8,128)(2,1)S(1)} collective-permute-done((bf16[128,256]{1,0:T(8,128)(2,1)S(1)}, bf16[128,256]{1,0:T(8,128)(2,1)S(1)}, u32[]{:S(2)}, u32[]{:S(2)}) %collective-permute-start.8) | collective-permute-done | bytes 65568 | tf_op jit(solution)/shard_map/ppermute | solution.py:42
  68.0 3.3 %collective-permute-done.7 = bf16[128,256]{1,0:T(8,128)(2,1)S(1)} collective-permute-done((bf16[128,256]{1,0:T(8,128)(2,1)S(1)}, bf16[128,256]{1,0:T(8,128)(2,1)S(1)}, u32[]{:S(2)}, u32[]{:S(2)}) %collective-permute-start.7) | collective-permute-done | bytes 65568 | tf_op jit(solution)/shard_map/ppermute | solution.py:42
  71.3 1.0 collective-permute-start.9
  72.3 3.3 %collective-permute-done.9 = bf16[128,256]{1,0:T(8,128)(2,1)S(1)} collective-permute-done((bf16[128,256]{1,0:T(8,128)(2,1)S(1)}, bf16[128,256]{1,0:T(8,128)(2,1)S(1)}, u32[]{:S(2)}, u32[]{:S(2)}) %collective-permute-start.9) | collective-permute-done | bytes 65568 | tf_op jit(solution)/shard_map/ppermute | solution.py:42
  75.7 12.8 %collective-permute-start.10 = (bf16[128,256]{1,0:T(8,128)(2,1)S(1)}, bf16[128,256]{1,0:T(8,128)(2,1)S(1)}, u32[]{:S(2)}, u32[]{:S(2)}) collective-permute-start(bf16[128,256]{1,0:T(8,128)(2,1)S(1)} %add_convert_fusion.4), channel_id=1, source_target_pairs={{0,32},{1,33},{2,34},{3,35},{4,36},{5,37},{6,38},{7,39},{8,40},{9,... | collective-permute-start | bytes 196616 | tf_op jit(solution)/shard_map/ppermute | solution.py:42
  88.5 2.2 %collective-permute-done.10 = bf16[128,256]{1,0:T(8,128)(2,1)S(1)} collective-permute-done((bf16[128,256]{1,0:T(8,128)(2,1)S(1)}, bf16[128,256]{1,0:T(8,128)(2,1)S(1)}, u32[]{:S(2)}, u32[]{:S(2)}) %collective-permute-start.10) | collective-permute-done | bytes 65568 | tf_op jit(solution)/shard_map/ppermute | solution.py:42
  91.1 1.4 collective-permute-start.3
  92.5 4.7 %collective-permute-done.11 = bf16[128,256]{1,0:T(8,128)(2,1)S(1)} collective-permute-done((bf16[128,256]{1,0:T(8,128)(2,1)S(1)}, bf16[128,256]{1,0:T(8,128)(2,1)S(1)}, u32[]{:S(2)}, u32[]{:S(2)}) %collective-permute-start.11) | collective-permute-done | bytes 65568 | tf_op jit(solution)/shard_map/ppermute | solution.py:42
  98.1 5.0 %collective-permute-start.13 = (bf16[128,256]{1,0:T(8,128)(2,1)S(1)}, bf16[128,256]{1,0:T(8,128)(2,1)S(1)}, u32[]{:S(2)}, u32[]{:S(2)}) collective-permute-start(bf16[128,256]{1,0:T(8,128)(2,1)S(1)} %add_convert_fusion.2), channel_id=1, source_target_pairs={{0,4},{1,5},{2,6},{3,7},{4,0},{5,1},{6,2},{7,3},{8,136},{9,137},{1... | collective-permute-start | bytes 196616 | tf_op jit(solution)/shard_map/ppermute | solution.py:42
  103.1 2.2 %collective-permute-done.13 = bf16[128,256]{1,0:T(8,128)(2,1)S(1)} collective-permute-done((bf16[128,256]{1,0:T(8,128)(2,1)S(1)}, bf16[128,256]{1,0:T(8,128)(2,1)S(1)}, u32[]{:S(2)}, u32[]{:S(2)}) %collective-permute-start.13) | collective-permute-done | bytes 65568 | tf_op jit(solution)/shard_map/ppermute | solution.py:42
  105.3 2.0 %collective-permute-done.12 = bf16[128,256]{1,0:T(8,128)(2,1)S(1)} collective-permute-done((bf16[128,256]{1,0:T(8,128)(2,1)S(1)}, bf16[128,256]{1,0:T(8,128)(2,1)S(1)}, u32[]{:S(2)}, u32[]{:S(2)}) %collective-permute-start.12) | collective-permute-done | bytes 65568 | tf_op jit(solution)/shard_map/ppermute | solution.py:42
  108.7 1.1 collective-permute-start.15
  109.9 2.6 %collective-permute-start.16 = (bf16[128,256]{1,0:T(8,128)(2,1)S(1)}, bf16[128,256]{1,0:T(8,128)(2,1)S(1)}, u32[]{:S(2)}, u32[]{:S(2)}) collective-permute-start(bf16[128,256]{1,0:T(8,128)(2,1)S(1)} %get-tuple-element.25), channel_id=1, source_target_pairs={{0,128},{1,129},{2,130},{3,131},{4,132},{5,133},{6,134},{7,135},{8... | collective-permute-start | bytes 196616 | tf_op jit(solution)/shard_map/ppermute | solution.py:42
  114.4 4.0 %collective-permute-done.16 = bf16[128,256]{1,0:T(8,128)(2,1)S(1)} collective-permute-done((bf16[128,256]{1,0:T(8,128)(2,1)S(1)}, bf16[128,256]{1,0:T(8,128)(2,1)S(1)}, u32[]{:S(2)}, u32[]{:S(2)}) %collective-permute-start.16) | collective-permute-done | bytes 65568 | tf_op jit(solution)/shard_map/ppermute | solution.py:42
  119.6 4.0 %collective-permute-start.18 = (bf16[512,256]{1,0:T(8,128)(2,1)}, bf16[512,256]{1,0:T(8,128)(2,1)}, u32[]{:S(2)}, u32[]{:S(2)}) collective-permute-start(bf16[512,256]{1,0:T(8,128)(2,1)} %constant_dynamic-update-slice_fusion.2), channel_id=1, source_target_pairs={{0,8},{1,9},{2,10},{3,11},{4,12},{5,13},{6,14},{7,15},{8,0},{9,1},... | collective-permute-start | bytes 786440 | tf_op jit(solution)/shard_map/ppermute | solution.py:42
  126.1 1.1 convert.1
  127.3 8.8 %collective-permute-start.4 = (bf16[2,256,256]{2,1,0:T(8,128)(2,1)S(1)}, bf16[2,256,256]{2,1,0:T(8,128)(2,1)S(1)}, u32[]{:S(2)}, u32[]{:S(2)}) collective-permute-start(bf16[2,256,256]{2,1,0:T(8,128)(2,1)S(1)} %add_convert_fusion), channel_id=1, source_target_pairs={{0,1},{1,2},{2,3},{3,4},{4,5},{5,6},{6,7},{8,9},{9,10},{10,11},{11... | collective-permute-start | bytes 786440 | tf_op jit(solution)/shard_map/ppermute | solution.py:19
  136.4 7.7 %collective-permute-done.4 = bf16[2,256,256]{2,1,0:T(8,128)(2,1)S(1)} collective-permute-done((bf16[2,256,256]{2,1,0:T(8,128)(2,1)S(1)}, bf16[2,256,256]{2,1,0:T(8,128)(2,1)S(1)}, u32[]{:S(2)}, u32[]{:S(2)}) %collective-permute-start.4) | collective-permute-done | bytes 262176 | tf_op jit(solution)/shard_map/ppermute | solution.py:19
  144.2 1.3 copy-done.4
  (48 shorter events, 13.7 us)
Async XLA Ops:
  0.6 30.8 %collective-permute-start = (bf16[2,256,1024]{2,1,0:T(8,128)(2,1)}, bf16[2,256,1024]{2,1,0:T(8,128)(2,1)S(1)}, u32[]{:S(2)}, u32[]{:S(2)}) collective-permute-start(bf16[2,256,1024]{2,1,0:T(8,128)(2,1)} %refs_3_.1), channel_id=1, source_target_pairs={{8,0},{16,8},{24,16},{32,24},{40,32},{48,40},{56,48},{64,56},{72,6... | collective-permute-start | bytes 3145736 | tf_op jit(solution)/shard_map/ppermute | solution.py:19
  2.9 16.8 %collective-permute-start.1 = (bf16[2,256,256]{2,1,0:T(8,128)(2,1)S(1)}, bf16[2,256,256]{2,1,0:T(8,128)(2,1)S(1)}, u32[]{:S(2)}, u32[]{:S(2)}) collective-permute-start(bf16[2,256,256]{2,1,0:T(8,128)(2,1)S(1)} %slice.33), channel_id=1, source_target_pairs={{1,0},{2,1},{3,2},{4,3},{5,4},{6,5},{7,6},{9,8},{10,9},{11,10},{12... | collective-permute-start | bytes 786440 | tf_op jit(solution)/shard_map/ppermute | solution.py:19
  19.7 11.8 %copy-start.8 = (bf16[2,256,256]{2,1,0:T(8,128)(2,1)}, bf16[2,256,256]{2,1,0:T(8,128)(2,1)S(1)}, u32[]{:S(2)}) copy-start(bf16[2,256,256]{2,1,0:T(8,128)(2,1)S(1)} %collective-permute-done.1.refs_5_) | copy-start | bytes 786436
  19.7 11.8 %collective-permute-start.2 = (bf16[2,256,256]{2,1,0:T(8,128)(2,1)S(1)}, bf16[2,256,256]{2,1,0:T(8,128)(2,1)S(1)}, u32[]{:S(2)}, u32[]{:S(2)}) collective-permute-start(bf16[2,256,256]{2,1,0:T(8,128)(2,1)S(1)} %collective-permute-done.1.refs_5_), channel_id=1, source_target_pairs={{8,0},{16,8},{24,16},{32,24},{40,32},{48,40},{56,48},{64,56},{72,6... | collective-permute-start | bytes 786440 | tf_op jit(solution)/shard_map/ppermute | solution.py:19
  23.0 1.4 copy-start
  24.4 0.9 copy-start.2
  25.3 0.9 copy-start.3
  30.3 1.2 copy-start.1
  31.5 0.7 copy-start.9
  31.5 1.0 copy-start.7
  40.7 11.9 %collective-permute-start.5 = (bf16[512,256]{1,0:T(8,128)(2,1)}, bf16[512,256]{1,0:T(8,128)(2,1)S(1)}, u32[]{:S(2)}, u32[]{:S(2)}) collective-permute-start(bf16[512,256]{1,0:T(8,128)(2,1)} %bitcast.13), channel_id=1, source_target_pairs={{0,8},{1,9},{2,10},{3,11},{4,12},{5,13},{6,14},{7,15},{8,0},{9,1},... | collective-permute-start | bytes 786440 | tf_op jit(solution)/shard_map/ppermute | solution.py:42
  53.7 14.3 %collective-permute-start.8 = (bf16[128,256]{1,0:T(8,128)(2,1)S(1)}, bf16[128,256]{1,0:T(8,128)(2,1)S(1)}, u32[]{:S(2)}, u32[]{:S(2)}) collective-permute-start(bf16[128,256]{1,0:T(8,128)(2,1)S(1)} %get-tuple-element.27), channel_id=1, source_target_pairs={{0,192},{1,193},{2,194},{3,195},{4,196},{5,197},{6,198},{7,199},{8... | collective-permute-start | bytes 196616 | tf_op jit(solution)/shard_map/ppermute | solution.py:42
  65.5 5.8 %collective-permute-start.7 = (bf16[128,256]{1,0:T(8,128)(2,1)S(1)}, bf16[128,256]{1,0:T(8,128)(2,1)S(1)}, u32[]{:S(2)}, u32[]{:S(2)}) collective-permute-start(bf16[128,256]{1,0:T(8,128)(2,1)S(1)} %get-tuple-element.28), channel_id=1, source_target_pairs={{0,128},{1,129},{2,130},{3,131},{4,132},{5,133},{6,134},{7,135},{8... | collective-permute-start | bytes 196616 | tf_op jit(solution)/shard_map/ppermute | solution.py:42
  65.5 5.8 %collective-permute-start.6 = (bf16[128,256]{1,0:T(8,128)(2,1)S(1)}, bf16[128,256]{1,0:T(8,128)(2,1)S(1)}, u32[]{:S(2)}, u32[]{:S(2)}) collective-permute-start(bf16[128,256]{1,0:T(8,128)(2,1)S(1)} %get-tuple-element.26), channel_id=1, source_target_pairs={{0,64},{1,65},{2,66},{3,67},{4,68},{5,69},{6,70},{7,71},{8,10},{9,... | collective-permute-start | bytes 196616 | tf_op jit(solution)/shard_map/ppermute | solution.py:42
  71.3 4.4 %collective-permute-start.9 = (bf16[128,256]{1,0:T(8,128)(2,1)S(1)}, bf16[128,256]{1,0:T(8,128)(2,1)S(1)}, u32[]{:S(2)}, u32[]{:S(2)}) collective-permute-start(bf16[128,256]{1,0:T(8,128)(2,1)S(1)} %add_convert_fusion.5), channel_id=1, source_target_pairs={{0,16},{1,17},{2,18},{3,19},{4,20},{5,21},{6,22},{7,23},{8,24},{9,... | collective-permute-start | bytes 196616 | tf_op jit(solution)/shard_map/ppermute | solution.py:42
  75.7 15.0 %collective-permute-start.10 = (bf16[128,256]{1,0:T(8,128)(2,1)S(1)}, bf16[128,256]{1,0:T(8,128)(2,1)S(1)}, u32[]{:S(2)}, u32[]{:S(2)}) collective-permute-start(bf16[128,256]{1,0:T(8,128)(2,1)S(1)} %add_convert_fusion.4), channel_id=1, source_target_pairs={{0,32},{1,33},{2,34},{3,35},{4,36},{5,37},{6,38},{7,39},{8,40},{9,... | collective-permute-start | bytes 196616 | tf_op jit(solution)/shard_map/ppermute | solution.py:42
  90.7 6.5 %collective-permute-start.11 = (bf16[128,256]{1,0:T(8,128)(2,1)S(1)}, bf16[128,256]{1,0:T(8,128)(2,1)S(1)}, u32[]{:S(2)}, u32[]{:S(2)}) collective-permute-start(bf16[128,256]{1,0:T(8,128)(2,1)S(1)} %add_convert_fusion.3), channel_id=1, source_target_pairs={{0,33},{1,32},{2,35},{3,34},{4,37},{5,36},{6,39},{7,38},{8,41},{9,... | collective-permute-start | bytes 196616 | tf_op jit(solution)/shard_map/ppermute | solution.py:42
  91.1 36.1 %collective-permute-start.3 = (bf16[2,256,1280]{2,1,0:T(8,128)(2,1)}, bf16[2,256,1280]{2,1,0:T(8,128)(2,1)S(1)}, u32[]{:S(2)}, u32[]{:S(2)}) collective-permute-start(bf16[2,256,1280]{2,1,0:T(8,128)(2,1)} %get-tuple-element.20), channel_id=1, source_target_pairs={{0,8},{8,16},{16,24},{24,32},{32,40},{40,48},{48,56},{56,64},{64,7... | collective-permute-start | bytes 3932168 | tf_op jit(solution)/shard_map/ppermute | solution.py:19
  97.2 5.9 %collective-permute-start.14 = (bf16[128,256]{1,0:T(8,128)(2,1)S(1)}, bf16[128,256]{1,0:T(8,128)(2,1)S(1)}, u32[]{:S(2)}, u32[]{:S(2)}) collective-permute-start(bf16[128,256]{1,0:T(8,128)(2,1)S(1)} %add_convert_fusion.2), channel_id=1, source_target_pairs={{0,6},{1,7},{2,4},{3,5},{4,2},{5,3},{6,0},{7,1},{8,200},{9,201},{1... | collective-permute-start | bytes 196616 | tf_op jit(solution)/shard_map/ppermute | solution.py:42
  98.1 7.2 %collective-permute-start.13 = (bf16[128,256]{1,0:T(8,128)(2,1)S(1)}, bf16[128,256]{1,0:T(8,128)(2,1)S(1)}, u32[]{:S(2)}, u32[]{:S(2)}) collective-permute-start(bf16[128,256]{1,0:T(8,128)(2,1)S(1)} %add_convert_fusion.2), channel_id=1, source_target_pairs={{0,4},{1,5},{2,6},{3,7},{4,0},{5,1},{6,2},{7,3},{8,136},{9,137},{1... | collective-permute-start | bytes 196616 | tf_op jit(solution)/shard_map/ppermute | solution.py:42
  103.1 4.3 %collective-permute-start.12 = (bf16[128,256]{1,0:T(8,128)(2,1)S(1)}, bf16[128,256]{1,0:T(8,128)(2,1)S(1)}, u32[]{:S(2)}, u32[]{:S(2)}) collective-permute-start(bf16[128,256]{1,0:T(8,128)(2,1)S(1)} %add_convert_fusion.2), channel_id=1, source_target_pairs={{0,2},{1,3},{2,0},{3,1},{4,6},{5,7},{6,4},{7,5},{8,72},{9,73},{10,... | collective-permute-start | bytes 196616 | tf_op jit(solution)/shard_map/ppermute | solution.py:42
  108.7 5.0 %collective-permute-start.15 = (bf16[128,256]{1,0:T(8,128)(2,1)S(1)}, bf16[128,256]{1,0:T(8,128)(2,1)S(1)}, u32[]{:S(2)}, u32[]{:S(2)}) collective-permute-start(bf16[128,256]{1,0:T(8,128)(2,1)S(1)} %get-tuple-element.25), channel_id=1, source_target_pairs={{0,64},{1,65},{2,66},{3,67},{4,68},{5,69},{6,70},{7,71},{8,10},{9,... | collective-permute-start | bytes 196616 | tf_op jit(solution)/shard_map/ppermute | solution.py:42
  109.9 8.5 %collective-permute-start.16 = (bf16[128,256]{1,0:T(8,128)(2,1)S(1)}, bf16[128,256]{1,0:T(8,128)(2,1)S(1)}, u32[]{:S(2)}, u32[]{:S(2)}) collective-permute-start(bf16[128,256]{1,0:T(8,128)(2,1)S(1)} %get-tuple-element.25), channel_id=1, source_target_pairs={{0,128},{1,129},{2,130},{3,131},{4,132},{5,133},{6,134},{7,135},{8... | collective-permute-start | bytes 196616 | tf_op jit(solution)/shard_map/ppermute | solution.py:42
  112.5 6.5 %collective-permute-start.17 = (bf16[128,256]{1,0:T(8,128)(2,1)S(1)}, bf16[128,256]{1,0:T(8,128)(2,1)S(1)}, u32[]{:S(2)}, u32[]{:S(2)}) collective-permute-start(bf16[128,256]{1,0:T(8,128)(2,1)S(1)} %get-tuple-element.25), channel_id=1, source_target_pairs={{0,192},{1,193},{2,194},{3,195},{4,196},{5,197},{6,198},{7,199},{8... | collective-permute-start | bytes 196616 | tf_op jit(solution)/shard_map/ppermute | solution.py:42
  114.4 21.7 %copy-start.5 = (f32[2,256,1024]{2,1,0:T(8,128)S(1)}, f32[2,256,1024]{2,1,0:T(8,128)}, u32[]{:S(2)}) copy-start(f32[2,256,1024]{2,1,0:T(8,128)} %get-tuple-element.19) | copy-start | bytes 6291460
  119.6 5.5 %collective-permute-start.18 = (bf16[512,256]{1,0:T(8,128)(2,1)}, bf16[512,256]{1,0:T(8,128)(2,1)}, u32[]{:S(2)}, u32[]{:S(2)}) collective-permute-start(bf16[512,256]{1,0:T(8,128)(2,1)} %constant_dynamic-update-slice_fusion.2), channel_id=1, source_target_pairs={{0,8},{1,9},{2,10},{3,11},{4,12},{5,13},{6,14},{7,15},{8,0},{9,1},... | collective-permute-start | bytes 786440 | tf_op jit(solution)/shard_map/ppermute | solution.py:42
  123.7 3.5 %copy-start.6 = (bf16[2,256,256]{2,1,0:T(8,128)(2,1)S(1)}, bf16[2,256,256]{2,1,0:T(8,128)(2,1)}, u32[]{:S(2)}) copy-start(bf16[2,256,256]{2,1,0:T(8,128)(2,1)} %get-tuple-element.21) | copy-start | bytes 786436
  127.3 16.8 %collective-permute-start.4 = (bf16[2,256,256]{2,1,0:T(8,128)(2,1)S(1)}, bf16[2,256,256]{2,1,0:T(8,128)(2,1)S(1)}, u32[]{:S(2)}, u32[]{:S(2)}) collective-permute-start(bf16[2,256,256]{2,1,0:T(8,128)(2,1)S(1)} %add_convert_fusion), channel_id=1, source_target_pairs={{0,1},{1,2},{2,3},{3,4},{4,5},{5,6},{6,7},{8,9},{9,10},{10,11},{11... | collective-permute-start | bytes 786440 | tf_op jit(solution)/shard_map/ppermute | solution.py:19
  144.2 1.3 copy-start.4
